TPU v7x, 32 devices: a whole 2x2x4 slice. The times are simulated.
32 devices in a mesh: grp: 4 (over y, x), gx: 8 (over z, core).
Axes of the slice: x: 2, y: 2, z: 4, core: 2. Of those that a mesh axis runs over, the one named last changes fastest.
Arguments:
- velocity: float32 [3, 64, 64, 4096], P(None, 'grp', 'gx'), may hold values from -6 to 6
- noise: float32 [3, 8, 64, 4096], P(None, None, None, 'gx'), may hold values from -6 to 6
- previous: float32 [3, 64, 4096], P(None, None, 'gx'), may hold values from -6 to 6
- decay: float32 [3, 64], replicated, may hold values from 0.6 to 0.99
- stress_factor: float32 [6, 64], replicated, may hold values from 0.2 to 1
- mean_profile: float32 [64], replicated, may hold values from 0.5 to 1.5
Outputs:
- advanced_velocity: float32 [3, 64, 64, 4096], P(None, 'grp', 'gx')
All inputs are finite; a program needn't handle non-finite values.
Results may differ from a plain program's by a relative error of at most 0.0003.
Values sent between devices are 32-bit elements; how exact they have to be, the bound alone decides.
No kernel may reach another device: no remote copies, remote signals or barrier semaphores. Data moves between devices by JAX's collectives and lax.ppermute only.
A program may use at most 128 MiB of HBM per device.

v0:
```python
import jax
import jax.numpy as jnp
from jax import lax
from jax.sharding import PartitionSpec as P

HALF = 32


TIME_STEP = 0.15
VISCOSITY = 0.2


def with_halo(array, sides, width, wrap):
    for axis, dim in sides:
        count, length = (lax.axis_size(axis), array.shape[dim])
        up = [(i, (i + 1) % count) for i in range(count if wrap else count - 1)]
        down = [(j, i) for i, j in up]
        last = lax.slice_in_dim(array, length - width, length, axis=dim)
        leading = lax.slice_in_dim(array, 0, width, axis=dim)
        before = lax.ppermute(last, axis, up)
        after = lax.ppermute(leading, axis, down)
        array = jnp.concatenate([before, array, after], axis=dim)
    return array


def kernel_weight(offset):
    length = HALF / 2.0
    return jnp.exp(-jnp.pi * offset * offset / (2.0 * length * length))


def kernel_norm():
    offsets = jnp.arange(-HALF, HALF + 1).astype(jnp.float32)
    return jnp.sqrt(jnp.sum(kernel_weight(offsets) ** 2))


def kernel_band(rows_count, cols_count, shift):
    offsets = (jnp.arange(rows_count)[:, None] - jnp.arange(cols_count)[None, :] - shift).astype(
        jnp.float32
    )
    inside = jnp.abs(offsets) <= HALF
    return jnp.where(inside, kernel_weight(offsets) / kernel_norm(), 0.0)


def widen(noise_part):
    return with_halo(noise_part, (("gx", 3),), HALF, True)


def filter_normal(field):
    depth = field.shape[2]
    z_band = kernel_band(depth, depth, 0)
    return jnp.einsum("zw,cpwy->cpzy", z_band, field, precision=lax.Precision.HIGHEST)


def filtered(widened, span_local):
    y_band = kernel_band(span_local + 2 * HALF, span_local, HALF)
    along_y = jnp.einsum("cpzj,jy->cpzy", widened, y_band, precision=lax.Precision.HIGHEST)
    return filter_normal(along_y)


def advance(smoothed, carried, decay_col):
    scale_col = jnp.sqrt(1.0 - decay_col * decay_col)
    outputs = []
    for plane_index in range(smoothed.shape[1]):
        carried = decay_col * carried + scale_col * smoothed[:, plane_index]
        outputs.append(carried)
    return (jnp.stack(outputs, axis=1), carried)


def colour(planes, stress_factor, mean_profile):
    factor = stress_factor[:, None, :, None]
    first = mean_profile[None, :, None] + factor[0] * planes[0]
    second = factor[1] * planes[0] + factor[2] * planes[1]
    third = factor[3] * planes[0] + factor[4] * planes[1] + factor[5] * planes[2]
    return jnp.stack([first, second, third])


def to_owners(generated):
    return lax.all_to_all(generated, "gx", split_axis=2, concat_axis=3, tiled=True)


def tendency(padded):
    centre = padded[:, 1:-1, 1:-1]
    x_next = padded[:, 2:, 1:-1]
    x_prev = padded[:, :-2, 1:-1]
    z_next = padded[:, 1:-1, 2:]
    z_prev = padded[:, 1:-1, :-2]
    y_next = jnp.roll(centre, -1, axis=3)
    y_prev = jnp.roll(centre, 1, axis=3)
    advect = centre[0:1] * (x_next - x_prev) * 0.5
    advect = advect + centre[1:2] * (z_next - z_prev) * 0.5
    advect = advect + centre[2:3] * (y_next - y_prev) * 0.5
    spread = x_next + x_prev + z_next + z_prev + y_next + y_prev - 6.0 * centre
    return -advect + VISCOSITY * spread


def faces(field):
    return with_halo(field, (("grp", 1), ("gx", 2)), 1, False)


def local(velocity, noise, previous, decay, stress_factor, mean_profile):
    row_index = lax.axis_index("grp")
    span_local = noise.shape[3]
    plane_count = noise.shape[1]
    decay_col = decay[:, :, None]
    widened = widen(noise)

    def produce():
        smoothed = filtered(widened, span_local)
        planes, unused = advance(smoothed, previous, decay_col)
        return colour(planes, stress_factor, mean_profile)

    def nothing():
        return jnp.zeros(noise.shape, jnp.float32)

    generated = lax.cond(row_index == 0, produce, nothing)
    slab_planes = to_owners(generated)
    updated = jnp.concatenate([slab_planes, velocity[:, plane_count:]], axis=1)
    start = jnp.where(row_index == 0, updated, velocity)
    section = start + TIME_STEP * tendency(faces(start))
    second = section + TIME_STEP * tendency(faces(section))
    return 0.5 * start + 0.5 * second


def solution(mesh):
    placed = (
        P(None, "grp", "gx", None),
        P(None, None, None, "gx"),
        P(None, None, "gx"),
        P(),
        P(),
        P(),
    )
    return jax.shard_map(
        local, mesh=mesh, in_specs=placed, out_specs=P(None, "grp", "gx", None), check_vma=False
    )
```

profile of v0, /device:TPU:1, one launch (start us, length us, event | category | flops | bytes accessed | tf_op | source)
XLA Modules:
  0.0 244.3 jit_solution(12985238514693766741)
XLA Ops:
  0.0 2.9 %fusion.79 = (f32[3,8,64,32]{3,2,1,0:T(8,128)}, f32[3,8,64,32]{3,2,1,0:T(8,128)}) fusion(f32[3,8,64,512]{3,2,1,0:T(8,128)} %param.9), kind=kLoop, calls=%fused_computation.139 | loop fusion | bytes 786432 | tf_op jit(solution)/shard_map/slice | solution.py:18
  2.9 2.1 copy.66
  5.1 0.1 collective-permute-start.1
  5.2 2.2 copy.65
  7.4 2.7 %collective-permute-start = (f32[3,8,64,32]{2,3,1,0:T(8,128)}, f32[3,8,64,32]{2,3,1,0:T(8,128)}, u32[]{:S(2)}, u32[]{:S(2)}) collective-permute-start(f32[3,8,64,32]{2,3,1,0:T(8,128)} %copy.65), channel_id=1, source_target_pairs={{0,1},{1,2},{2,3},{3,4},{4,5},{5,6},{6,7},{7,0},{8,9},{9,10},{10,1... | collective-permute-start | bytes 589832 | tf_op jit(solution)/shard_map/ppermute | solution.py:20
  10.1 3.5 %collective-permute-done.1 = f32[3,8,64,32]{2,3,1,0:T(8,128)} collective-permute-done((f32[3,8,64,32]{2,3,1,0:T(8,128)}, f32[3,8,64,32]{2,3,1,0:T(8,128)}, u32[]{:S(2)}, u32[]{:S(2)}) %collective-permute-start.1) | collective-permute-done | bytes 196640 | tf_op jit(solution)/shard_map/ppermute | solution.py:21
  13.6 2.2 copy.45
  15.8 3.3 %collective-permute-done = f32[3,8,64,32]{2,3,1,0:T(8,128)} collective-permute-done((f32[3,8,64,32]{2,3,1,0:T(8,128)}, f32[3,8,64,32]{2,3,1,0:T(8,128)}, u32[]{:S(2)}, u32[]{:S(2)}) %collective-permute-start) | collective-permute-done | bytes 196640 | tf_op jit(solution)/shard_map/ppermute | solution.py:20
  19.1 2.2 copy.44
  21.3 4.6 %pad_maximum_fusion.21 = f32[3,8,64,576]{3,2,1,0:T(8,128)} fusion(f32[3,8,64,32]{3,2,1,0:T(8,128)} %copy.45, f32[3,8,64,512]{3,2,1,0:T(8,128)S(1)} %copy-done.2, f32[3,8,64,32]{3,2,1,0:T(8,128)} %copy.44), kind=kLoop, calls=%fused_computation.120 | loop fusion | flops 1769472 | bytes 7077888 | tf_op jit(solution)/shard_map/concatenate | solution.py:22
  25.9 17.7 %conditional.1 = (f32[3,8,64,512]{3,2,0,1:T(8,128)S(1)}) conditional(s32[]{:T(128)} %convert_element_type.17, () %tuple.11, (f32[64]{0:T(128)S(1)}, f32[6,64]{1,0:T(8,128)S(1)}, f32[3,64]{1,0:T(4,128)S(1)}, f32[3,64,512]{2,1,0:T(8,128)S(1)}, f32[3,8,64,576]{3,2,1,0:T(8,128)}) %tuple.41), branch_computations={%region_0.0_spmd, %region_1.3_spmd} | conditional | flops 6050518016 | bytes 37785372 | solution.py:115
  25.9 1.1 fusion.60
  27.6 10.2 %fusion.10 = f32[512,3,8,64]{0,3,2,1:T(8,128)S(1)} fusion(f32[3,8,64,576]{3,2,1,0:T(8,128)} %get-tuple-element.23, f32[]{:T(128)S(6)} %sqrt.7), kind=kOutput, calls=%fused_computation.10 | convolution fusion | flops 5438767104 | bytes 6684676 | tf_op jit(solution)/shard_map/cond/branch_1_fun/cpzj,jy->cpzy/dot_general | solution.py:56
  37.8 3.3 %fusion.2 = f32[3,8,64,512]{3,2,1,0:T(8,128)S(1)} fusion(f32[512,3,8,64]{0,3,2,1:T(8,128)S(1)} %fusion.10, f32[]{:T(128)S(6)} %sqrt.7), kind=kOutput, calls=%fused_computation.3 | convolution fusion | flops 604016640 | bytes 6291460 | tf_op jit(solution)/shard_map/cond/branch_1_fun/zw,cpwy->cpzy/dot_general | solution.py:51
  41.2 0.1 bitcast_dynamic-update-slice_fusion.6
  41.3 0.2 bitcast_dynamic-update-slice_fusion.5
  41.5 0.1 bitcast_dynamic-update-slice_fusion.4
  41.6 0.2 bitcast_dynamic-update-slice_fusion.3
  41.8 0.1 bitcast_dynamic-update-slice_fusion.2
  41.9 0.2 bitcast_dynamic-update-slice_fusion.1
  42.0 0.1 bitcast_dynamic-update-slice_fusion
  42.2 0.1 fusion.27
  42.3 0.6 multiply_add_fusion.1
  43.0 0.4 pad_maximum_fusion
  43.5 3.5 %copy.46 = f32[3,8,64,512]{3,1,0,2:T(8,128)} copy(f32[3,8,64,512]{3,2,0,1:T(8,128)S(1)} %get-tuple-element.71) | data formatting | bytes 6291456 | tf_op jit(solution)/shard_map/cond | solution.py:115
  47.0 7.3 %all-to-all-start = ((f32[3,8,64,512]{3,1,0,2:T(8,128)}), f32[3,8,64,512]{3,1,0,2:T(8,128)S(1)}, u32[]{:S(2)}, u32[]{:S(2)}) async-start(f32[3,8,64,512]{3,1,0,2:T(8,128)} %copy.46), calls=%async_computation | async-start | bytes 6291456 | tf_op jit(solution)/shard_map/all_to_all | solution.py:78
  54.3 3.9 %slice.173 = f32[3,8,8,4096]{3,2,1,0:T(8,128)} slice(f32[3,16,8,4096]{3,2,1,0:T(8,128)} %param.8), slice={[0:3], [8:16], [0:8], [0:4096]} | slice | bytes 6291456 | tf_op jit(solution)/shard_map/slice | solution.py:117
  58.2 66.7 %all-to-all-done = f32[3,8,64,512]{3,1,0,2:T(8,128)S(1)} async-done(((f32[3,8,64,512]{3,1,0,2:T(8,128)}), f32[3,8,64,512]{3,1,0,2:T(8,128)S(1)}, u32[]{:S(2)}, u32[]{:S(2)}) %all-to-all-start) | async-done | bytes 3145760 | tf_op jit(solution)/shard_map/all_to_all | solution.py:78
  124.9 1.8 copy.47
  126.7 0.1 copy-done.1
  126.8 1.0 maximum_select_fusion
  127.7 0.9 fusion.76
  128.7 1.3 collective-permute-start.3
  130.0 1.3 collective-permute-start.2
  131.3 7.2 %fusion.77 = (f32[3,16,8,4095]{3,2,1,0:T(8,128)}, f32[3,16,8,4095]{3,2,1,0:T(8,128)}) fusion(f32[3,16,8,4096]{3,2,1,0:T(8,128)S(1)} %maximum_select_fusion), kind=kLoop, calls=%fused_computation.137 | loop fusion | bytes 25159680 | tf_op jit(solution)/shard_map/jit(_roll_static)/slice | solution.py:87
  138.5 0.1 fusion.78
  138.6 4.7 %collective-permute-done.2 = f32[3,1,8,4096]{3,2,1,0:T(8,128)} collective-permute-done((f32[3,1,8,4096]{3,2,1,0:T(8,128)}, f32[3,1,8,4096]{3,2,1,0:T(8,128)}, u32[]{:S(2)}, u32[]{:S(2)}) %collective-permute-start.2) | collective-permute-done | bytes 393248 | tf_op jit(solution)/shard_map/ppermute | solution.py:21
  143.3 2.7 %pad_maximum_fusion.25 = (f32[3,18,1,4096]{3,2,1,0:T(1,128)S(1)}, f32[3,18,1,4096]{3,2,1,0:T(1,128)S(1)}) fusion(f32[3,1,8,4096]{3,2,1,0:T(8,128)} %collective-permute-done.2, f32[3,16,8,4096]{3,2,1,0:T(8,128)S(1)} %maximum_select_fusion, f32[3,1,8,4096]{3,2,1,0:T(8,128)S(1)} %collective-permute-done.3), kind=kLoop, calls=%fused_computation.130 | loop fusion | flops 884736 | bytes 8847360 | tf_op jit(solution)/shard_map/concatenate | solution.py:22
  146.0 0.5 copy.50
  146.5 0.5 copy.48
  147.1 3.6 %collective-permute-start.4 = (f32[3,18,1,4096]{3,1,2,0:T(8,128)S(1)}, f32[3,18,1,4096]{3,1,2,0:T(8,128)S(1)}, u32[]{:S(2)}, u32[]{:S(2)}) collective-permute-start(f32[3,18,1,4096]{3,1,2,0:T(8,128)S(1)} %copy.48), channel_id=1, source_target_pairs={{1,0},{2,1},{3,2},{4,3},{5,4},{6,5},{7,6},{9,8},{10,9},{11,10},{12... | collective-permute-start | bytes 2654216 | tf_op jit(solution)/shard_map/ppermute | solution.py:21
  150.7 2.4 collective-permute-start.5
  153.1 2.0 slice_bitcast_fusion.19
  155.1 9.7 %collective-permute-done.4 = f32[3,18,1,4096]{3,1,2,0:T(8,128)S(1)} collective-permute-done((f32[3,18,1,4096]{3,1,2,0:T(8,128)S(1)}, f32[3,18,1,4096]{3,1,2,0:T(8,128)S(1)}, u32[]{:S(2)}, u32[]{:S(2)}) %collective-permute-start.4) | collective-permute-done | bytes 884768 | tf_op jit(solution)/shard_map/ppermute | solution.py:21
  164.8 1.9 copy.49
  166.8 1.9 copy.51
  168.7 11.3 %multiply_add_fusion.2 = f32[3,16,8,4096]{3,2,1,0:T(8,128)S(1)} fusion(f32[3,16,8,4096]{3,2,1,0:T(8,128)S(1)} %maximum_select_fusion, f32[3,16,8,4095]{3,2,1,0:T(8,128)} %get-tuple-element.66, f32[3,16,8,1]{3,2,1,0:T(8,128)S(1)} %get-tuple-element.68, f32[3,16,8,1]{3,2,1,0:T(8,128)S(1)} %get-tuple-element.67, f32[3,16,8,4095]{3,2,1,0:T(8,128)S(1)} %bitcast.157, ...), kind=kLoop, calls=%fused_computation.119 | loop fusion | flops 48758784 | bytes 34013184 | tf_op jit(solution)/shard_map/add | solution.py:119
  180.0 2.7 %copy-done = f32[3,16,8,4096]{3,2,1,0:T(8,128)} copy-done((f32[3,16,8,4096]{3,2,1,0:T(8,128)}, f32[3,16,8,4096]{3,2,1,0:T(8,128)S(1)}, u32[]{:S(2)}) %copy-start) | copy-done | bytes 6291480
  182.7 0.9 fusion.73
  183.7 2.7 %collective-permute-start.7 = (f32[3,1,8,4096]{3,2,1,0:T(8,128)}, f32[3,1,8,4096]{3,2,1,0:T(8,128)S(1)}, u32[]{:S(2)}, u32[]{:S(2)}) collective-permute-start(f32[3,1,8,4096]{3,2,1,0:T(8,128)} %get-tuple-element.54), channel_id=1, source_target_pairs={{0,8},{8,16},{16,24},{1,9},{9,17},{17,25},{2,10},{10,18},{18,26},{... | collective-permute-start | bytes 1179656 | tf_op jit(solution)/shard_map/ppermute | solution.py:20
  186.4 1.3 collective-permute-start.6
  187.7 11.0 %fusion.74 = (f32[3,16,8,4095]{3,2,1,0:T(8,128)}, f32[3,16,8,4095]{3,2,1,0:T(8,128)}) fusion(f32[3,16,8,4096]{3,2,1,0:T(8,128)} %copy-done), kind=kLoop, calls=%fused_computation.134 | loop fusion | bytes 25159680 | tf_op jit(solution)/shard_map/jit(_roll_static)/slice | solution.py:87
  198.7 1.3 fusion.75
  200.0 6.0 %pad_maximum_fusion.22 = (f32[3,18,1,4096]{3,2,1,0:T(1,128)S(1)}, f32[3,18,1,4096]{3,2,1,0:T(1,128)S(1)}) fusion(f32[3,1,8,4096]{3,2,1,0:T(8,128)} %collective-permute-done.6, f32[3,16,8,4096]{3,2,1,0:T(8,128)} %copy-done, f32[3,1,8,4096]{3,2,1,0:T(8,128)S(1)} %collective-permute-done.7), kind=kLoop, calls=%fused_computation.127 | loop fusion | flops 884736 | bytes 8847360 | tf_op jit(solution)/shard_map/concatenate | solution.py:22
  206.0 0.5 copy.54
  206.5 0.5 copy.52
  207.1 2.2 collective-permute-start.8
  209.3 7.0 %collective-permute-start.9 = (f32[3,18,1,4096]{3,1,2,0:T(8,128)S(1)}, f32[3,18,1,4096]{3,1,2,0:T(8,128)S(1)}, u32[]{:S(2)}, u32[]{:S(2)}) collective-permute-start(f32[3,18,1,4096]{3,1,2,0:T(8,128)S(1)} %copy.54), channel_id=1, source_target_pairs={{0,1},{1,2},{2,3},{3,4},{4,5},{5,6},{6,7},{8,9},{9,10},{10,11},{11... | collective-permute-start | bytes 2654216 | tf_op jit(solution)/shard_map/ppermute | solution.py:20
  216.3 2.8 %slice_bitcast_fusion.16 = (f32[16,8,4096]{2,1,0:T(8,128)}, f32[16,8,4096]{2,1,0:T(8,128)}, f32[16,8,4096]{2,1,0:T(8,128)}) fusion(f32[3,16,8,4096]{3,2,1,0:T(8,128)S(1)} %bitcast.153), kind=kLoop, calls=%fused_computation.123 | loop fusion | bytes 12582912 | tf_op jit(solution)/shard_map/mul | solution.py:89
  219.1 8.9 %collective-permute-done.8 = f32[3,18,1,4096]{3,1,2,0:T(8,128)S(1)} collective-permute-done((f32[3,18,1,4096]{3,1,2,0:T(8,128)S(1)}, f32[3,18,1,4096]{3,1,2,0:T(8,128)S(1)}, u32[]{:S(2)}, u32[]{:S(2)}) %collective-permute-start.8) | collective-permute-done | bytes 884768 | tf_op jit(solution)/shard_map/ppermute | solution.py:21
  228.0 0.9 copy.53
  228.9 0.3 collective-permute-done.9
  229.1 1.9 copy.55
  231.0 12.9 %add_multiply_fusion = f32[3,16,8,4096]{3,2,1,0:T(8,128)} fusion(f32[3,16,8,4096]{3,2,1,0:T(8,128)S(1)} %maximum_select_fusion, f32[3,16,8,4096]{3,2,1,0:T(8,128)S(1)} %bitcast.153, f32[3,16,8,4095]{3,2,1,0:T(8,128)} %get-tuple-element.57, f32[3,16,8,1]{3,2,1,0:T(8,128)S(1)} %get-tuple-element.59, f32[3,16,8,1]{3,2,1,0:T(8,128)S(1)} %get-tuple-element.58, ...), kind=kLoop, calls=%fused_computation.118 | loop fusion | flops 51904512 | bytes 40304640 | tf_op jit(solution)/shard_map/add | solution.py:121
  (33 shorter events, 0.1 us)
Async XLA Ops:
  0.0 21.3 %copy-start.2 = (f32[3,8,64,512]{3,2,1,0:T(8,128)S(1)}, f32[3,8,64,512]{3,2,1,0:T(8,128)}, u32[]{:S(2)}) copy-start(f32[3,8,64,512]{3,2,1,0:T(8,128)} %param.9) | copy-start | bytes 9437188
  5.1 20.8 %copy-start.3 = (f32[3,64,512]{2,1,0:T(8,128)S(1)}, f32[3,64,512]{2,1,0:T(8,128)}, u32[]{:S(2)}) copy-start(f32[3,64,512]{2,1,0:T(8,128)} %param.10) | copy-start | bytes 1179652
  5.1 20.8 %copy-start.4 = (f32[3,64]{1,0:T(4,128)S(1)}, f32[3,64]{1,0:T(4,128)}, u32[]{:S(2)}) copy-start(f32[3,64]{1,0:T(4,128)} %param.11) | copy-start | bytes 2308
  5.1 20.8 %copy-start.5 = (f32[6,64]{1,0:T(8,128)S(1)}, f32[6,64]{1,0:T(8,128)}, u32[]{:S(2)}) copy-start(f32[6,64]{1,0:T(8,128)} %param.12) | copy-start | bytes 4612
  5.1 20.8 %copy-start.6 = (f32[64]{0:T(128)S(1)}, f32[64]{0:T(128)}, u32[]{:S(2)}) copy-start(f32[64]{0:T(128)} %param.13) | copy-start | bytes 772
  5.1 8.5 %collective-permute-start.1 = (f32[3,8,64,32]{2,3,1,0:T(8,128)}, f32[3,8,64,32]{2,3,1,0:T(8,128)}, u32[]{:S(2)}, u32[]{:S(2)}) collective-permute-start(f32[3,8,64,32]{2,3,1,0:T(8,128)} %copy.66), channel_id=1, source_target_pairs={{1,0},{2,1},{3,2},{4,3},{5,4},{6,5},{7,6},{0,7},{9,8},{10,9},{11,1... | collective-permute-start | bytes 589832 | tf_op jit(solution)/shard_map/ppermute | solution.py:21
  7.4 11.7 %collective-permute-start = (f32[3,8,64,32]{2,3,1,0:T(8,128)}, f32[3,8,64,32]{2,3,1,0:T(8,128)}, u32[]{:S(2)}, u32[]{:S(2)}) collective-permute-start(f32[3,8,64,32]{2,3,1,0:T(8,128)} %copy.65), channel_id=1, source_target_pairs={{0,1},{1,2},{2,3},{3,4},{4,5},{5,6},{6,7},{7,0},{8,9},{9,10},{10,1... | collective-permute-start | bytes 589832 | tf_op jit(solution)/shard_map/ppermute | solution.py:20
  47.0 77.9 %all-to-all-start = ((f32[3,8,64,512]{3,1,0,2:T(8,128)}), f32[3,8,64,512]{3,1,0,2:T(8,128)S(1)}, u32[]{:S(2)}, u32[]{:S(2)}) async-start(f32[3,8,64,512]{3,1,0,2:T(8,128)} %copy.46), calls=%async_computation | async-start | bytes 6291456 | tf_op jit(solution)/shard_map/all_to_all | solution.py:78
  124.9 1.9 copy-start.1
  128.7 10.0 %collective-permute-start.3 = (f32[3,1,8,4096]{3,2,1,0:T(8,128)}, f32[3,1,8,4096]{3,2,1,0:T(8,128)S(1)}, u32[]{:S(2)}, u32[]{:S(2)}) collective-permute-start(f32[3,1,8,4096]{3,2,1,0:T(8,128)} %get-tuple-element.63), channel_id=1, source_target_pairs={{0,8},{8,16},{16,24},{1,9},{9,17},{17,25},{2,10},{10,18},{18,26},{... | collective-permute-start | bytes 1179656 | tf_op jit(solution)/shard_map/ppermute | solution.py:20
  130.0 13.3 %collective-permute-start.2 = (f32[3,1,8,4096]{3,2,1,0:T(8,128)}, f32[3,1,8,4096]{3,2,1,0:T(8,128)}, u32[]{:S(2)}, u32[]{:S(2)}) collective-permute-start(f32[3,1,8,4096]{3,2,1,0:T(8,128)} %get-tuple-element.64), channel_id=1, source_target_pairs={{8,0},{16,8},{24,16},{9,1},{17,9},{25,17},{10,2},{18,10},{26,18},{... | collective-permute-start | bytes 1179656 | tf_op jit(solution)/shard_map/ppermute | solution.py:21
  146.5 22.2 %slice-start.4 = ((s8[6291456]{0:T(1024)(128)(4,1)}), s8[4194304]{0:T(1024)(128)(4,1)S(1)}, s32[]{:S(2)}) async-start(s8[6291456]{0:T(1024)(128)(4,1)} %bitcast.156), calls=%async_computation.5 | async-start | bytes 8388608
  147.0 21.7 %slice-start.5 = ((s8[6291456]{0:T(1024)(128)(4,1)}), s8[2097152]{0:T(1024)(128)(4,1)S(1)}, s32[]{:S(2)}) async-start(s8[6291456]{0:T(1024)(128)(4,1)} %bitcast.156), calls=%async_computation.6 | async-start | bytes 4194304
  147.1 17.8 %collective-permute-start.4 = (f32[3,18,1,4096]{3,1,2,0:T(8,128)S(1)}, f32[3,18,1,4096]{3,1,2,0:T(8,128)S(1)}, u32[]{:S(2)}, u32[]{:S(2)}) collective-permute-start(f32[3,18,1,4096]{3,1,2,0:T(8,128)S(1)} %copy.48), channel_id=1, source_target_pairs={{1,0},{2,1},{3,2},{4,3},{5,4},{6,5},{7,6},{9,8},{10,9},{11,10},{12... | collective-permute-start | bytes 2654216 | tf_op jit(solution)/shard_map/ppermute | solution.py:21
  150.7 16.1 %collective-permute-start.5 = (f32[3,18,1,4096]{3,1,2,0:T(8,128)S(1)}, f32[3,18,1,4096]{3,1,2,0:T(8,128)S(1)}, u32[]{:S(2)}, u32[]{:S(2)}) collective-permute-start(f32[3,18,1,4096]{3,1,2,0:T(8,128)S(1)} %copy.50), channel_id=1, source_target_pairs={{0,1},{1,2},{2,3},{3,4},{4,5},{5,6},{6,7},{8,9},{9,10},{10,11},{11... | collective-permute-start | bytes 2654216 | tf_op jit(solution)/shard_map/ppermute | solution.py:20
  180.0 2.7 %copy-start = (f32[3,16,8,4096]{3,2,1,0:T(8,128)}, f32[3,16,8,4096]{3,2,1,0:T(8,128)S(1)}, u32[]{:S(2)}) copy-start(f32[3,16,8,4096]{3,2,1,0:T(8,128)S(1)} %multiply_add_fusion.2) | copy-start | bytes 18874372
  183.7 16.3 %collective-permute-start.7 = (f32[3,1,8,4096]{3,2,1,0:T(8,128)}, f32[3,1,8,4096]{3,2,1,0:T(8,128)S(1)}, u32[]{:S(2)}, u32[]{:S(2)}) collective-permute-start(f32[3,1,8,4096]{3,2,1,0:T(8,128)} %get-tuple-element.54), channel_id=1, source_target_pairs={{0,8},{8,16},{16,24},{1,9},{9,17},{17,25},{2,10},{10,18},{18,26},{... | collective-permute-start | bytes 1179656 | tf_op jit(solution)/shard_map/ppermute | solution.py:20
  186.4 13.6 %collective-permute-start.6 = (f32[3,1,8,4096]{3,2,1,0:T(8,128)}, f32[3,1,8,4096]{3,2,1,0:T(8,128)}, u32[]{:S(2)}, u32[]{:S(2)}) collective-permute-start(f32[3,1,8,4096]{3,2,1,0:T(8,128)} %get-tuple-element.55), channel_id=1, source_target_pairs={{8,0},{16,8},{24,16},{9,1},{17,9},{25,17},{10,2},{18,10},{26,18},{... | collective-permute-start | bytes 1179656 | tf_op jit(solution)/shard_map/ppermute | solution.py:21
  198.7 17.6 %slice-start = ((s8[6291456]{0:T(1024)(128)(4,1)}), s8[4194304]{0:T(1024)(128)(4,1)S(1)}, s32[]{:S(2)}) async-start(s8[6291456]{0:T(1024)(128)(4,1)} %bitcast.152), calls=%async_computation.1 | async-start | bytes 8388608
  200.0 16.3 %slice-start.1 = ((s8[6291456]{0:T(1024)(128)(4,1)}), s8[2097152]{0:T(1024)(128)(4,1)S(1)}, s32[]{:S(2)}) async-start(s8[6291456]{0:T(1024)(128)(4,1)} %bitcast.152), calls=%async_computation.2 | async-start | bytes 4194304
  206.5 24.5 %slice-start.2 = ((s8[6291456]{0:T(1024)(128)(4,1)}), s8[4194304]{0:T(1024)(128)(4,1)S(1)}, s32[]{:S(2)}) async-start(s8[6291456]{0:T(1024)(128)(4,1)} %bitcast.154), calls=%async_computation.3 | async-start | bytes 8388608
  207.1 24.0 %slice-start.3 = ((s8[6291456]{0:T(1024)(128)(4,1)}), s8[2097152]{0:T(1024)(128)(4,1)S(1)}, s32[]{:S(2)}) async-start(s8[6291456]{0:T(1024)(128)(4,1)} %bitcast.154), calls=%async_computation.4 | async-start | bytes 4194304
  207.1 20.9 %collective-permute-start.8 = (f32[3,18,1,4096]{3,1,2,0:T(8,128)S(1)}, f32[3,18,1,4096]{3,1,2,0:T(8,128)S(1)}, u32[]{:S(2)}, u32[]{:S(2)}) collective-permute-start(f32[3,18,1,4096]{3,1,2,0:T(8,128)S(1)} %copy.52), channel_id=1, source_target_pairs={{1,0},{2,1},{3,2},{4,3},{5,4},{6,5},{7,6},{9,8},{10,9},{11,10},{12... | collective-permute-start | bytes 2654216 | tf_op jit(solution)/shard_map/ppermute | solution.py:21
  209.3 19.9 %collective-permute-start.9 = (f32[3,18,1,4096]{3,1,2,0:T(8,128)S(1)}, f32[3,18,1,4096]{3,1,2,0:T(8,128)S(1)}, u32[]{:S(2)}, u32[]{:S(2)}) collective-permute-start(f32[3,18,1,4096]{3,1,2,0:T(8,128)S(1)} %copy.54), channel_id=1, source_target_pairs={{0,1},{1,2},{2,3},{3,4},{4,5},{5,6},{6,7},{8,9},{9,10},{10,11},{11... | collective-permute-start | bytes 2654216 | tf_op jit(solution)/shard_map/ppermute | solution.py:20
where the time goes:
time: 248 us; the launch traced here: 244 us
  waiting for transfers between devices  97.1 us (39%)
  local copies, waits for them, and re-layouts  58.7 us (24%)
  other arithmetic  41.6 us (17%)
  starting transfers between devices  31.9 us (13%)
  matrix products  13.5 us (5%)
    all_to_all x1, waiting for transfers between devices, to_owners(): lax.all_to_all(generated, 'gx', split_axis=2, concat_axis=3, tiled=True)  66.7 us
    ppermute x5, waiting for transfers between devices, with_halo(): after = lax.ppermute(leading, axis, down)  26.8 us
    slice x4, local copies, waits for them, and re-layouts, tendency(): y_next = jnp.roll(centre, -1, axis=3)  19.6 us
    ppermute x5, starting transfers between devices, with_halo(): before = lax.ppermute(last, axis, up)  16.1 us
    concatenate x3, other arithmetic, with_halo(): array = jnp.concatenate([before, array, after], axis=dim)  13.2 us
    add x1, other arithmetic, local(): return 0.5 * start + 0.5 * second  12.9 us
    add x1, other arithmetic, local(): section = start + TIME_STEP * tendency(faces(start))  11.3 us
    dot_general x1, matrix products, filtered(): jnp.einsum('cpzj,jy->cpzy', widened, y_band, precision=lax.Precision.HIGH...  10.2 us
  transfers between devices with their start and end apart: 11, of which 7 were waited for; matrix products, arithmetic and copies ran while one was open for 15% of the time, Pallas kernels for 0%

commit v1 on v0

v1 whole, which is shorter than its diff:
```python
import functools
import math

import jax
import jax.numpy as jnp
from jax import lax
from jax.experimental import pallas as pl
from jax.experimental.pallas import tpu as pltpu
from jax.sharding import PartitionSpec as P

HALF = 32
TIME_STEP = 0.15
VISCOSITY = 0.2
LANES = 128
SUB = 8
PARTS = 4
VMEM_LIMIT = 60 * 1024 * 1024

ANY = pl.BlockSpec(memory_space=pl.ANY)
SMEM = pl.BlockSpec(memory_space=pltpu.SMEM)
VMEM = pl.BlockSpec(memory_space=pltpu.VMEM)
F32 = jnp.float32


def params():
    return pltpu.CompilerParams(vmem_limit_bytes=VMEM_LIMIT)


def cost(flops, nbytes):
    return pl.CostEstimate(flops=flops, bytes_accessed=nbytes, transcendentals=0)


def kernel_norm():
    length = HALF / 2.0
    total = sum(
        math.exp(-math.pi * k * k / (2.0 * length * length)) ** 2 for k in range(-HALF, HALF + 1)
    )
    return math.sqrt(total)


def weights(offset):
    length = HALF / 2.0
    off = offset.astype(F32)
    value = jnp.exp(off * off * (-math.pi / (2.0 * length * length))) * (1.0 / kernel_norm())
    return jnp.where(jnp.abs(offset) <= HALF, value, 0.0)


def split(x):
    high = x.astype(jnp.bfloat16)
    low = (x - high.astype(F32)).astype(jnp.bfloat16)
    return high, low


def dot(a, b):
    return jnp.dot(a, b, preferred_element_type=F32)


def rim_kernel(left_ref, noise_ref, out_ref):
    depth = noise_ref.shape[2]
    span = noise_ref.shape[3]
    groups = LANES // HALF
    rows = depth // groups
    lane = lax.broadcasted_iota(jnp.int32, (rows, LANES), 1)
    use_left = left_ref[0] == 1

    def plane(i, _):
        c, p = i // noise_ref.shape[1], i % noise_ref.shape[1]
        result = None
        for q in range(groups):
            first = noise_ref[c, p, rows * q : rows * (q + 1), 0:LANES]
            last = noise_ref[c, p, rows * q : rows * (q + 1), span - LANES : span]
            last = pltpu.roll(last, HALF, 1)
            piece = jnp.where(use_left, first, last)
            if q:
                piece = pltpu.roll(piece, HALF * q, 1)
            result = piece if q == 0 else jnp.where(lane >= HALF * q, piece, result)
        out_ref[c, p] = result
        return 0

    lax.fori_loop(0, noise_ref.shape[0] * noise_ref.shape[1], plane, 0)


def filter_kernel(width, with_rim, meta_ref, noise_ref, rim_ref, prev_ref, decay_ref, factor_ref,
                  mean_ref, out_ref, planes_ref):
    comps, count, depth, span = noise_ref.shape
    base = meta_ref[0]
    rim_at = meta_ref[1]
    row = lax.broadcasted_iota(jnp.int32, (span, width), 0)
    col = lax.broadcasted_iota(jnp.int32, (span, width), 1)
    band_h, band_l = split(weights(row - col - base))
    zrow = lax.broadcasted_iota(jnp.int32, (depth, depth), 0)
    zcol = lax.broadcasted_iota(jnp.int32, (depth, depth), 1)
    zh, zl = split(weights(zrow - zcol))
    zband = jnp.concatenate([zh, zh, zl], axis=1)
    groups = LANES // HALF
    rows = depth // groups
    if with_rim:
        hrow = lax.broadcasted_iota(jnp.int32, (LANES, width), 0)
        hcol = lax.broadcasted_iota(jnp.int32, (LANES, width), 1)
        rim_bands = []
        for q in range(groups):
            cell = hrow - HALF * q
            value = weights(cell + rim_at - hcol - base)
            rim_bands.append(split(jnp.where((cell >= 0) & (cell < HALF), value, 0.0)))
    for c in range(comps):
        high, low = split(noise_ref[c].reshape(count * depth, span))
        along = dot(high, band_h) + dot(low, band_h) + dot(high, band_l)
        along = along.reshape(count, depth, width)
        if with_rim:
            rh, rl = split(rim_ref[c].reshape(count * rows, LANES))
            extra = []
            for bh, bl in rim_bands:
                part = dot(rh, bh) + dot(rl, bh) + dot(rh, bl)
                extra.append(part.reshape(count, rows, width))
            along = along + jnp.concatenate(extra, axis=1)
        wide = jnp.concatenate([along[p] for p in range(count)], axis=1)
        yh, yl = split(wide)
        smooth = dot(zband, jnp.concatenate([yh, yl, yh], axis=0))
        dec = decay_ref[c]
        scale = jnp.sqrt(1.0 - dec * dec)
        carried = prev_ref[c]
        for p in range(count):
            carried = dec * carried + scale * smooth[:, p * width : (p + 1) * width]
            planes_ref[c, p] = carried
    owners = out_ref.shape[0]
    slab = depth // owners

    def put(c, p, value):
        for d in range(owners):
            out_ref[d, c, p] = value[slab * d : slab * (d + 1)]

    for p in range(count):
        a, b, d = planes_ref[0, p], planes_ref[1, p], planes_ref[2, p]
        put(0, p, mean_ref[...] + factor_ref[0] * a)
        put(1, p, factor_ref[1] * a + factor_ref[2] * b)
        put(2, p, factor_ref[3] * a + factor_ref[4] * b + factor_ref[5] * d)


def faces_kernel(vel, low_dn, low_up, high_dn, high_up, tiles, sem):
    blocks = tiles.shape[0]
    copies = [
        pltpu.make_async_copy(vel.at[:, :, pl.ds(t * LANES, LANES)], tiles.at[t], sem.at[t])
        for t in range(blocks)
    ]
    for copy in copies:
        copy.start()
    for copy in copies:
        copy.wait()
    slab = SUB

    def block(t, _):
        at = pl.multiple_of(t * LANES, LANES)
        for c in range(3):
            for dn, up, first in ((low_dn, low_up, 0), (high_dn, high_up, low_dn.shape[2])):
                for j in range(2):
                    for ref, z in ((dn, j), (up, slab - 2 + j)):
                        for x in range(0, dn.shape[2], SUB):
                            ref[c, j, x : x + SUB, pl.ds(at, LANES)] = tiles[
                                t, c, pl.ds((first + x) * slab + z, SUB, stride=slab), :
                            ]
        return 0

    lax.fori_loop(0, blocks, block, 0)


def inflow_faces_kernel(*refs):
    parts = refs[:-2]
    dn, up = refs[-2:]
    width = parts[0].shape[3]
    slab = SUB
    cells = dn.shape[2]
    for k, part in enumerate(parts):
        for s in range(part.shape[0]):
            at = (s * len(parts) + k) * width
            for c in range(part.shape[1]):
                for j in range(2):
                    for ref, z in ((dn, j), (up, slab - 2 + j)):
                        for x in range(0, cells, SUB):
                            ref[c, j, x : x + SUB, at : at + width] = part[
                                s, c, pl.ds(x * slab + z, SUB, stride=slab), :
                            ]


A = VISCOSITY * TIME_STEP
H = 0.5 * TIME_STEP
B = 1.0 - 6.0 * A
BLOCK = 512


def combine(scale, cs, xp, xn, zp, zn, yp, yn):
    a, h, b = A * scale, H * scale, B * scale
    cu, cw, cv = h * cs[0], h * cs[1], h * cs[2]
    out = []
    for i in range(3):
        total = xn[i] * (a - cu) + xp[i] * (a + cu)
        total = total + (zn[i] * (a - cw) + zp[i] * (a + cw))
        total = total + (yn[i] * (a - cv) + yp[i] * (a + cv))
        out.append(total + b * cs[i])
    return out


def spanwise(load, at, width, span):
    centre = load(at, width)
    wide = jnp.concatenate(
        [load((at - LANES) % span, LANES), centre, load((at + width) % span, LANES)], axis=1
    )
    total = width + 2 * LANES
    before = pltpu.roll(wide, 1, 1)[:, LANES : LANES + width]
    after = pltpu.roll(wide, total - 1, 1)[:, LANES : LANES + width]
    return centre, before, after


def main_block(scale, field, x, zb, za, zrow, at, width, span):
    top = lax.broadcasted_iota(jnp.int32, (SUB, width), 0)
    cs, xp, xn, zp, zn, yp, yn = [], [], [], [], [], [], []
    for c in range(3):
        centre, before, after = spanwise(
            lambda l, w, c=c: field[c, x, :, pl.ds(l, w)], at, width, span
        )
        cs.append(centre)
        yp.append(before)
        yn.append(after)
        xp.append(field[c, x - 1, :, pl.ds(at, width)])
        xn.append(field[c, x + 1, :, pl.ds(at, width)])
        low = jnp.broadcast_to(zb[c, pl.ds(zrow, 1), pl.ds(at, width)], (SUB, width))
        high = jnp.broadcast_to(za[c, pl.ds(zrow, 1), pl.ds(at, width)], (SUB, width))
        zp.append(jnp.where(top == 0, low, pltpu.roll(centre, 1, 0)))
        zn.append(jnp.where(top == SUB - 1, high, pltpu.roll(centre, SUB - 1, 0)))
    return combine(scale, cs, xp, xn, zp, zn, yp, yn)


def edge_rows(near, before, after, out, keep, groups, span):
    def block(i, _):
        at = pl.multiple_of(i * BLOCK, BLOCK)
        left = pl.multiple_of(lax.rem(at + span - LANES, span), LANES)
        right = pl.multiple_of(lax.rem(at + BLOCK, span), LANES)
        for g in range(groups):
            cs, xp, xn, zp, zn, yp, yn = [], [], [], [], [], [], []
            for c in range(3):
                r = SUB * (g + 1)
                centre = near[c, r : r + SUB, pl.ds(at, BLOCK)]
                wide = jnp.concatenate(
                    [
                        near[c, r : r + SUB, pl.ds(left, LANES)],
                        centre,
                        near[c, r : r + SUB, pl.ds(right, LANES)],
                    ],
                    axis=1,
                )
                total = BLOCK + 2 * LANES
                cs.append(centre)
                yp.append(pltpu.roll(wide, 1, 1)[:, LANES : LANES + BLOCK])
                yn.append(pltpu.roll(wide, total - 1, 1)[:, LANES : LANES + BLOCK])
                xp.append(near[c, r - 1 : r - 1 + SUB, pl.ds(at, BLOCK)])
                xn.append(near[c, r + 1 : r + 1 + SUB, pl.ds(at, BLOCK)])
                zp.append(before[c, SUB * g : SUB * (g + 1), pl.ds(at, BLOCK)])
                zn.append(after[c, SUB * g : SUB * (g + 1), pl.ds(at, BLOCK)])
            new = combine(1.0, cs, xp, xn, zp, zn, yp, yn)
            for c in range(3):
                out[c, SUB * (g + 1) : SUB * (g + 2), pl.ds(at, BLOCK)] = jnp.where(
                    keep, new[c], 0.0
                )
        return 0

    lax.fori_loop(0, span // BLOCK, block, 0)


def section_plane(x, start, sect, nb, na, span, keep=None):
    for at in range(0, span, BLOCK):
        new = main_block(1.0, start, x + 2, nb, na, SUB + x, at, BLOCK, span)
        for c in range(3):
            value = new[c] if keep is None else jnp.where(keep, new[c], 0.0)
            sect[c, x + 1, :, at : at + BLOCK] = value


def second_plane(x, start, sect, eb, ea, out, span):
    for at in range(0, span, BLOCK):
        new = main_block(0.5, sect, x + 1, eb, ea, SUB + x, at, BLOCK, span)
        for c in range(3):
            out[c, x, :, at : at + BLOCK] = new[c] + 0.5 * start[c, x + 2, :, at : at + BLOCK]


def rows_scratch(cells, span):
    shift = [
        pltpu.VMEM((3, cells + 2 * SUB, span), F32),
        pltpu.VMEM((3, cells + 2 * SUB, span), F32),
    ]
    side = [pltpu.VMEM((3, cells, span), F32)] * 4
    return shift + side + shift


def run_copies(copies):
    for copy in copies:
        copy.start()
    for copy in copies:
        copy.wait()


def own_kernel(meta, vel, left, right, corners, dn_lo, dn_hi, up_lo, up_hi, b_lo, b_hi, a_lo, a_hi,
               out_hbm, start, sect, out, nb, na, b2, b0, a0, a2, eb, ea, corner, sem, out_sem):
    cells = vel.shape[1]
    low = dn_lo.shape[2]
    span = vel.shape[3]
    pieces = [
        (vel, start.at[:, pl.ds(2, cells)]),
        (left, start.at[:, pl.ds(0, 2)]),
        (right, start.at[:, pl.ds(cells + 2, 2)]),
        (corners, corner),
    ]
    for lo, hi, j, ref, first in (
        (b_lo, b_hi, 1, nb, SUB),
        (a_lo, a_hi, 0, na, SUB),
        (b_lo, b_hi, 0, b2, 0),
        (a_lo, a_hi, 1, a2, 0),
        (dn_lo, dn_hi, 0, b0, 0),
        (up_lo, up_hi, 1, a0, 0),
    ):
        pieces.append((lo.at[:, j], ref.at[:, pl.ds(first, low)]))
        pieces.append((hi.at[:, j], ref.at[:, pl.ds(first + low, cells - low)]))
    run_copies(
        [pltpu.make_async_copy(src, dst, sem.at[i]) for i, (src, dst) in enumerate(pieces)]
    )
    for c in range(3):
        nb[c, SUB - 1 : SUB, :] = corner[c, 0:1, :]
        nb[c, SUB + cells : SUB + cells + 1, :] = corner[c, 1:2, :]
        na[c, SUB - 1 : SUB, :] = corner[c, 2:3, :]
        na[c, SUB + cells : SUB + cells + 1, :] = corner[c, 3:4, :]
    groups = cells // SUB
    edge_rows(nb, b2, b0, eb, meta[0] == 1, groups, span)
    edge_rows(na, a0, a2, ea, meta[1] == 1, groups, span)
    first = meta[4]

    def make(x, keep=None):
        section_plane(x, start, sect, nb, na, span, keep)

    def body(x, _):
        keep = jnp.logical_or(
            jnp.logical_and(x >= 0, x < cells),
            jnp.where(x < 0, meta[2], meta[3]) == 1,
        )
        make(x, keep)

        @pl.when(x >= first + 1)
        def _():
            second_plane(x - 1, start, sect, eb, ea, out, span)
            pltpu.make_async_copy(out.at[:, x - 1], out_hbm.at[:, x - 1], out_sem.at[x - 1]).start()

        return 0

    lax.fori_loop(first - 1, cells + 1, body, 0)

    def drain(x, _):
        pltpu.make_async_copy(out.at[:, x], out_hbm.at[:, x], out_sem.at[x]).wait()
        return 0

    lax.fori_loop(first, cells, drain, 0)


def inflow_kernel(meta, vel, *refs):
    parts, refs = refs[:-23], refs[-23:]
    dn_in, up_in, b_in, a_in, dn_hi, up_hi, b_hi, a_hi, _, out_hbm = refs[:10]
    start, sect, out, nb, na, b2, b0, a0, a2, eb, ea, sem, out_sem = refs[10:]
    low = dn_in.shape[2]
    span = vel.shape[3]
    reach = out.shape[1]
    cells = b2.shape[1]

    @pl.when(meta[5] == 1)
    def _():
        pieces = [(vel.at[:, pl.ds(low, 4)], start.at[:, pl.ds(low + 2, 4)])]
        width = parts[0].shape[4]
        for k, part in enumerate(parts):
            for s in range(part.shape[0]):
                at = (s * len(parts) + k) * width
                pieces.append((part.at[s], start.at[:, pl.ds(2, low), :, pl.ds(at, width)]))
        for lo, hi, j, ref, first in (
            (b_in, b_hi, 1, nb, SUB),
            (a_in, a_hi, 0, na, SUB),
            (b_in, b_hi, 0, b2, 0),
            (a_in, a_hi, 1, a2, 0),
            (dn_in, dn_hi, 0, b0, 0),
            (up_in, up_hi, 1, a0, 0),
        ):
            pieces.append((lo.at[:, j], ref.at[:, pl.ds(first, low)]))
            pieces.append((hi.at[:, j], ref.at[:, pl.ds(first + low, cells - low)]))
        copies = [
            pltpu.make_async_copy(src, dst, sem.at[i]) for i, (src, dst) in enumerate(pieces)
        ]
        for copy in copies:
            copy.start()
        zero = jnp.zeros((SUB, span), F32)
        for c in range(3):
            start[c, 1] = zero
            sect[c, 0] = zero
            for ref in (nb, na):
                ref[c, 0:SUB, :] = zero
                ref[c, SUB + cells :, :] = zero
        for copy in copies:
            copy.wait()
        groups = cells // SUB
        edge_rows(nb, b2, b0, eb, meta[0] == 1, groups, span)
        edge_rows(na, a0, a2, ea, meta[1] == 1, groups, span)
        section_plane(0, start, sect, nb, na, span)

        def body(x, _):
            section_plane(x + 1, start, sect, nb, na, span)
            second_plane(x, start, sect, eb, ea, out, span)
            pltpu.make_async_copy(out.at[:, x], out_hbm.at[:, x], out_sem.at[x]).start()
            return 0

        lax.fori_loop(0, reach, body, 0)

        def drain(x, _):
            pltpu.make_async_copy(out.at[:, x], out_hbm.at[:, x], out_sem.at[x]).wait()
            return 0

        lax.fori_loop(0, reach, drain, 0)


def shift(array, axis, step, count, wrap=False):
    pairs = [(i, (i + step) % count) for i in range(count) if wrap or 0 <= i + step < count]
    return lax.ppermute(array, axis, pairs)


def on_lines(array, lines, step, count):
    pairs = [
        (r * count + i, r * count + i + step) for r in lines for i in range(count)
        if 0 <= i + step < count
    ]
    return lax.ppermute(array, ("grp", "gx"), pairs)


def local(velocity, noise, previous, decay, stress_factor, mean_profile):
    rows = lax.axis_size("grp")
    ranks = lax.axis_size("gx")
    r = lax.axis_index("grp")
    g = lax.axis_index("gx")
    comps, count, depth, span_local = noise.shape
    cells, slab, span = velocity.shape[1:]
    width = span_local // PARTS
    low = count
    high = cells - low

    packed = (comps, count, depth * HALF // LANES, LANES)
    is_second = (r == 2).astype(jnp.int32)
    rim_out = pl.pallas_call(
        rim_kernel,
        out_shape=jax.ShapeDtypeStruct(packed, F32),
        in_specs=[SMEM, VMEM],
        out_specs=VMEM,
        compiler_params=params(),
        cost_estimate=cost(0, 4 * noise.size),
        name="rim",
    )(is_second.reshape(1), noise)
    pairs = []
    for line in range(rows):
        step = -1 if line == 2 else 1
        pairs += [(line * ranks + i, line * ranks + (i + step) % ranks) for i in range(ranks)]
    rim = lax.ppermute(rim_out, ("grp", "gx"), pairs)

    face = jax.ShapeDtypeStruct((3, 2, low, span), F32)
    face_hi = jax.ShapeDtypeStruct((3, 2, high, span), F32)
    dn_lo, up_lo, dn_hi, up_hi = pl.pallas_call(
        faces_kernel,
        out_shape=[face, face, face_hi, face_hi],
        in_specs=[ANY],
        out_specs=[VMEM] * 4,
        scratch_shapes=[
            pltpu.VMEM((span // LANES, 3, cells * slab, LANES), F32),
            pltpu.SemaphoreType.DMA((span // LANES,)),
        ],
        compiler_params=params(),
        cost_estimate=cost(0, 8 * velocity.size),
        name="faces",
    )(velocity.reshape(3, cells * slab, span))
    b_hi = shift(up_hi, "gx", 1, ranks)
    a_hi = shift(dn_hi, "gx", -1, ranks)
    left = shift(velocity[:, cells - 2 :], "grp", 1, rows)
    right = shift(velocity[:, :2], "grp", -1, rows)
    up_corner = jnp.stack([left[:, 1, slab - 1], right[:, 0, slab - 1]], axis=1)
    dn_corner = jnp.stack([left[:, 1, 0], right[:, 0, 0]], axis=1)
    corners = jnp.concatenate(
        [shift(up_corner, "gx", 1, ranks), shift(dn_corner, "gx", -1, ranks)], axis=1
    )

    wide = (comps, depth, width)
    decay_wide = jnp.broadcast_to(decay[:, :, None], wide)
    factor_wide = jnp.broadcast_to(stress_factor[:, :, None], (6, depth, width))
    mean_wide = jnp.broadcast_to(mean_profile[:, None], (depth, width))

    def make(part, with_rim):
        base = part * width
        meta = jnp.stack([base, jnp.where(r == 2, span_local, -HALF)]).astype(jnp.int32)
        prev = lax.dynamic_slice_in_dim(previous, base, width, 2)
        return pl.pallas_call(
            functools.partial(filter_kernel, width, with_rim),
            out_shape=jax.ShapeDtypeStruct((ranks, comps, count, depth // ranks, width), F32),
            in_specs=[SMEM] + [VMEM] * 6,
            out_specs=VMEM,
            scratch_shapes=[pltpu.VMEM((comps, count, depth, width), F32)],
            compiler_params=params(),
            cost_estimate=cost(6 * noise.size * width, 4 * noise.size),
            name="filter_a" if with_rim else "filter_b",
        )(meta, noise, rim if with_rim else rim_out, prev, decay_wide, factor_wide, mean_wide)

    part_a = jnp.where(r == 1, 0, jnp.where(r == 2, 3, 1))
    made_a = make(part_a, True)
    made_b = make(jnp.int32(2), False)
    got_a = lax.all_to_all(made_a, "gx", 0, 0, tiled=True)
    got_b = lax.all_to_all(made_b, "gx", 0, 0, tiled=True)
    hop_1 = lax.ppermute(got_a, "grp", [(1, 0)])
    hop_2 = lax.ppermute(got_a, "grp", [(2, 0)])
    parts = [hop_1, got_a, got_b, hop_2]
    if width != LANES:
        joined = jnp.concatenate(parts, axis=4)
        parts = [joined[..., at : at + LANES] for at in range(0, span_local, LANES)]
    many, part_width = len(parts), parts[0].shape[4]

    others = list(range(1, rows))
    b_lo = on_lines(up_lo, others, 1, ranks)
    a_lo = on_lines(dn_lo, others, -1, ranks)

    meta = jnp.stack(
        [
            g > 0,
            g < ranks - 1,
            r > 0,
            r < rows - 1,
            jnp.where(r == 0, low + 2, 0),
            r == 0,
        ]
    ).astype(jnp.int32)

    full = jax.ShapeDtypeStruct(velocity.shape, F32)
    own = pl.pallas_call(
        own_kernel,
        out_shape=full,
        in_specs=[SMEM] + [ANY] * 12,
        out_specs=ANY,
        scratch_shapes=[
            pltpu.VMEM((3, cells + 4, slab, span), F32),
            pltpu.VMEM((3, cells + 2, slab, span), F32),
            pltpu.VMEM((3, cells, slab, span), F32),
        ]
        + rows_scratch(cells, span)
        + [
            pltpu.VMEM((3, 4, span), F32),
            pltpu.SemaphoreType.DMA((16,)),
            pltpu.SemaphoreType.DMA((cells,)),
        ],
        compiler_params=params(),
        cost_estimate=cost(50 * velocity.size, 8 * velocity.size),
        name="own",
    )(meta, velocity, left, right, corners, dn_lo, dn_hi, up_lo, up_hi, b_lo, b_hi, a_lo, a_hi)

    dn_in, up_in = pl.pallas_call(
        inflow_faces_kernel,
        out_shape=[face, face],
        in_specs=[VMEM] * many,
        out_specs=[VMEM] * 2,
        compiler_params=params(),
        cost_estimate=cost(0, 8 * noise.size),
        name="inflow_faces",
    )(*[p.reshape(ranks, comps, count * slab, part_width) for p in parts])
    b_in = on_lines(up_in, [0], 1, ranks)
    a_in = on_lines(dn_in, [0], -1, ranks)

    reach = low + 2
    return pl.pallas_call(
        inflow_kernel,
        out_shape=full,
        in_specs=[SMEM] + [ANY] * (many + 10),
        out_specs=ANY,
        scratch_shapes=[
            pltpu.VMEM((3, reach + 4, slab, span), F32),
            pltpu.VMEM((3, reach + 2, slab, span), F32),
            pltpu.VMEM((3, reach, slab, span), F32),
        ]
        + rows_scratch(low + high, span)
        + [
            pltpu.SemaphoreType.DMA((many * ranks + 13,)),
            pltpu.SemaphoreType.DMA((reach,)),
        ],
        input_output_aliases={many + 10: 0},
        compiler_params=params(),
        cost_estimate=cost(30 * velocity.size, 5 * velocity.size),
        name="inflow",
    )(meta, velocity, *parts, dn_in, up_in, b_in, a_in, dn_hi, up_hi, b_hi, a_hi, own)


def solution(mesh):
    placed = (
        P(None, "grp", "gx", None),
        P(None, None, None, "gx"),
        P(None, None, "gx"),
        P(),
        P(),
        P(),
    )
    return jax.shard_map(
        local, mesh=mesh, in_specs=placed, out_specs=P(None, "grp", "gx", None), check_vma=False
    )
```

time: 248 us -> 130 us (0.52); the launches traced: 244 us -> 130 us
  waiting for transfers between devices: 97.1 us -> 16.9 us
  Pallas kernels: 0 us -> 54.4 us
  local copies, waits for them, and re-layouts: 58.7 us -> 17.8 us
  other arithmetic: 41.6 us -> 2.11 us
  matrix products: 13.5 us -> 0 us
  starting transfers between devices: 31.9 us -> 38.2 us
    all_to_all x1 -> x2, waiting for transfers between devices: 66.7 us -> 3.62 us  [the longest x1 3.62 us: local(): got_a = lax.all_to_all(made_a, 'gx', 0, 0, tiled=True)]
    pallas_call x0 -> x7, Pallas kernels: none -> 54.4 us  [the longest x1 14.7 us: local(): pl.pallas_call(inflow_kernel, out_shape=full, in_specs=[SMEM] + [ANY] * (...]
    slice x12 -> x1, local copies, waits for them, and re-layouts: 30.4 us -> 1.47 us  [local(): right = shift(velocity[:, :2], 'grp', -1, rows)]
    add x3 -> x0, other arithmetic: 24.9 us -> none  [the longest x1 12.9 us: local(): return 0.5 * start + 0.5 * second]
    ppermute x10 -> x13, waiting for transfers between devices: 30.4 us -> 13.3 us  [the longest x1 13.2 us: local(): hop_2 = lax.ppermute(got_a, 'grp', [(2, 0)])]
    dot_general x2 -> x0, matrix products: 13.5 us -> none  [the longest x1 10.2 us: filtered(): jnp.einsum('cpzj,jy->cpzy', widened, y_band, precision=lax.Precision.HIGH...]
    concatenate x3 -> x1, other arithmetic: 13.2 us -> 0.76 us  [local(): jnp.concatenate([shift(up_corner, 'gx', 1, ranks), shift(dn_corner, 'gx',...]
    ppermute x6 -> x2, local copies, waits for them, and re-layouts: 11 us -> 4.99 us  [shift(): return lax.ppermute(array, axis, pairs)]
  transfers between devices with their start and end apart: 11 -> 15, of which waited for: 7 -> 2; matrix products, arithmetic and copies ran while one was open for 15% -> 13% of each run, Pallas kernels for 0% -> 26%
where the time goes in v1:
time: 130 us
  Pallas kernels  54.4 us (42%)
  starting transfers between devices  38.2 us (29%)
  local copies, waits for them, and re-layouts  17.8 us (14%)
  waiting for transfers between devices  16.9 us (13%)
  other arithmetic  2.11 us (2%)
    ppermute x6, starting transfers between devices, shift(): return lax.ppermute(array, axis, pairs)  15.7 us
    pallas_call x1, Pallas kernels, local(): pl.pallas_call(inflow_kernel, out_shape=full, in_specs=[SMEM] + [ANY] * (...  14.7 us
    pallas_call x1, Pallas kernels, local(): pl.pallas_call(own_kernel, out_shape=full, in_specs=[SMEM] + [ANY] * 12,...  13.5 us
    ppermute x1, waiting for transfers between devices, local(): hop_2 = lax.ppermute(got_a, 'grp', [(2, 0)])  13.2 us
    pallas_call x2, Pallas kernels, make(): pl.pallas_call(functools.partial(filter_kernel, width, with_rim), out_sha...  11.3 us
    ppermute x4, starting transfers between devices, on_lines(): return lax.ppermute(array, ('grp', 'gx'), pairs)  8.79 us
    unnamed x30, local copies, waits for them, and re-layouts  6.6 us
    pallas_call x1, Pallas kernels, local(): pl.pallas_call(rim_kernel, out_shape=jax.ShapeDtypeStruct(packed, F32), i...  6.09 us
  transfers between devices with their start and end apart: 15, of which 2 were waited for; matrix products, arithmetic and copies ran while one was open for 13% of the time, Pallas kernels for 26%

profile of v1, /device:TPU:1, one launch (start us, length us, event | category | flops | bytes accessed | tf_op | source)
XLA Modules:
  0.0 129.7 jit_solution(10309011956559174424)
XLA Ops:
  0.0 0.0 copy-start.11
  0.0 6.1 %rim.1.rim_ref = f32[3,8,16,128]{3,2,1,0:T(8,128)} custom-call(s32[1]{0:T(128)} %bitcast.8.left_ref, f32[3,8,64,512]{3,2,1,0:T(8,128)} %noise_ref.5), custom_call_target="tpu_custom_call" | custom-call | bytes 3145728 | tf_op jit(solution)/shard_map/rim/pallas_call | solution.py:446
  6.1 2.7 %collective-permute-start = (f32[3,8,16,128]{3,2,1,0:T(8,128)}, f32[3,8,16,128]{3,2,1,0:T(8,128)S(1)}, u32[]{:S(2)}, u32[]{:S(2)}) collective-permute-start(f32[3,8,16,128]{3,2,1,0:T(8,128)} %rim.1.rim_ref), channel_id=1, source_target_pairs={{0,1},{1,2},{2,3},{3,4},{4,5},{5,6},{6,7},{7,0},{8,9},{9,10},{10,1... | collective-permute-start | bytes 589832 | tf_op jit(solution)/shard_map/ppermute | solution.py:459
  8.8 1.5 %fusion = (f32[3,2,8,4096]{3,2,1,0:T(8,128)S(1)}, f32[3,2,8,4096]{3,2,1,0:T(8,128)S(1)}) fusion(f32[3,16,8,4096]{3,2,1,0:T(8,128)} %vel.3), kind=kLoop, calls=%fused_computation.10 | loop fusion | bytes 3145728 | tf_op jit(solution)/shard_map/slice | solution.py:479
  10.3 1.5 %copy.12 = f32[3,2,8,4096]{3,1,2,0:T(2,128)} copy(f32[3,2,8,4096]{3,2,1,0:T(8,128)S(1)} %get-tuple-element.18) | data formatting | bytes 1572864
  11.8 3.2 %collective-permute-start.7 = (f32[3,2,8,4096]{3,1,2,0:T(2,128)}, f32[3,2,8,4096]{3,1,2,0:T(2,128)S(1)}, u32[]{:S(2)}, u32[]{:S(2)}) collective-permute-start(f32[3,2,8,4096]{3,1,2,0:T(2,128)} %copy.12), channel_id=1, source_target_pairs={{0,8},{8,16},{16,24},{1,9},{9,17},{17,25},{2,10},{10,18},{18,26},{... | collective-permute-start | bytes 2359304 | tf_op jit(solution)/shard_map/ppermute | solution.py:422
  15.0 0.6 pad_add_fusion.meta_ref
  15.6 0.0 copy-done.10
  15.6 0.7 fusion.1
  16.3 0.0 collective-permute-done.rim_ref
  16.3 0.0 copy-done.13
  16.3 0.7 broadcast_in_dim.8.mean_ref
  17.0 0.7 broadcast_in_dim.6.decay_ref
  17.7 0.8 broadcast_in_dim.7.factor_ref
  18.6 5.7 %filter_a.1 = f32[8,3,8,8,128]{4,3,2,1,0:T(8,128)} custom-call(s32[2]{0:T(128)} %pad_add_fusion.meta_ref, f32[3,8,64,512]{3,2,1,0:T(8,128)} %noise_ref.5, f32[3,8,16,128]{3,2,1,0:T(8,128)} %copy-done.9, f32[3,64,128]{2,1,0:T(8,128)} %get-tuple-element.24.prev_ref, f32[3,64,128]{2,1,0:T(8,128)} %broadcast_in_dim.6.decay_ref, ...), custom_call_target="tpu_custom_call" | custom-call | flops 603979776 | bytes 3145728 | tf_op jit(solution)/shard_map/filter_a/pallas_call | solution.py:495
  24.3 4.0 %all-to-all-start = ((f32[8,3,8,8,128]{4,3,2,1,0:T(8,128)}), f32[8,3,8,8,128]{4,3,2,1,0:T(8,128)S(1)}, u32[]{:S(2)}, u32[]{:S(2)}) async-start(f32[8,3,8,8,128]{4,3,2,1,0:T(8,128)} %filter_a.1), calls=%async_computation | async-start | bytes 1572864 | tf_op jit(solution)/shard_map/all_to_all | solution.py:509
  28.3 1.5 %copy.13 = f32[3,2,8,4096]{3,1,2,0:T(2,128)} copy(f32[3,2,8,4096]{3,2,1,0:T(8,128)S(1)} %get-tuple-element.17) | data formatting | bytes 1572864
  29.8 1.3 collective-permute-start.8
  31.1 5.6 %faces.1 = (f32[3,2,8,4096]{3,2,1,0:T(8,128)}, f32[3,2,8,4096]{3,2,1,0:T(8,128)}, f32[3,2,8,4096]{3,2,1,0:T(8,128)}, f32[3,2,8,4096]{3,2,1,0:T(8,128)}) custom-call(f32[3,128,4096]{2,1,0:T(8,128)} %bitcast.22), custom_call_target="tpu_custom_call" | custom-call | bytes 12582912 | tf_op jit(solution)/shard_map/faces/pallas_call | solution.py:463
  36.7 0.0 copy-start.2
  36.7 0.0 copy-start.3
  36.7 1.7 %collective-permute-start.12 = (f32[3,2,8,4096]{3,2,1,0:T(8,128)}, f32[3,2,8,4096]{3,2,1,0:T(8,128)}, u32[]{:S(2)}, u32[]{:S(2)}) collective-permute-start(f32[3,2,8,4096]{3,2,1,0:T(8,128)} %get-tuple-element.15.dn_lo), channel_id=1, source_target_pairs={{9,8},{10,9},{11,10},{12,11},{13,12},{14,13},{15,14},{17,16},{18,1... | collective-permute-start | bytes 2359304 | tf_op jit(solution)/shard_map/ppermute | solution.py:430
  38.4 0.6 pad_add_fusion.1.meta_ref
  38.9 5.6 %filter_b.1 = f32[8,3,8,8,128]{4,3,2,1,0:T(8,128)} custom-call(s32[2]{0:T(128)} %pad_add_fusion.1.meta_ref, f32[3,8,64,512]{3,2,1,0:T(8,128)} %noise_ref.5, f32[3,8,16,128]{3,2,1,0:T(8,128)} %rim.1.rim_ref, f32[3,64,128]{2,1,0:T(8,128)} %get-tuple-element.23.prev_ref, f32[3,64,128]{2,1,0:T(8,128)} %broadcast_in_dim.6.decay_ref, ...), custom_call_target="tpu_custom_call" | custom-call | flops 603979776 | bytes 3145728 | tf_op jit(solution)/shard_map/filter_b/pallas_call | solution.py:495
  44.5 0.0 collective-permute-done.7
  44.5 0.1 slice_bitcast_fusion.3
  44.6 3.6 %all-to-all-done.refs_1_ = f32[8,3,8,8,128]{4,3,2,1,0:T(8,128)S(1)} async-done(((f32[8,3,8,8,128]{4,3,2,1,0:T(8,128)}), f32[8,3,8,8,128]{4,3,2,1,0:T(8,128)S(1)}, u32[]{:S(2)}, u32[]{:S(2)}) %all-to-all-start) | async-done | bytes 786464 | tf_op jit(solution)/shard_map/all_to_all | solution.py:509
  48.3 4.4 %all-to-all-start.1 = ((f32[8,3,8,8,128]{4,3,2,1,0:T(8,128)}), f32[8,3,8,8,128]{4,3,2,1,0:T(8,128)S(1)}, u32[]{:S(2)}, u32[]{:S(2)}) async-start(f32[8,3,8,8,128]{4,3,2,1,0:T(8,128)} %filter_b.1), calls=%async_computation.1 | async-start | bytes 1572864 | tf_op jit(solution)/shard_map/all_to_all | solution.py:510
  52.7 0.0 collective-permute-done.8
  52.7 1.0 slice_bitcast_fusion.2
  53.7 1.3 collective-permute-start.2
  55.0 1.3 collective-permute-start.1
  56.3 0.1 pad_maximum_fusion.2
  56.4 2.5 %collective-permute-start.10 = (f32[3,2,4096]{2,1,0:T(2,128)S(1)}, f32[3,2,4096]{2,1,0:T(2,128)S(1)}, u32[]{:S(2)}, u32[]{:S(2)}) collective-permute-start(f32[3,2,4096]{2,1,0:T(2,128)S(1)} %pad_maximum_fusion.2), channel_id=1, source_target_pairs={{1,0},{2,1},{3,2},{4,3},{5,4},{6,5},{7,6},{9,8},{10,9},{11,10},{12... | collective-permute-start | bytes 294920 | tf_op jit(solution)/shard_map/ppermute | solution.py:422
  58.9 0.1 pad_maximum_fusion.1
  59.0 3.2 %collective-permute-start.9 = (f32[3,2,4096]{2,1,0:T(2,128)S(1)}, f32[3,2,4096]{2,1,0:T(2,128)S(1)}, u32[]{:S(2)}, u32[]{:S(2)}) collective-permute-start(f32[3,2,4096]{2,1,0:T(2,128)S(1)} %pad_maximum_fusion.1), channel_id=1, source_target_pairs={{0,1},{1,2},{2,3},{3,4},{4,5},{5,6},{6,7},{8,9},{9,10},{10,11},{11... | collective-permute-start | bytes 294920 | tf_op jit(solution)/shard_map/ppermute | solution.py:422
  62.2 0.0 collective-permute-done.12.a_lo
  62.2 1.5 %collective-permute-start.11 = (f32[3,2,8,4096]{3,2,1,0:T(8,128)}, f32[3,2,8,4096]{3,2,1,0:T(8,128)}, u32[]{:S(2)}, u32[]{:S(2)}) collective-permute-start(f32[3,2,8,4096]{3,2,1,0:T(8,128)} %get-tuple-element.16.up_lo), channel_id=1, source_target_pairs={{8,9},{9,10},{10,11},{11,12},{12,13},{13,14},{14,15},{16,17},{17,1... | collective-permute-start | bytes 2359304 | tf_op jit(solution)/shard_map/ppermute | solution.py:430
  63.7 13.2 %collective-permute-done.2.refs_3_ = f32[8,3,8,8,128]{4,3,2,1,0:T(8,128)S(1)} collective-permute-done((f32[8,3,8,8,128]{4,3,2,1,0:T(8,128)S(1)}, f32[8,3,8,8,128]{4,3,2,1,0:T(8,128)S(1)}, u32[]{:S(2)}, u32[]{:S(2)}) %collective-permute-start.2) | collective-permute-done | bytes 786464 | tf_op jit(solution)/shard_map/ppermute | solution.py:512
  77.0 0.0 copy-done.2
  77.0 2.5 %collective-permute-start.6 = (f32[3,2,8,4096]{3,2,1,0:T(8,128)S(1)}, f32[3,2,8,4096]{3,2,1,0:T(8,128)}, u32[]{:S(2)}, u32[]{:S(2)}) collective-permute-start(f32[3,2,8,4096]{3,2,1,0:T(8,128)S(1)} %copy-done.2), channel_id=1, source_target_pairs={{1,0},{2,1},{3,2},{4,3},{5,4},{6,5},{7,6},{9,8},{10,9},{11,10},{12... | collective-permute-start | bytes 2359304 | tf_op jit(solution)/shard_map/ppermute | solution.py:422
  79.5 0.0 collective-permute-done.1.refs_0_
  79.5 0.9 copy-done.5
  80.4 3.1 %collective-permute-start.5 = (f32[3,2,8,4096]{3,2,1,0:T(8,128)S(1)}, f32[3,2,8,4096]{3,2,1,0:T(8,128)}, u32[]{:S(2)}, u32[]{:S(2)}) collective-permute-start(f32[3,2,8,4096]{3,2,1,0:T(8,128)S(1)} %copy-done.3), channel_id=1, source_target_pairs={{0,1},{1,2},{2,3},{3,4},{4,5},{5,6},{6,7},{8,9},{9,10},{10,11},{11... | collective-permute-start | bytes 2359304 | tf_op jit(solution)/shard_map/ppermute | solution.py:422
  83.5 0.0 all-to-all-done.1.refs_2_
  83.6 0.9 copy-done.1
  84.4 3.3 %inflow_faces.1 = (f32[3,2,8,4096]{3,2,1,0:T(8,128)}, f32[3,2,8,4096]{3,2,1,0:T(8,128)}) custom-call(f32[8,3,64,128]{3,2,1,0:T(8,128)} %bitcast.26, f32[8,3,64,128]{3,2,1,0:T(8,128)} %bitcast.23, f32[8,3,64,128]{3,2,1,0:T(8,128)} %bitcast.24, f32[8,3,64,128]{3,2,1,0:T(8,128)} %bitcast.25), custom_call_target="tpu_custom_call" | custom-call | bytes 6291456 | tf_op jit(solution)/shard_map/inflow_faces/pallas_call | solution.py:556
  87.7 0.0 collective-permute-done.10
  87.7 2.1 %collective-permute-start.4 = (f32[3,2,8,4096]{3,2,1,0:T(8,128)}, f32[3,2,8,4096]{3,2,1,0:T(8,128)S(1)}, u32[]{:S(2)}, u32[]{:S(2)}) collective-permute-start(f32[3,2,8,4096]{3,2,1,0:T(8,128)} %get-tuple-element.11.refs_4_), channel_id=1, source_target_pairs={{1,0},{2,1},{3,2},{4,3},{5,4},{6,5},{7,6}} | collective-permute-start | bytes 2359304 | tf_op jit(solution)/shard_map/ppermute | solution.py:430
  89.8 0.0 collective-permute-done.9
  89.8 3.5 %collective-permute-start.3 = (f32[3,2,8,4096]{3,2,1,0:T(8,128)}, f32[3,2,8,4096]{3,2,1,0:T(8,128)S(1)}, u32[]{:S(2)}, u32[]{:S(2)}) collective-permute-start(f32[3,2,8,4096]{3,2,1,0:T(8,128)} %get-tuple-element.12.refs_5_), channel_id=1, source_target_pairs={{0,1},{1,2},{2,3},{3,4},{4,5},{5,6},{6,7}} | collective-permute-start | bytes 2359304 | tf_op jit(solution)/shard_map/ppermute | solution.py:430
  93.3 0.7 stack.66.meta
  94.0 2.5 %copy.10.left = f32[3,2,8,4096]{3,2,1,0:T(8,128)} copy(f32[3,2,8,4096]{3,1,2,0:T(2,128)} %copy-done.6) | data formatting | bytes 1572864 | tf_op jit(solution)/shard_map/ppermute | solution.py:422
  96.5 2.5 %copy.11.right = f32[3,2,8,4096]{3,2,1,0:T(8,128)} copy(f32[3,2,8,4096]{3,1,2,0:T(2,128)} %collective-permute-done.8) | data formatting | bytes 1572864 | tf_op jit(solution)/shard_map/ppermute | solution.py:422
  99.0 0.8 pad_maximum_fusion.corners
  99.7 0.0 collective-permute-done.11.b_lo
  99.7 0.0 collective-permute-done.6.a_hi.refs_11_
  99.7 0.0 collective-permute-done.5.b_hi.refs_10_
  99.7 13.5 %own.1.refs_12_ = f32[3,16,8,4096]{3,2,1,0:T(8,128)} custom-call(s32[6]{0:T(128)} %stack.66.meta, f32[3,16,8,4096]{3,2,1,0:T(8,128)} %vel.3, f32[3,2,8,4096]{3,2,1,0:T(8,128)} %copy.10.left, f32[3,2,8,4096]{3,2,1,0:T(8,128)} %copy.11.right, f32[3,4,4096]{2,1,0:T(4,128)} %pad_maximum_fusion.corners, f32[3,2,8,4096]{3,2,1,0:T(8,128)} %get-tuple-element.15.dn_lo, ...), custom_call_target="tpu_custom_call" | custom-call | flops 78643200 | bytes 12582912 | tf_op jit(solution)/shard_map/own/pallas_call | solution.py:535
  113.2 0.0 collective-permute-done.4.refs_7_
  113.2 0.0 collective-permute-done.3.refs_6_
  113.2 0.9 copy-done.7
  114.1 0.9 copy-done.8
  115.0 14.7 %inflow.1 = f32[3,16,8,4096]{3,2,1,0:T(8,128)} custom-call(s32[6]{0:T(128)} %stack.66.meta, f32[3,16,8,4096]{3,2,1,0:T(8,128)} %vel.3, f32[8,3,8,8,128]{4,3,2,1,0:T(8,128)} %copy-done.5, f32[8,3,8,8,128]{4,3,2,1,0:T(8,128)} %copy-done, f32[8,3,8,8,128]{4,3,2,1,0:T(8,128)} %copy-done.1, ...), custom_call_target="tpu_custom_call", output_to_operand_aliasing={{}: (14, {})} | custom-call | flops 47185920 | bytes 7864320 | tf_op jit(solution)/shard_map/inflow/pallas_call | solution.py:569
  (18 shorter events, 0.0 us)
Async XLA Ops:
  0.0 15.6 %copy-start.10 = (f32[3,64,512]{2,1,0:T(8,128)S(1)}, f32[3,64,512]{2,1,0:T(8,128)}, u32[]{:S(2)}) copy-start(f32[3,64,512]{2,1,0:T(8,128)} %param.8) | copy-start | bytes 1179652
  0.0 16.3 %copy-start.13 = (f32[64]{0:T(128)S(1)}, f32[64]{0:T(128)}, u32[]{:S(2)}) copy-start(f32[64]{0:T(128)} %param.11) | copy-start | bytes 772
  0.0 17.0 %copy-start.12 = (f32[3,64]{1,0:T(4,128)S(1)}, f32[3,64]{1,0:T(4,128)}, u32[]{:S(2)}) copy-start(f32[3,64]{1,0:T(4,128)} %param.9) | copy-start | bytes 2308
  0.0 17.7 %copy-start.11 = (f32[6,64]{1,0:T(8,128)S(1)}, f32[6,64]{1,0:T(8,128)}, u32[]{:S(2)}) copy-start(f32[6,64]{1,0:T(8,128)} %param.10) | copy-start | bytes 4612
  6.1 10.2 %collective-permute-start = (f32[3,8,16,128]{3,2,1,0:T(8,128)}, f32[3,8,16,128]{3,2,1,0:T(8,128)S(1)}, u32[]{:S(2)}, u32[]{:S(2)}) collective-permute-start(f32[3,8,16,128]{3,2,1,0:T(8,128)} %rim.1.rim_ref), channel_id=1, source_target_pairs={{0,1},{1,2},{2,3},{3,4},{4,5},{5,6},{6,7},{7,0},{8,9},{9,10},{10,1... | collective-permute-start | bytes 589832 | tf_op jit(solution)/shard_map/ppermute | solution.py:459
  11.8 32.7 %collective-permute-start.7 = (f32[3,2,8,4096]{3,1,2,0:T(2,128)}, f32[3,2,8,4096]{3,1,2,0:T(2,128)S(1)}, u32[]{:S(2)}, u32[]{:S(2)}) collective-permute-start(f32[3,2,8,4096]{3,1,2,0:T(2,128)} %copy.12), channel_id=1, source_target_pairs={{0,8},{8,16},{16,24},{1,9},{9,17},{17,25},{2,10},{10,18},{18,26},{... | collective-permute-start | bytes 2359304 | tf_op jit(solution)/shard_map/ppermute | solution.py:422
  16.3 2.2 %copy-start.9 = (f32[3,8,16,128]{3,2,1,0:T(8,128)}, f32[3,8,16,128]{3,2,1,0:T(8,128)S(1)}, u32[]{:S(2)}) copy-start(f32[3,8,16,128]{3,2,1,0:T(8,128)S(1)} %collective-permute-done.rim_ref) | copy-start | bytes 589828
  24.3 24.0 %all-to-all-start = ((f32[8,3,8,8,128]{4,3,2,1,0:T(8,128)}), f32[8,3,8,8,128]{4,3,2,1,0:T(8,128)S(1)}, u32[]{:S(2)}, u32[]{:S(2)}) async-start(f32[8,3,8,8,128]{4,3,2,1,0:T(8,128)} %filter_a.1), calls=%async_computation | async-start | bytes 1572864 | tf_op jit(solution)/shard_map/all_to_all | solution.py:509
  29.8 22.9 %collective-permute-start.8 = (f32[3,2,8,4096]{3,1,2,0:T(2,128)}, f32[3,2,8,4096]{3,1,2,0:T(2,128)}, u32[]{:S(2)}, u32[]{:S(2)}) collective-permute-start(f32[3,2,8,4096]{3,1,2,0:T(2,128)} %copy.13), channel_id=1, source_target_pairs={{8,0},{16,8},{24,16},{9,1},{17,9},{25,17},{10,2},{18,10},{26,18},{... | collective-permute-start | bytes 2359304 | tf_op jit(solution)/shard_map/ppermute | solution.py:422
  36.7 40.3 %copy-start.2 = (f32[3,2,8,4096]{3,2,1,0:T(8,128)S(1)}, f32[3,2,8,4096]{3,2,1,0:T(8,128)}, u32[]{:S(2)}) copy-start(f32[3,2,8,4096]{3,2,1,0:T(8,128)} %get-tuple-element.13.dn_hi.refs_8_) | copy-start | bytes 2359300
  36.7 43.7 %copy-start.3 = (f32[3,2,8,4096]{3,2,1,0:T(8,128)S(1)}, f32[3,2,8,4096]{3,2,1,0:T(8,128)}, u32[]{:S(2)}) copy-start(f32[3,2,8,4096]{3,2,1,0:T(8,128)} %get-tuple-element.14.up_hi.refs_9_) | copy-start | bytes 2359300
  36.7 25.5 %collective-permute-start.12 = (f32[3,2,8,4096]{3,2,1,0:T(8,128)}, f32[3,2,8,4096]{3,2,1,0:T(8,128)}, u32[]{:S(2)}, u32[]{:S(2)}) collective-permute-start(f32[3,2,8,4096]{3,2,1,0:T(8,128)} %get-tuple-element.15.dn_lo), channel_id=1, source_target_pairs={{9,8},{10,9},{11,10},{12,11},{13,12},{14,13},{15,14},{17,16},{18,1... | collective-permute-start | bytes 2359304 | tf_op jit(solution)/shard_map/ppermute | solution.py:430
  44.5 3.7 %copy-start.6 = (f32[3,2,8,4096]{3,1,2,0:T(2,128)}, f32[3,2,8,4096]{3,1,2,0:T(2,128)S(1)}, u32[]{:S(2)}) copy-start(f32[3,2,8,4096]{3,1,2,0:T(2,128)S(1)} %collective-permute-done.7) | copy-start | bytes 2359300
  48.3 35.3 %copy-start = (f32[8,3,8,8,128]{4,3,2,1,0:T(8,128)}, f32[8,3,8,8,128]{4,3,2,1,0:T(8,128)S(1)}, u32[]{:S(2)}) copy-start(f32[8,3,8,8,128]{4,3,2,1,0:T(8,128)S(1)} %all-to-all-done.refs_1_) | copy-start | bytes 2359300
  48.3 35.3 %all-to-all-start.1 = ((f32[8,3,8,8,128]{4,3,2,1,0:T(8,128)}), f32[8,3,8,8,128]{4,3,2,1,0:T(8,128)S(1)}, u32[]{:S(2)}, u32[]{:S(2)}) async-start(f32[8,3,8,8,128]{4,3,2,1,0:T(8,128)} %filter_b.1), calls=%async_computation.1 | async-start | bytes 1572864 | tf_op jit(solution)/shard_map/all_to_all | solution.py:510
  53.7 23.3 %collective-permute-start.2 = (f32[8,3,8,8,128]{4,3,2,1,0:T(8,128)S(1)}, f32[8,3,8,8,128]{4,3,2,1,0:T(8,128)S(1)}, u32[]{:S(2)}, u32[]{:S(2)}) collective-permute-start(f32[8,3,8,8,128]{4,3,2,1,0:T(8,128)S(1)} %all-to-all-done.refs_1_), channel_id=1, source_target_pairs={{16,0},{17,1},{18,2},{19,3},{20,4},{21,5},{22,6},{23,7}} | collective-permute-start | bytes 2359304 | tf_op jit(solution)/shard_map/ppermute | solution.py:512
  55.0 24.5 %collective-permute-start.1 = (f32[8,3,8,8,128]{4,3,2,1,0:T(8,128)S(1)}, f32[8,3,8,8,128]{4,3,2,1,0:T(8,128)S(1)}, u32[]{:S(2)}, u32[]{:S(2)}) collective-permute-start(f32[8,3,8,8,128]{4,3,2,1,0:T(8,128)S(1)} %all-to-all-done.refs_1_), channel_id=1, source_target_pairs={{8,0},{9,1},{10,2},{11,3},{12,4},{13,5},{14,6},{15,7}} | collective-permute-start | bytes 2359304 | tf_op jit(solution)/shard_map/ppermute | solution.py:511
  56.4 31.3 %collective-permute-start.10 = (f32[3,2,4096]{2,1,0:T(2,128)S(1)}, f32[3,2,4096]{2,1,0:T(2,128)S(1)}, u32[]{:S(2)}, u32[]{:S(2)}) collective-permute-start(f32[3,2,4096]{2,1,0:T(2,128)S(1)} %pad_maximum_fusion.2), channel_id=1, source_target_pairs={{1,0},{2,1},{3,2},{4,3},{5,4},{6,5},{7,6},{9,8},{10,9},{11,10},{12... | collective-permute-start | bytes 294920 | tf_op jit(solution)/shard_map/ppermute | solution.py:422
  59.0 30.8 %collective-permute-start.9 = (f32[3,2,4096]{2,1,0:T(2,128)S(1)}, f32[3,2,4096]{2,1,0:T(2,128)S(1)}, u32[]{:S(2)}, u32[]{:S(2)}) collective-permute-start(f32[3,2,4096]{2,1,0:T(2,128)S(1)} %pad_maximum_fusion.1), channel_id=1, source_target_pairs={{0,1},{1,2},{2,3},{3,4},{4,5},{5,6},{6,7},{8,9},{9,10},{10,11},{11... | collective-permute-start | bytes 294920 | tf_op jit(solution)/shard_map/ppermute | solution.py:422
  62.2 37.5 %collective-permute-start.11 = (f32[3,2,8,4096]{3,2,1,0:T(8,128)}, f32[3,2,8,4096]{3,2,1,0:T(8,128)}, u32[]{:S(2)}, u32[]{:S(2)}) collective-permute-start(f32[3,2,8,4096]{3,2,1,0:T(8,128)} %get-tuple-element.16.up_lo), channel_id=1, source_target_pairs={{8,9},{9,10},{10,11},{11,12},{12,13},{13,14},{14,15},{16,17},{17,1... | collective-permute-start | bytes 2359304 | tf_op jit(solution)/shard_map/ppermute | solution.py:430
  77.0 2.5 %copy-start.4 = (f32[8,3,8,8,128]{4,3,2,1,0:T(8,128)}, f32[8,3,8,8,128]{4,3,2,1,0:T(8,128)S(1)}, u32[]{:S(2)}) copy-start(f32[8,3,8,8,128]{4,3,2,1,0:T(8,128)S(1)} %collective-permute-done.2.refs_3_) | copy-start | bytes 2359300
  77.0 22.8 %collective-permute-start.6 = (f32[3,2,8,4096]{3,2,1,0:T(8,128)S(1)}, f32[3,2,8,4096]{3,2,1,0:T(8,128)}, u32[]{:S(2)}, u32[]{:S(2)}) collective-permute-start(f32[3,2,8,4096]{3,2,1,0:T(8,128)S(1)} %copy-done.2), channel_id=1, source_target_pairs={{1,0},{2,1},{3,2},{4,3},{5,4},{6,5},{7,6},{9,8},{10,9},{11,10},{12... | collective-permute-start | bytes 2359304 | tf_op jit(solution)/shard_map/ppermute | solution.py:422
  79.5 0.9 copy-start.5
  80.4 19.4 %collective-permute-start.5 = (f32[3,2,8,4096]{3,2,1,0:T(8,128)S(1)}, f32[3,2,8,4096]{3,2,1,0:T(8,128)}, u32[]{:S(2)}, u32[]{:S(2)}) collective-permute-start(f32[3,2,8,4096]{3,2,1,0:T(8,128)S(1)} %copy-done.3), channel_id=1, source_target_pairs={{0,1},{1,2},{2,3},{3,4},{4,5},{5,6},{6,7},{8,9},{9,10},{10,11},{11... | collective-permute-start | bytes 2359304 | tf_op jit(solution)/shard_map/ppermute | solution.py:422
  83.6 0.9 copy-start.1
  87.7 25.5 %collective-permute-start.4 = (f32[3,2,8,4096]{3,2,1,0:T(8,128)}, f32[3,2,8,4096]{3,2,1,0:T(8,128)S(1)}, u32[]{:S(2)}, u32[]{:S(2)}) collective-permute-start(f32[3,2,8,4096]{3,2,1,0:T(8,128)} %get-tuple-element.11.refs_4_), channel_id=1, source_target_pairs={{1,0},{2,1},{3,2},{4,3},{5,4},{6,5},{7,6}} | collective-permute-start | bytes 2359304 | tf_op jit(solution)/shard_map/ppermute | solution.py:430
  89.8 23.4 %collective-permute-start.3 = (f32[3,2,8,4096]{3,2,1,0:T(8,128)}, f32[3,2,8,4096]{3,2,1,0:T(8,128)S(1)}, u32[]{:S(2)}, u32[]{:S(2)}) collective-permute-start(f32[3,2,8,4096]{3,2,1,0:T(8,128)} %get-tuple-element.12.refs_5_), channel_id=1, source_target_pairs={{0,1},{1,2},{2,3},{3,4},{4,5},{5,6},{6,7}} | collective-permute-start | bytes 2359304 | tf_op jit(solution)/shard_map/ppermute | solution.py:430
  113.2 0.9 copy-start.7
  114.1 0.9 copy-start.8

commit v2 on v1

v2 whole, which is shorter than its diff:
```python
import functools
import math

import jax
import jax.numpy as jnp
from jax import lax
from jax.experimental import pallas as pl
from jax.experimental.pallas import tpu as pltpu
from jax.sharding import PartitionSpec as P


HALF = 32
TIME_STEP = 0.15
VISCOSITY = 0.2
LANES = 128
SUB = 8
PARTS = 4
VMEM_LIMIT = 60 * 1024 * 1024

ANY = pl.BlockSpec(memory_space=pltpu.HBM)
VMEM = pl.BlockSpec(memory_space=pltpu.VMEM)
F32 = jnp.float32


def params():
    return pltpu.CompilerParams(vmem_limit_bytes=VMEM_LIMIT)


def cost(flops, nbytes):
    return pl.CostEstimate(flops=flops, bytes_accessed=nbytes, transcendentals=0)


def kernel_norm():
    length = HALF / 2.0
    total = sum(
        math.exp(-math.pi * k * k / (2.0 * length * length)) ** 2 for k in range(-HALF, HALF + 1)
    )
    return math.sqrt(total)


def weights(offset):
    length = HALF / 2.0
    off = offset.astype(F32)
    value = jnp.exp(off * off * (-math.pi / (2.0 * length * length))) * (1.0 / kernel_norm())
    return jnp.where(jnp.abs(offset) <= HALF, value, 0.0)


def split(x):
    high = x.astype(jnp.bfloat16)
    low = (x - high.astype(F32)).astype(jnp.bfloat16)
    return high, low


def dot(a, b):
    return jnp.dot(a, b, preferred_element_type=F32)


def first_kernel(noise, rim_ref, edge, sem):
    comps, count, depth, span = noise.shape
    groups = LANES // HALF
    rows = depth // groups
    use_left = lax.axis_index("grp") == 2
    at = pl.multiple_of(jnp.where(use_left, 0, span - LANES), LANES)
    copies = [
        pltpu.make_async_copy(noise.at[c, :, :, pl.ds(at, LANES)], edge.at[c], sem.at[c])
        for c in range(comps)
    ]
    for copy in copies:
        copy.start()
    lane = lax.broadcasted_iota(jnp.int32, (count, rows, LANES), 2)
    for c in range(comps):
        copies[c].wait()
        result = None
        for q in range(groups):
            piece = edge[c, :, rows * q : rows * (q + 1), :]
            to_left = piece if q == 0 else pltpu.roll(piece, HALF * q, 2)
            to_right = pltpu.roll(piece, (HALF * (q + 1)) % LANES, 2) if (q + 1) % groups else piece
            piece = jnp.where(use_left, to_left, to_right)
            result = piece if q == 0 else jnp.where(lane >= HALF * q, piece, result)
        rim_ref[c] = result


def face_copies(vel, first, cells, dn, up, sem, at):
    slab = vel.shape[2]
    copies = []
    for c in range(3):
        for j in range(2):
            for ref, z in ((dn, j), (up, slab - 2 + j)):
                copies.append(
                    pltpu.make_async_copy(
                        vel.at[c, pl.ds(first, cells), z], ref.at[c, j], sem.at[at + len(copies)]
                    )
                )
    return copies


def xfaces_kernel(vel, after, near_ref, far_ref, sem):
    del after
    cells = vel.shape[1]
    even = lax.rem(lax.axis_index("grp"), 2) == 0
    at = jnp.where(even, cells - 2, 0)
    run_copies(
        [
            pltpu.make_async_copy(vel.at[:, pl.ds(at, 2)], near_ref, sem.at[0]),
            pltpu.make_async_copy(vel.at[:, pl.ds(cells - 2 - at, 2)], far_ref, sem.at[1]),
        ]
    )


def zfaces_kernel(vel, after, all_dn, all_up, high_dn, high_up, sem):
    del after
    cells, high = all_dn.shape[2], high_dn.shape[2]
    is_first = lax.axis_index("grp") == 0

    @pl.when(is_first)
    def _():
        run_copies(face_copies(vel, cells - high, high, high_dn, high_up, sem, 0))

    @pl.when(jnp.logical_not(is_first))
    def _():
        run_copies(face_copies(vel, 0, cells, all_dn, all_up, sem, 0))


def mark_kernel(after, out_ref):
    del after
    out_ref[...] = jnp.zeros_like(out_ref)


def column(ref, c, width):
    depth = ref.shape[1]
    row = lax.broadcasted_iota(jnp.int32, (depth, depth), 0)
    col = lax.broadcasted_iota(jnp.int32, (depth, depth), 1)
    value = jnp.where(row == col, jnp.broadcast_to(ref[c : c + 1, :], (depth, depth)), 0.0)
    return jnp.broadcast_to(jnp.sum(value, axis=1, keepdims=True), (depth, width))


def part_of(line):
    return jnp.where(line == 0, 1, jnp.where(line == 1, 0, jnp.where(line == 2, PARTS - 1, 2)))


def window_of(line, width, whole, span):
    first = part_of(line) * width
    start = jnp.minimum(jnp.maximum((first - HALF) // LANES * LANES, 0), whole - span)
    return first, pl.multiple_of(start, LANES)


def spanwise_band(base, span, width):
    row = lax.broadcasted_iota(jnp.int32, (span, width), 0)
    col = lax.broadcasted_iota(jnp.int32, (span, width), 1)
    high, low = split(weights(row - col - base))
    return jnp.concatenate([high, high, low], axis=0)


def window_copies(noise, noise_ref, start, sem):
    comps, _, _, span = noise_ref.shape
    return [
        pltpu.make_async_copy(noise.at[c, :, :, pl.ds(start, span)], noise_ref.at[c], sem.at[c])
        for c in range(comps)
    ]


def along_kernel(noise, out_ref, noise_ref, sem):
    comps, count, depth, span = noise_ref.shape
    width = out_ref.shape[3]
    line = lax.axis_index("grp")
    first, start = window_of(line, width, noise.shape[3], span)
    copies = window_copies(noise, noise_ref, start, sem)
    for copy in copies:
        copy.start()
    band = spanwise_band(first - start, span, width)
    for c in range(comps):
        copies[c].wait()
        high, low = split(noise_ref[c].reshape(count * depth, span))
        along = dot(jnp.concatenate([high, low, high], axis=1), band)
        out_ref[c] = along.reshape(count, depth, width)


def filter_kernel(whole, along_hbm, rim, after, previous, decay_ref, factor_ref, mean_ref,
                    out_ref, planes_ref, prev_ref, along_ref, rim_ref, sem):
    del after
    comps, count, depth, width = along_ref.shape
    line = lax.axis_index("grp")
    first = part_of(line) * width
    before = previous_copy(previous, prev_ref, first, sem.at[0])
    rim_copy = pltpu.make_async_copy(rim, rim_ref, sem.at[1])
    along_copies = [
        pltpu.make_async_copy(along_hbm.at[c], along_ref.at[c], sem.at[2 + c])
        for c in range(comps)
    ]
    for copy in [rim_copy, before] + along_copies:
        copy.start()
    groups = LANES // HALF
    rows = depth // groups
    rim_at = jnp.where(line == 2, whole, -HALF) - first
    hrow = lax.broadcasted_iota(jnp.int32, (LANES, width), 0)
    hcol = lax.broadcasted_iota(jnp.int32, (LANES, width), 1)
    bands = []
    for q in range(groups):
        cell = hrow - HALF * q
        value = weights(cell + rim_at - hcol)
        high, low = split(jnp.where((cell >= 0) & (cell < HALF), value, 0.0))
        bands.append(jnp.concatenate([high, high, low], axis=0))
    band = jnp.concatenate(bands, axis=1)

    rim_copy.wait()

    def along(c):
        along_copies[c].wait()
        high, low = split(rim_ref[c].reshape(count * rows, LANES))
        part = dot(jnp.concatenate([high, low, high], axis=1), band)
        part = part.reshape(count, rows, groups * width)
        extra = [part[:, :, width * q : width * (q + 1)] for q in range(groups)]
        return along_ref[c] + jnp.concatenate(extra, axis=1)

    inflow_planes(along, before, decay_ref, factor_ref, mean_ref, out_ref, planes_ref, prev_ref)


def previous_copy(previous, prev_ref, first, sem):
    width = prev_ref.shape[2]
    if width % LANES == 0:
        previous = previous.at[:, :, pl.ds(pl.multiple_of(first, LANES), width)]
    return pltpu.make_async_copy(previous, prev_ref, sem)


def inflow_planes(along, before, decay_ref, factor_ref, mean_ref, out_ref, planes_ref, prev_ref):
    comps, count, depth, width = planes_ref.shape
    zrow = lax.broadcasted_iota(jnp.int32, (depth, depth), 0)
    zcol = lax.broadcasted_iota(jnp.int32, (depth, depth), 1)
    zh, zl = split(weights(zrow - zcol))
    zband = jnp.concatenate([zh, zh, zl], axis=1)
    for c in range(comps):
        value = along(c)
        wide = jnp.concatenate([value[p] for p in range(count)], axis=1)
        yh, yl = split(wide)
        smooth = dot(zband, jnp.concatenate([yh, yl, yh], axis=0))
        if c == 0:
            before.wait()
        dec = column(decay_ref, c, width)
        scale = jnp.sqrt(1.0 - dec * dec)
        carried = prev_ref[c]
        for p in range(count):
            carried = dec * carried + scale * smooth[:, p * width : (p + 1) * width]
            planes_ref[c, p] = carried
    owners = out_ref.shape[0]
    slab = depth // owners

    def put(c, p, value):
        for d in range(owners):
            out_ref[d, c, p] = value[slab * d : slab * (d + 1)]

    mean = column(mean_ref, 0, width)
    factor = [column(factor_ref, i, width) for i in range(6)]
    for p in range(count):
        a, b, d = planes_ref[0, p], planes_ref[1, p], planes_ref[2, p]
        put(0, p, mean + factor[0] * a)
        put(1, p, factor[1] * a + factor[2] * b)
        put(2, p, factor[3] * a + factor[4] * b + factor[5] * d)


def sides(near, far):
    even = lax.rem(lax.axis_index("grp"), 2) == 0
    return [(even, far, near), (jnp.logical_not(even), near, far)]


def corners_kernel(near, far, after, up_ref, dn_ref, sem):
    del after
    slab = near.shape[2]

    def rows(left, right):
        copies = []
        for ref, z in ((up_ref, slab - 1), (dn_ref, 0)):
            for i, (face, x) in enumerate(((left, 1), (right, 0))):
                for c in range(3):
                    copies.append(
                        pltpu.make_async_copy(face.at[c, x, z], ref.at[c, i], sem.at[len(copies)])
                    )
        return copies

    for condition, left, right in sides(near, far):

        @pl.when(condition)
        def _(left=left, right=right):
            run_copies(rows(left, right))


def inflow_faces_kernel(places, *refs):
    pieces = refs[:-3]
    dn, up, sem = refs[-3:]
    copies = []
    for piece, (source, part, parts) in zip(pieces, places):
        slab, width = piece.shape[3:]
        for s in range(piece.shape[0]):
            at = ((source + s) * parts + part) * width
            for j in range(2):
                for ref, z in ((dn, j), (up, slab - 2 + j)):
                    copies.append(
                        pltpu.make_async_copy(
                            piece.at[s, :, :, z],
                            ref.at[:, j, :, pl.ds(at, width)],
                            sem.at[len(copies)],
                        )
                    )

    @pl.when(lax.axis_index("grp") == 0)
    def _():
        run_copies(copies)


A = VISCOSITY * TIME_STEP
H = 0.5 * TIME_STEP
B = 1.0 - 6.0 * A
BLOCK = 512


def combine(scale, cs, xp, xn, zp, zn, yp, yn):
    a, h, b = A * scale, H * scale, B * scale
    cu, cw, cv = h * cs[0], h * cs[1], h * cs[2]
    out = []
    for i in range(3):
        total = xn[i] * (a - cu) + xp[i] * (a + cu)
        total = total + (zn[i] * (a - cw) + zp[i] * (a + cw))
        total = total + (yn[i] * (a - cv) + yp[i] * (a + cv))
        out.append(total + b * cs[i])
    return out


def spanwise(load, at, width, span):
    centre = load(at, width)
    wide = jnp.concatenate(
        [load((at - LANES) % span, LANES), centre, load((at + width) % span, LANES)], axis=1
    )
    total = width + 2 * LANES
    before = pltpu.roll(wide, 1, 1)[:, LANES : LANES + width]
    after = pltpu.roll(wide, total - 1, 1)[:, LANES : LANES + width]
    return centre, before, after


def main_block(scale, field, x, zb, za, zrow, at, width, span):
    top = lax.broadcasted_iota(jnp.int32, (SUB, width), 0)
    cs, xp, xn, zp, zn, yp, yn = [], [], [], [], [], [], []
    for c in range(3):
        centre, before, after = spanwise(
            lambda l, w, c=c: field[c, x, :, pl.ds(l, w)], at, width, span
        )
        cs.append(centre)
        yp.append(before)
        yn.append(after)
        xp.append(field[c, x - 1, :, pl.ds(at, width)])
        xn.append(field[c, x + 1, :, pl.ds(at, width)])
        low = jnp.broadcast_to(zb[c, pl.ds(zrow, 1), pl.ds(at, width)], (SUB, width))
        high = jnp.broadcast_to(za[c, pl.ds(zrow, 1), pl.ds(at, width)], (SUB, width))
        zp.append(jnp.where(top == 0, low, pltpu.roll(centre, 1, 0)))
        zn.append(jnp.where(top == SUB - 1, high, pltpu.roll(centre, SUB - 1, 0)))
    return combine(scale, cs, xp, xn, zp, zn, yp, yn)


def edge_rows(near, before, after, out, keep, begin, groups, span):
    def block(i, _):
        at = pl.multiple_of(i * BLOCK, BLOCK)
        left = pl.multiple_of(lax.rem(at + span - LANES, span), LANES)
        right = pl.multiple_of(lax.rem(at + BLOCK, span), LANES)
        for g in range(begin, groups):
            cs, xp, xn, zp, zn, yp, yn = [], [], [], [], [], [], []
            for c in range(3):
                r = SUB * (g + 1)
                centre = near[c, r : r + SUB, pl.ds(at, BLOCK)]
                wide = jnp.concatenate(
                    [
                        near[c, r : r + SUB, pl.ds(left, LANES)],
                        centre,
                        near[c, r : r + SUB, pl.ds(right, LANES)],
                    ],
                    axis=1,
                )
                total = BLOCK + 2 * LANES
                cs.append(centre)
                yp.append(pltpu.roll(wide, 1, 1)[:, LANES : LANES + BLOCK])
                yn.append(pltpu.roll(wide, total - 1, 1)[:, LANES : LANES + BLOCK])
                xp.append(near[c, r - 1 : r - 1 + SUB, pl.ds(at, BLOCK)])
                xn.append(near[c, r + 1 : r + 1 + SUB, pl.ds(at, BLOCK)])
                zp.append(before[c, SUB * g : SUB * (g + 1), pl.ds(at, BLOCK)])
                zn.append(after[c, SUB * g : SUB * (g + 1), pl.ds(at, BLOCK)])
            new = combine(1.0, cs, xp, xn, zp, zn, yp, yn)
            for c in range(3):
                out[c, SUB * (g + 1) : SUB * (g + 2), pl.ds(at, BLOCK)] = jnp.where(
                    keep, new[c], 0.0
                )
        return 0

    lax.fori_loop(0, span // BLOCK, block, 0)


def section_plane(x, start, sect, nb, na, span, keep=None):
    for at in range(0, span, BLOCK):
        new = main_block(1.0, start, x + 2, nb, na, SUB + x, at, BLOCK, span)
        for c in range(3):
            value = new[c] if keep is None else jnp.where(keep, new[c], 0.0)
            sect[c, x + 1, :, at : at + BLOCK] = value


def second_plane(x, start, sect, eb, ea, out, span):
    for at in range(0, span, BLOCK):
        new = main_block(0.5, sect, x + 1, eb, ea, SUB + x, at, BLOCK, span)
        for c in range(3):
            out[c, x, :, at : at + BLOCK] = new[c] + 0.5 * start[c, x + 2, :, at : at + BLOCK]


def rows_scratch(cells, span):
    shift = [
        pltpu.VMEM((3, cells + 2 * SUB, span), F32),
        pltpu.VMEM((3, cells + 2 * SUB, span), F32),
    ]
    side = [pltpu.VMEM((3, cells, span), F32)] * 4
    return shift + side + shift


def run_copies(copies):
    for copy in copies:
        copy.start()
    for copy in copies:
        copy.wait()


def roles(rows, ranks):
    r, g = lax.axis_index("grp"), lax.axis_index("gx")
    return g > 0, g < ranks - 1, r > 0, r < rows - 1, r == 0


def row_pieces(faces, first, nb, na, b2, b0, a0, a2):
    count = faces[0].shape[2]
    return [
        (faces[i].at[:, j], ref.at[:, pl.ds(at + first, count)])
        for i, j, ref, at in ((2, 1, nb, SUB), (3, 0, na, SUB), (2, 0, b2, 0), (3, 1, a2, 0),
                              (0, 0, b0, 0), (1, 1, a0, 0))
    ]


def own_kernel(rows, ranks, vel, *refs):
    (near, far, up_corners, dn_corners, dn_all, up_all, b_all, a_all, dn_hi, up_hi, b_hi, a_hi,
     out_hbm, start, sect, out, nb, na, b2, b0, a0, a2, eb, ea, corner, sem, out_sem) = refs
    cells = vel.shape[1]
    low = cells - dn_hi.shape[2]
    span = vel.shape[3]
    has_before, has_after, has_left, has_right, is_first = roles(rows, ranks)
    first = jnp.where(is_first, low + 2, 0)
    always = [
        (vel.at[:, pl.ds(low, cells - low)], start.at[:, pl.ds(2 + low, cells - low)]),
        (up_corners, corner.at[0]),
        (dn_corners, corner.at[1]),
    ]
    always = [pltpu.make_async_copy(p, q, sem.at[i]) for i, (p, q) in enumerate(always)]
    for copy in always:
        copy.start()

    def rest(pieces):
        run_copies(
            [
                pltpu.make_async_copy(p, q, sem.at[len(always) + i])
                for i, (p, q) in enumerate(pieces)
            ]
        )

    for condition, left, right in sides(near, far):

        @pl.when(condition)
        def _(left=left, right=right):
            rest(
                [(left, start.at[:, pl.ds(0, 2)]), (right, start.at[:, pl.ds(cells + 2, 2)])]
            )

    @pl.when(is_first)
    def _():
        rest(row_pieces((dn_hi, up_hi, b_hi, a_hi), low, nb, na, b2, b0, a0, a2))

    @pl.when(jnp.logical_not(is_first))
    def _():
        pieces = row_pieces((dn_all, up_all, b_all, a_all), 0, nb, na, b2, b0, a0, a2)
        rest(pieces + [(vel.at[:, pl.ds(0, low)], start.at[:, pl.ds(2, low)])])

    for copy in always:
        copy.wait()

    @pl.when(jnp.logical_not(has_right))
    def _():
        for c in range(3):
            start[c, cells + 2] = jnp.zeros((SUB, span), F32)
            for i in range(2):
                corner[i, c, 1:2, :] = jnp.zeros((1, span), F32)

    for c in range(3):
        nb[c, SUB - 1 : SUB, :] = corner[0, c, 0:1, :]
        nb[c, SUB + cells : SUB + cells + 1, :] = corner[0, c, 1:2, :]
        na[c, SUB - 1 : SUB, :] = corner[1, c, 0:1, :]
        na[c, SUB + cells : SUB + cells + 1, :] = corner[1, c, 1:2, :]
    groups = cells // SUB

    @pl.when(jnp.logical_not(is_first))
    def _():
        edge_rows(nb, b2, b0, eb, has_before, 0, low // SUB, span)
        edge_rows(na, a0, a2, ea, has_after, 0, low // SUB, span)

    edge_rows(nb, b2, b0, eb, has_before, low // SUB, groups, span)
    edge_rows(na, a0, a2, ea, has_after, low // SUB, groups, span)

    def make(x, keep=None):
        section_plane(x, start, sect, nb, na, span, keep)

    def body(x, _):
        keep = jnp.logical_or(
            jnp.logical_and(x >= 0, x < cells),
            jnp.logical_or(jnp.logical_and(x < 0, has_left), jnp.logical_and(x >= cells, has_right)),
        )
        make(x, keep)

        @pl.when(x >= first + 1)
        def _():
            second_plane(x - 1, start, sect, eb, ea, out, span)
            pltpu.make_async_copy(out.at[:, x - 1], out_hbm.at[:, x - 1], out_sem.at[x - 1]).start()

        return 0

    lax.fori_loop(first - 1, cells + 1, body, 0)

    def drain(x, _):
        pltpu.make_async_copy(out.at[:, x], out_hbm.at[:, x], out_sem.at[x]).wait()
        return 0

    lax.fori_loop(first, cells, drain, 0)


def inflow_kernel(rows, ranks, places, vel, *refs):
    parts, refs = refs[:-23], refs[-23:]
    dn_in, up_in, b_in, a_in, dn_hi, up_hi, b_hi, a_hi, _, out_hbm = refs[:10]
    start, sect, out, nb, na, b2, b0, a0, a2, eb, ea, sem, out_sem = refs[10:]
    low = dn_in.shape[2]
    span = vel.shape[3]
    reach = out.shape[1]
    cells = b2.shape[1]
    has_before, has_after, _, _, is_first = roles(rows, ranks)

    @pl.when(is_first)
    def _():
        pieces = [(vel.at[:, pl.ds(low, 4)], start.at[:, pl.ds(low + 2, 4)])]
        for piece, (source, part, many) in zip(parts, places):
            width = piece.shape[4]
            for s in range(piece.shape[0]):
                at = ((source + s) * many + part) * width
                pieces.append((piece.at[s], start.at[:, pl.ds(2, low), :, pl.ds(at, width)]))
        for lo, hi, j, ref, first in (
            (b_in, b_hi, 1, nb, SUB),
            (a_in, a_hi, 0, na, SUB),
            (b_in, b_hi, 0, b2, 0),
            (a_in, a_hi, 1, a2, 0),
            (dn_in, dn_hi, 0, b0, 0),
            (up_in, up_hi, 1, a0, 0),
        ):
            pieces.append((lo.at[:, j], ref.at[:, pl.ds(first, low)]))
            pieces.append((hi.at[:, j], ref.at[:, pl.ds(first + low, cells - low)]))
        copies = [
            pltpu.make_async_copy(src, dst, sem.at[i]) for i, (src, dst) in enumerate(pieces)
        ]
        for copy in copies:
            copy.start()
        zero = jnp.zeros((SUB, span), F32)
        for c in range(3):
            start[c, 1] = zero
            sect[c, 0] = zero
            for ref in (nb, na):
                ref[c, 0:SUB, :] = zero
                ref[c, SUB + cells :, :] = zero
        for copy in copies:
            copy.wait()
        groups = cells // SUB
        edge_rows(nb, b2, b0, eb, has_before, 0, groups, span)
        edge_rows(na, a0, a2, ea, has_after, 0, groups, span)
        section_plane(0, start, sect, nb, na, span)

        def body(x, _):
            section_plane(x + 1, start, sect, nb, na, span)
            second_plane(x, start, sect, eb, ea, out, span)
            pltpu.make_async_copy(out.at[:, x], out_hbm.at[:, x], out_sem.at[x]).start()
            return 0

        lax.fori_loop(0, reach, body, 0)

        def drain(x, _):
            pltpu.make_async_copy(out.at[:, x], out_hbm.at[:, x], out_sem.at[x]).wait()
            return 0

        lax.fori_loop(0, reach, drain, 0)


def call(kernel, out_shape, out_specs, in_specs, scratch, estimate, alias=None):
    def run(*args):
        return pl.pallas_call(
            kernel,
            out_shape=out_shape,
            in_specs=in_specs,
            out_specs=out_specs,
            scratch_shapes=scratch,
            input_output_aliases=alias or {},
            compiler_params=params(),
            cost_estimate=estimate,
        )(*args)

    return run


def local(velocity, noise, previous, decay, stress_factor, mean_profile):
    rows = lax.axis_size("grp")
    ranks = lax.axis_size("gx")
    comps, count, depth, span_local = noise.shape
    cells, slab, span = velocity.shape[1:]
    width = span_local // PARTS
    low = count
    high = cells - low
    dma = pltpu.SemaphoreType.DMA

    def along_gx(array, step, lines, idlers=()):
        pairs = idle(idlers) + [
            (r * ranks + i, r * ranks + i + step)
            for r in lines
            for i in range(ranks)
            if 0 <= i + step < ranks
        ]
        return lax.ppermute(array, ("grp", "gx"), pairs)

    packed = jax.ShapeDtypeStruct((comps, count, depth * HALF // LANES, LANES), F32)
    face = jax.ShapeDtypeStruct((3, 2, low, span), F32)
    face_hi = jax.ShapeDtypeStruct((3, 2, high, span), F32)
    xface = jax.ShapeDtypeStruct((3, 2, slab, span), F32)
    full = jax.ShapeDtypeStruct(velocity.shape, F32)
    rim_out = call(
        first_kernel,
        packed,
        VMEM,
        [ANY],
        [pltpu.VMEM((comps, count, depth, LANES), F32), dma((comps,))],
        cost(0, noise.size),
    )(noise)

    def idle(lines):
        return [(r * ranks + i, r * ranks + (i ^ 1)) for r in lines for i in range(ranks)]

    def across(array, moves, idlers):
        pairs = [(a * ranks + i, b * ranks + i) for a, b in moves for i in range(ranks)]
        return lax.ppermute(array, ("grp", "gx"), pairs + idle(idlers))

    pairs = idle([r for r in range(rows) if r not in (1, 2)])
    for line, step in ((1, 1), (2, -1)):
        pairs += [(line * ranks + i, line * ranks + (i + step) % ranks) for i in range(ranks)]
    rim = lax.ppermute(rim_out, ("grp", "gx"), pairs)
    everyone = range(rows)
    evens = range(0, rows - 1, 2)
    odds = range(1, rows - 1, 2)
    lone = [0] + ([rows - 1] if rows % 2 == 0 else [])

    window = min(span_local, LANES * (-(-(width + 2 * HALF) // LANES) + 1))
    made_shape = jax.ShapeDtypeStruct((ranks, comps, count, depth // ranks, width), F32)

    windowed = pltpu.VMEM((comps, count, depth, window), F32)

    def make(kernel, inputs, specs, scratch):
        prev = previous
        if width % LANES:
            at = part_of(lax.axis_index("grp")) * width
            prev = lax.dynamic_slice_in_dim(previous, at, width, 2)
        return call(
            kernel,
            made_shape,
            VMEM,
            specs + [ANY, VMEM, VMEM, VMEM],
            [
                pltpu.VMEM((comps, count, depth, width), F32),
                pltpu.VMEM((comps, depth, width), F32),
            ]
            + scratch,
            cost(6 * noise.size * width, 4 * noise.size),
        )(*inputs, prev, decay, stress_factor, mean_profile[None])

    near_out, far_out = call(
        xfaces_kernel, [xface, xface], [VMEM] * 2, [ANY] * 2, [dma((2,))], cost(0, velocity.size)
    )(velocity, rim_out)
    far = across(far_out, [p for i in odds for p in ((i, i + 1), (i + 1, i))], lone)
    along = call(
        along_kernel,
        jax.ShapeDtypeStruct((comps, count, depth, width), F32),
        VMEM,
        [ANY],
        [windowed, dma((comps,))],
        cost(6 * noise.size * width, 4 * noise.size),
    )(noise)
    kernel_a = functools.partial(filter_kernel, span_local)
    made_a = make(
        kernel_a, [along, rim, near_out], [ANY] * 3,
        [
            pltpu.VMEM((comps, count, depth, width), F32),
            pltpu.VMEM(packed.shape, F32),
            dma((comps + 2,)),
        ],
    )
    got_a = lax.all_to_all(made_a, "gx", 0, 0, tiled=True)

    near = across(near_out, [p for i in evens for p in ((i, i + 1), (i + 1, i))], [])
    face_all = jax.ShapeDtypeStruct((3, 2, cells, span), F32)
    dn_all, up_all, dn_hi, up_hi = call(
        zfaces_kernel, [face_all, face_all, face_hi, face_hi], [VMEM] * 4, [ANY] * 2,
        [dma((12,))], cost(0, velocity.size),
    )(velocity, made_a)
    others = range(1, rows)
    b_hi = along_gx(up_hi, 1, [0], others)
    a_hi = along_gx(dn_hi, -1, [0], others)

    half = ranks // 2
    side = lax.ppermute(got_a[half:], "grp", [(3, 1)])
    hop_1 = lax.ppermute(got_a, "grp", [(1, 0)])
    hop_2 = lax.ppermute(got_a, "grp", [(2, 0)])
    hop_3 = lax.ppermute(got_a[:half], "grp", [(3, 0)])

    b_all = along_gx(up_all, 1, others)
    a_all = along_gx(dn_all, -1, others)

    mark = call(
        mark_kernel, jax.ShapeDtypeStruct((SUB, LANES), F32), VMEM, [ANY], [], cost(0, 1024)
    )(made_a)
    pair = jax.ShapeDtypeStruct((3, 2, span), F32)
    up_corner, dn_corner = call(
        corners_kernel, [pair, pair], [VMEM] * 2, [ANY] * 3, [dma((12,))], cost(0, 24 * span)
    )(near, far, mark)
    up_corners = along_gx(up_corner, 1, everyone)
    dn_corners = along_gx(dn_corner, -1, everyone)

    def fields(planes):
        return [
            pltpu.VMEM((3, planes + 4, slab, span), F32),
            pltpu.VMEM((3, planes + 2, slab, span), F32),
            pltpu.VMEM((3, planes, slab, span), F32),
        ]

    hop_4 = lax.ppermute(side, "grp", [(1, 0)])
    own = call(
        functools.partial(own_kernel, rows, ranks),
        full,
        ANY,
        [ANY] * 13,
        fields(cells)
        + rows_scratch(cells, span)
        + [pltpu.VMEM((2, 3, 2, span), F32), dma((12,)), dma((cells,))],
        cost(50 * velocity.size, 8 * velocity.size),
    )(velocity, near, far, up_corners, dn_corners, dn_all, up_all, b_all, a_all, dn_hi, up_hi, b_hi,
      a_hi)

    parts = [hop_1, got_a, hop_3, hop_4, hop_2]
    places = [(0, 0, PARTS), (0, 1, PARTS), (0, 2, PARTS), (half, 2, PARTS), (0, 3, PARTS)]
    if width != LANES:
        joined = [hop_1, got_a, jnp.concatenate([hop_3, hop_4], axis=0), hop_2]
        joined = jnp.concatenate(joined, axis=4)
        parts = [joined[..., at : at + LANES] for at in range(0, span_local, LANES)]
        places = [(0, i, len(parts)) for i in range(len(parts))]
    many = len(parts)
    dn_in, up_in = call(
        functools.partial(inflow_faces_kernel, places),
        [face, face],
        [VMEM] * 2,
        [ANY] * many,
        [dma((4 * sum(p.shape[0] for p in parts),))],
        cost(0, 8 * noise.size),
    )(*parts)
    b_in = along_gx(up_in, 1, [0])
    a_in = along_gx(dn_in, -1, [0])

    reach = low + 2
    return call(
        functools.partial(inflow_kernel, rows, ranks, places),
        full,
        ANY,
        [ANY] * (many + 10),
        fields(reach)
        + rows_scratch(low + high, span)
        + [dma((sum(p.shape[0] for p in parts) + 13,)), dma((reach,))],
        cost(30 * velocity.size, 5 * velocity.size),
        {many + 9: 0},
    )(velocity, *parts, dn_in, up_in, b_in, a_in, dn_hi, up_hi, b_hi, a_hi, own)


def solution(mesh):
    placed = (
        P(None, "grp", "gx", None),
        P(None, None, None, "gx"),
        P(None, None, "gx"),
        P(),
        P(),
        P(),
    )

    return jax.shard_map(
        local, mesh=mesh, in_specs=placed, out_specs=P(None, "grp", "gx", None), check_vma=False
    )
```

time: 130 us -> 140 us (1.077)
  waiting for transfers between devices: 16.9 us -> 50.9 us
  local copies, waits for them, and re-layouts: 17.8 us -> 5.23 us
  Pallas kernels: 54.4 us -> 48.4 us
  starting transfers between devices: 38.2 us -> 34.1 us
  other arithmetic: 2.11 us -> 0 us
    ppermute x10 -> x13, waiting for transfers between devices: 0.03 us -> 19.7 us  [the longest x1 17.4 us: local(): hop_4 = lax.ppermute(side, 'grp', [(1, 0)])]
    all_to_all x1, waiting for transfers between devices: 3.62 us -> 18.2 us  [local(): got_a = lax.all_to_all(made_a, 'gx', 0, 0, tiled=True)]
    ppermute x1, waiting for transfers between devices: 13.2 us -> 0.01 us  [local(): hop_2 = lax.ppermute(got_a, 'grp', [(2, 0)])]
    ppermute x1, waiting for transfers between devices: 0.01 us -> 13 us  [local(): hop_1 = lax.ppermute(got_a, 'grp', [(1, 0)])]
    pallas_call x7 -> x10, Pallas kernels: 54.4 us -> 48.4 us  [run(): pl.pallas_call(kernel, out_shape=out_shape, in_specs=in_specs, out_specs=...]
    ppermute x2 -> x0, local copies, waits for them, and re-layouts: 4.99 us -> none  [shift(): return lax.ppermute(array, axis, pairs)]
    all_to_all x1 -> x0, starting transfers between devices: 4.42 us -> none  [local(): got_b = lax.all_to_all(made_b, 'gx', 0, 0, tiled=True)]
    ppermute x1, starting transfers between devices: 2.67 us -> 0.07 us  [local(): rim = lax.ppermute(rim_out, ('grp', 'gx'), pairs)]
  transfers between devices with their start and end apart: 15 -> 17, of which waited for: 2 -> 4; matrix products, arithmetic and copies ran while one was open for 13% -> 0% of each run, Pallas kernels for 26% -> 20%
where the time goes in v2:
time: 140 us; the launch traced here: 139 us
  waiting for transfers between devices  50.9 us (36%)
  Pallas kernels  48.4 us (35%)
  starting transfers between devices  34.1 us (24%)
  local copies, waits for them, and re-layouts  5.23 us (4%)
    pallas_call x10, Pallas kernels, run(): pl.pallas_call(kernel, out_shape=out_shape, in_specs=in_specs, out_specs=...  48.4 us
    ppermute x8, starting transfers between devices, along_gx(): return lax.ppermute(array, ('grp', 'gx'), pairs)  19.2 us
    all_to_all x1, waiting for transfers between devices, local(): got_a = lax.all_to_all(made_a, 'gx', 0, 0, tiled=True)  18.2 us
    ppermute x1, waiting for transfers between devices, local(): hop_4 = lax.ppermute(side, 'grp', [(1, 0)])  17.4 us
    ppermute x1, waiting for transfers between devices, local(): hop_1 = lax.ppermute(got_a, 'grp', [(1, 0)])  13 us
    all_to_all x1, starting transfers between devices, local(): got_a = lax.all_to_all(made_a, 'gx', 0, 0, tiled=True)  6.47 us
    unnamed x28, local copies, waits for them, and re-layouts  5.18 us
  transfers between devices with their start and end apart: 17, of which 4 were waited for; matrix products, arithmetic and copies ran while one was open for 0% of the time, Pallas kernels for 20%

profile of v2, /device:TPU:1, one launch (start us, length us, event | category | flops | bytes accessed | tf_op | source)
XLA Modules:
  0.0 139.0 jit_solution(3161463278974999608)
XLA Ops:
  0.0 2.2 %shard_map.65.after = f32[3,8,16,128]{3,2,1,0:T(8,128)} custom-call(f32[3,8,64,512]{3,2,1,0:T(8,128)} %noise.3), custom_call_target="tpu_custom_call" | custom-call | bytes 786432 | tf_op jit(solution)/shard_map/pallas_call | solution.py:595
  2.2 0.1 collective-permute-start
  2.3 2.6 %shard_map.66 = (f32[3,2,8,4096]{3,2,1,0:T(8,128)}, f32[3,2,8,4096]{3,2,1,0:T(8,128)}) custom-call(f32[3,16,8,4096]{3,2,1,0:T(8,128)} %vel.7, f32[3,8,16,128]{3,2,1,0:T(8,128)} %shard_map.65.after), custom_call_target="tpu_custom_call" | custom-call | bytes 1572864 | tf_op jit(solution)/shard_map/pallas_call | solution.py:595
  4.8 3.9 %shard_map.64.along_hbm = f32[3,8,64,128]{3,2,1,0:T(8,128)} custom-call(f32[3,8,64,512]{3,2,1,0:T(8,128)} %noise.3), custom_call_target="tpu_custom_call" | custom-call | flops 603979776 | bytes 3145728 | tf_op jit(solution)/shard_map/pallas_call | solution.py:595
  8.8 0.0 copy-start.10
  8.8 0.0 collective-permute-done.rim
  8.8 0.0 copy-start.11
  8.8 0.7 copy-done.11
  9.5 4.1 %shard_map.67.after = f32[8,3,8,8,128]{4,3,2,1,0:T(8,128)} custom-call(f32[3,8,64,128]{3,2,1,0:T(8,128)} %shard_map.64.along_hbm, f32[3,8,16,128]{3,2,1,0:T(8,128)} %copy-done.11, f32[3,2,8,4096]{3,2,1,0:T(8,128)} %get-tuple-element.15.after, f32[3,64,512]{2,1,0:T(8,128)} %previous.1, f32[3,64]{1,0:T(4,128)} %decay_ref.1, f32[6,64]{1,0:T(8,128)} %factor_ref.1, ...), custom_call_target="tpu_custom_call" | custom-call | flops 603979776 | bytes 3145728 | tf_op jit(solution)/shard_map/pallas_call | solution.py:595
  13.6 6.5 %all-to-all-start = ((f32[8,3,8,8,128]{4,3,2,1,0:T(8,128)}), f32[8,3,8,8,128]{4,3,2,1,0:T(8,128)S(1)}, u32[]{:S(2)}, u32[]{:S(2)}) async-start(f32[8,3,8,8,128]{4,3,2,1,0:T(8,128)} %shard_map.67.after), calls=%async_computation | async-start | bytes 1572864 | tf_op jit(solution)/shard_map/all_to_all | solution.py:702
  20.1 0.0 copy-done.10
  20.1 1.4 collective-permute-start.10
  21.5 0.4 collective-permute-start.11
  21.8 18.2 %all-to-all-done.refs_1_ = f32[8,3,8,8,128]{4,3,2,1,0:T(8,128)S(1)} async-done(((f32[8,3,8,8,128]{4,3,2,1,0:T(8,128)}), f32[8,3,8,8,128]{4,3,2,1,0:T(8,128)S(1)}, u32[]{:S(2)}, u32[]{:S(2)}) %all-to-all-start) | async-done | bytes 786464 | tf_op jit(solution)/shard_map/all_to_all | solution.py:702
  40.1 0.1 fusion
  40.1 1.4 %collective-permute-start.3 = (f32[4,3,8,8,128]{4,3,2,1,0:T(8,128)S(1)}, f32[4,3,8,8,128]{4,3,2,1,0:T(8,128)}, u32[]{:S(2)}, u32[]{:S(2)}) collective-permute-start(f32[4,3,8,8,128]{4,3,2,1,0:T(8,128)S(1)} %get-tuple-element.25), channel_id=1, source_target_pairs={{24,8},{25,9},{26,10},{27,11},{28,12},{29,13},{30,14},{31,15}} | collective-permute-start | bytes 1179656 | tf_op jit(solution)/shard_map/ppermute | solution.py:715
  41.5 1.3 collective-permute-start.2
  42.8 0.0 collective-permute-done.3
  42.8 1.3 collective-permute-start.4
  44.1 0.6 shard_map.70.after
  44.7 0.0 collective-permute-done.10.near.refs_0_
  44.7 0.0 collective-permute-done.11.far.refs_1_
  44.7 0.9 copy-done.5
  45.6 0.9 copy-done.6
  46.5 1.7 %shard_map.71 = (f32[3,2,4096]{2,1,0:T(2,128)}, f32[3,2,4096]{2,1,0:T(2,128)}) custom-call(f32[3,2,8,4096]{3,2,1,0:T(8,128)} %copy-done.5, f32[3,2,8,4096]{3,2,1,0:T(8,128)} %copy-done.6, f32[8,128]{1,0:T(8,128)} %shard_map.70.after), custom_call_target="tpu_custom_call" | custom-call | bytes 98304 | tf_op jit(solution)/shard_map/pallas_call | solution.py:595
  48.2 1.9 %collective-permute-start.12 = (f32[3,2,4096]{2,1,0:T(2,128)}, f32[3,2,4096]{2,1,0:T(2,128)S(1)}, u32[]{:S(2)}, u32[]{:S(2)}) collective-permute-start(f32[3,2,4096]{2,1,0:T(2,128)} %get-tuple-element.21), channel_id=1, source_target_pairs={{0,1},{1,2},{2,3},{3,4},{4,5},{5,6},{6,7},{8,9},{9,10},{10,11},{11... | collective-permute-start | bytes 294920 | tf_op jit(solution)/shard_map/ppermute | solution.py:626
  50.1 1.3 collective-permute-start.1
  51.4 4.0 %shard_map.69 = (f32[3,2,16,4096]{3,2,1,0:T(8,128)}, f32[3,2,16,4096]{3,2,1,0:T(8,128)}, f32[3,2,8,4096]{3,2,1,0:T(8,128)}, f32[3,2,8,4096]{3,2,1,0:T(8,128)}) custom-call(f32[3,16,8,4096]{3,2,1,0:T(8,128)} %vel.7, f32[8,3,8,8,128]{4,3,2,1,0:T(8,128)} %shard_map.67.after), custom_call_target="tpu_custom_call" | custom-call | bytes 1572864 | tf_op jit(solution)/shard_map/pallas_call | solution.py:595
  55.5 0.0 copy-done
  55.5 1.3 collective-permute-start.5
  56.8 0.0 collective-permute-done.12.refs_2_
  56.8 0.0 copy-start.12
  56.8 1.8 %collective-permute-start.14 = (f32[3,2,16,4096]{3,2,1,0:T(8,128)}, f32[3,2,16,4096]{3,2,1,0:T(8,128)}, u32[]{:S(2)}, u32[]{:S(2)}) collective-permute-start(f32[3,2,16,4096]{3,2,1,0:T(8,128)} %get-tuple-element.24.refs_5_), channel_id=1, source_target_pairs={{8,9},{9,10},{10,11},{11,12},{12,13},{13,14},{14,15},{16,17},{17,1... | collective-permute-start | bytes 4718600 | tf_op jit(solution)/shard_map/ppermute | solution.py:626
  58.6 0.0 collective-permute-done.2.refs_2_
  58.6 1.9 %collective-permute-start.15 = (f32[3,2,16,4096]{3,2,1,0:T(8,128)}, f32[3,2,16,4096]{3,2,1,0:T(8,128)}, u32[]{:S(2)}, u32[]{:S(2)}) collective-permute-start(f32[3,2,16,4096]{3,2,1,0:T(8,128)} %get-tuple-element.23.refs_4_), channel_id=1, source_target_pairs={{9,8},{10,9},{11,10},{12,11},{13,12},{14,13},{15,14},{17,16},{18,1... | collective-permute-start | bytes 4718600 | tf_op jit(solution)/shard_map/ppermute | solution.py:626
  60.5 17.4 %collective-permute-done.4.refs_3_ = f32[4,3,8,8,128]{4,3,2,1,0:T(8,128)} collective-permute-done((f32[4,3,8,8,128]{4,3,2,1,0:T(8,128)}, f32[4,3,8,8,128]{4,3,2,1,0:T(8,128)}, u32[]{:S(2)}, u32[]{:S(2)}) %collective-permute-start.4) | collective-permute-done | bytes 393248 | tf_op jit(solution)/shard_map/ppermute | solution.py:740
  78.0 0.0 copy-done.7
  78.0 4.2 %collective-permute-start.8 = (f32[3,2,8,4096]{3,2,1,0:T(8,128)}, f32[3,2,8,4096]{3,2,1,0:T(8,128)S(1)}, u32[]{:S(2)}, u32[]{:S(2)}) collective-permute-start(f32[3,2,8,4096]{3,2,1,0:T(8,128)} %get-tuple-element.19.refs_9_.refs_10_), channel_id=1, source_target_pairs={{8,9},{9,8},{10,11},{11,10},{12,13},{13,12},{14,15},{15,14},{16,17... | collective-permute-start | bytes 2359304 | tf_op jit(solution)/shard_map/ppermute | solution.py:626
  82.2 13.0 %collective-permute-done.1.refs_0_ = f32[8,3,8,8,128]{4,3,2,1,0:T(8,128)S(1)} collective-permute-done((f32[8,3,8,8,128]{4,3,2,1,0:T(8,128)S(1)}, f32[8,3,8,8,128]{4,3,2,1,0:T(8,128)S(1)}, u32[]{:S(2)}, u32[]{:S(2)}) %collective-permute-start.1) | collective-permute-done | bytes 786464 | tf_op jit(solution)/shard_map/ppermute | solution.py:716
  95.2 1.9 %collective-permute-start.13 = (f32[3,2,4096]{2,1,0:T(2,128)}, f32[3,2,4096]{2,1,0:T(2,128)S(1)}, u32[]{:S(2)}, u32[]{:S(2)}) collective-permute-start(f32[3,2,4096]{2,1,0:T(2,128)} %get-tuple-element.22), channel_id=1, source_target_pairs={{1,0},{2,1},{3,2},{4,3},{5,4},{6,5},{7,6},{9,8},{10,9},{11,10},{12... | collective-permute-start | bytes 294920 | tf_op jit(solution)/shard_map/ppermute | solution.py:626
  97.1 0.0 collective-permute-done.5.refs_4_
  97.1 0.0 copy-start.4
  97.1 1.9 %collective-permute-start.9 = (f32[3,2,8,4096]{3,2,1,0:T(8,128)}, f32[3,2,8,4096]{3,2,1,0:T(8,128)S(1)}, u32[]{:S(2)}, u32[]{:S(2)}) collective-permute-start(f32[3,2,8,4096]{3,2,1,0:T(8,128)} %get-tuple-element.18.refs_8_.refs_9_), channel_id=1, source_target_pairs={{8,9},{9,8},{10,11},{11,10},{12,13},{13,12},{14,15},{15,14},{16,17... | collective-permute-start | bytes 2359304 | tf_op jit(solution)/shard_map/ppermute | solution.py:626
  99.1 0.0 copy-done.3
  99.1 0.0 copy-done.4
  99.1 3.7 %shard_map.68 = (f32[3,2,8,4096]{3,2,1,0:T(8,128)}, f32[3,2,8,4096]{3,2,1,0:T(8,128)}) custom-call(f32[8,3,8,8,128]{4,3,2,1,0:T(8,128)} %copy-done.3, f32[8,3,8,8,128]{4,3,2,1,0:T(8,128)} %copy-done, f32[4,3,8,8,128]{4,3,2,1,0:T(8,128)} %copy-done.7, f32[4,3,8,8,128]{4,3,2,1,0:T(8,128)} %collective-permute-done.4.refs_3_, f32[8,3,8,8,128]{4,3,2,1,0:T(8,128)} %copy-done.4), custom_call_target="tpu_custom_call" | custom-call | bytes 6291456 | tf_op jit(solution)/shard_map/pallas_call | solution.py:595
  102.8 0.0 collective-permute-done.13.refs_3_
  102.8 0.0 copy-start.13
  102.8 3.6 %collective-permute-start.6 = (f32[3,2,8,4096]{3,2,1,0:T(8,128)}, f32[3,2,8,4096]{3,2,1,0:T(8,128)S(1)}, u32[]{:S(2)}, u32[]{:S(2)}) collective-permute-start(f32[3,2,8,4096]{3,2,1,0:T(8,128)} %get-tuple-element.17.refs_6_), channel_id=1, source_target_pairs={{0,1},{1,2},{2,3},{3,4},{4,5},{5,6},{6,7}} | collective-permute-start | bytes 2359304 | tf_op jit(solution)/shard_map/ppermute | solution.py:626
  106.5 0.0 collective-permute-done.8.refs_10_.refs_11_
  106.5 0.0 copy-start.1
  106.5 1.9 %collective-permute-start.7 = (f32[3,2,8,4096]{3,2,1,0:T(8,128)}, f32[3,2,8,4096]{3,2,1,0:T(8,128)S(1)}, u32[]{:S(2)}, u32[]{:S(2)}) collective-permute-start(f32[3,2,8,4096]{3,2,1,0:T(8,128)} %get-tuple-element.16.refs_5_), channel_id=1, source_target_pairs={{1,0},{2,1},{3,2},{4,3},{5,4},{6,5},{7,6}} | collective-permute-start | bytes 2359304 | tf_op jit(solution)/shard_map/ppermute | solution.py:626
  108.4 2.2 %collective-permute-done.9.refs_11_.refs_12_ = f32[3,2,8,4096]{3,2,1,0:T(8,128)S(1)} collective-permute-done((f32[3,2,8,4096]{3,2,1,0:T(8,128)}, f32[3,2,8,4096]{3,2,1,0:T(8,128)S(1)}, u32[]{:S(2)}, u32[]{:S(2)}) %collective-permute-start.9) | collective-permute-done | bytes 786464 | tf_op jit(solution)/shard_map/ppermute | solution.py:626
  110.7 0.0 collective-permute-done.14.refs_6_
  110.7 0.0 collective-permute-done.15.refs_7_
  110.7 0.0 copy-done.12
  110.7 0.0 copy-done.13
  110.7 0.9 copy-done.2
  111.6 11.7 %shard_map.72.refs_13_ = f32[3,16,8,4096]{3,2,1,0:T(8,128)} custom-call(f32[3,16,8,4096]{3,2,1,0:T(8,128)} %vel.7, f32[3,2,8,4096]{3,2,1,0:T(8,128)} %copy-done.5, f32[3,2,8,4096]{3,2,1,0:T(8,128)} %copy-done.6, f32[3,2,4096]{2,1,0:T(2,128)} %copy-done.12, f32[3,2,4096]{2,1,0:T(2,128)} %copy-done.13, f32[3,2,16,4096]{3,2,1,0:T(8,128)} %get-tuple-element.23.refs_4_, ...), custom_call_target="tpu_custom_call" | custom-call | flops 78643200 | bytes 12582912 | tf_op jit(solution)/shard_map/pallas_call | solution.py:595
  123.2 0.0 collective-permute-done.6.refs_7_
  123.3 0.0 collective-permute-done.7.refs_8_
  123.3 0.9 copy-done.8
  124.1 0.9 copy-done.9
  125.1 14.0 %shard_map.73 = f32[3,16,8,4096]{3,2,1,0:T(8,128)} custom-call(f32[3,16,8,4096]{3,2,1,0:T(8,128)} %vel.7, f32[8,3,8,8,128]{4,3,2,1,0:T(8,128)} %copy-done.3, f32[8,3,8,8,128]{4,3,2,1,0:T(8,128)} %copy-done, f32[4,3,8,8,128]{4,3,2,1,0:T(8,128)} %copy-done.7, f32[4,3,8,8,128]{4,3,2,1,0:T(8,128)} %collective-permute-done.4.refs_3_, ...), custom_call_target="tpu_custom_call", output_to_operand_aliasing={{}: (14, {})} | custom-call | flops 47185920 | bytes 7864320 | tf_op jit(solution)/shard_map/pallas_call | solution.py:595
  (9 shorter events, 0.0 us)
Async XLA Ops:
  2.2 6.6 %collective-permute-start = (f32[3,8,16,128]{3,2,1,0:T(8,128)}, f32[3,8,16,128]{3,2,1,0:T(8,128)S(1)}, u32[]{:S(2)}, u32[]{:S(2)}) collective-permute-start(f32[3,8,16,128]{3,2,1,0:T(8,128)} %shard_map.65.after), channel_id=1, source_target_pairs={{0,1},{1,0},{2,3},{3,2},{4,5},{5,4},{6,7},{7,6},{24,25},{25,24},{2... | collective-permute-start | bytes 589832 | tf_op jit(solution)/shard_map/ppermute | solution.py:652
  8.8 11.3 %copy-start.10 = (f32[3,2,8,4096]{3,2,1,0:T(8,128)S(1)}, f32[3,2,8,4096]{3,2,1,0:T(8,128)}, u32[]{:S(2)}) copy-start(f32[3,2,8,4096]{3,2,1,0:T(8,128)} %get-tuple-element.15.after) | copy-start | bytes 2359300
  8.8 0.7 copy-start.11
  13.6 26.4 %all-to-all-start = ((f32[8,3,8,8,128]{4,3,2,1,0:T(8,128)}), f32[8,3,8,8,128]{4,3,2,1,0:T(8,128)S(1)}, u32[]{:S(2)}, u32[]{:S(2)}) async-start(f32[8,3,8,8,128]{4,3,2,1,0:T(8,128)} %shard_map.67.after), calls=%async_computation | async-start | bytes 1572864 | tf_op jit(solution)/shard_map/all_to_all | solution.py:702
  20.1 24.7 %collective-permute-start.10 = (f32[3,2,8,4096]{3,2,1,0:T(8,128)S(1)}, f32[3,2,8,4096]{3,2,1,0:T(8,128)S(1)}, u32[]{:S(2)}, u32[]{:S(2)}) collective-permute-start(f32[3,2,8,4096]{3,2,1,0:T(8,128)S(1)} %copy-done.10), channel_id=1, source_target_pairs={{0,8},{1,9},{2,10},{3,11},{4,12},{5,13},{6,14},{7,15},{8,0},{9,1},... | collective-permute-start | bytes 2359304 | tf_op jit(solution)/shard_map/ppermute | solution.py:647
  21.5 23.3 %collective-permute-start.11 = (f32[3,2,8,4096]{3,2,1,0:T(8,128)}, f32[3,2,8,4096]{3,2,1,0:T(8,128)S(1)}, u32[]{:S(2)}, u32[]{:S(2)}) collective-permute-start(f32[3,2,8,4096]{3,2,1,0:T(8,128)} %get-tuple-element.20), channel_id=1, source_target_pairs={{8,16},{9,17},{10,18},{11,19},{12,20},{13,21},{14,22},{15,23},{16,... | collective-permute-start | bytes 2359304 | tf_op jit(solution)/shard_map/ppermute | solution.py:647
  40.0 15.4 %copy-start = (f32[8,3,8,8,128]{4,3,2,1,0:T(8,128)}, f32[8,3,8,8,128]{4,3,2,1,0:T(8,128)S(1)}, u32[]{:S(2)}) copy-start(f32[8,3,8,8,128]{4,3,2,1,0:T(8,128)S(1)} %all-to-all-done.refs_1_) | copy-start | bytes 2359300
  40.1 2.7 %collective-permute-start.3 = (f32[4,3,8,8,128]{4,3,2,1,0:T(8,128)S(1)}, f32[4,3,8,8,128]{4,3,2,1,0:T(8,128)}, u32[]{:S(2)}, u32[]{:S(2)}) collective-permute-start(f32[4,3,8,8,128]{4,3,2,1,0:T(8,128)S(1)} %get-tuple-element.25), channel_id=1, source_target_pairs={{24,8},{25,9},{26,10},{27,11},{28,12},{29,13},{30,14},{31,15}} | collective-permute-start | bytes 1179656 | tf_op jit(solution)/shard_map/ppermute | solution.py:715
  41.5 17.1 %collective-permute-start.2 = (f32[4,3,8,8,128]{4,3,2,1,0:T(8,128)S(1)}, f32[4,3,8,8,128]{4,3,2,1,0:T(8,128)S(1)}, u32[]{:S(2)}, u32[]{:S(2)}) collective-permute-start(f32[4,3,8,8,128]{4,3,2,1,0:T(8,128)S(1)} %get-tuple-element.26), channel_id=1, source_target_pairs={{24,0},{25,1},{26,2},{27,3},{28,4},{29,5},{30,6},{31,7}} | collective-permute-start | bytes 1179656 | tf_op jit(solution)/shard_map/ppermute | solution.py:718
  42.8 35.1 %collective-permute-start.4 = (f32[4,3,8,8,128]{4,3,2,1,0:T(8,128)}, f32[4,3,8,8,128]{4,3,2,1,0:T(8,128)}, u32[]{:S(2)}, u32[]{:S(2)}) collective-permute-start(f32[4,3,8,8,128]{4,3,2,1,0:T(8,128)} %collective-permute-done.3), channel_id=1, source_target_pairs={{8,0},{9,1},{10,2},{11,3},{12,4},{13,5},{14,6},{15,7}} | collective-permute-start | bytes 1179656 | tf_op jit(solution)/shard_map/ppermute | solution.py:740
  44.7 0.9 copy-start.5
  45.6 0.9 copy-start.6
  48.2 8.6 %collective-permute-start.12 = (f32[3,2,4096]{2,1,0:T(2,128)}, f32[3,2,4096]{2,1,0:T(2,128)S(1)}, u32[]{:S(2)}, u32[]{:S(2)}) collective-permute-start(f32[3,2,4096]{2,1,0:T(2,128)} %get-tuple-element.21), channel_id=1, source_target_pairs={{0,1},{1,2},{2,3},{3,4},{4,5},{5,6},{6,7},{8,9},{9,10},{10,11},{11... | collective-permute-start | bytes 294920 | tf_op jit(solution)/shard_map/ppermute | solution.py:626
  50.1 45.1 %collective-permute-start.1 = (f32[8,3,8,8,128]{4,3,2,1,0:T(8,128)S(1)}, f32[8,3,8,8,128]{4,3,2,1,0:T(8,128)S(1)}, u32[]{:S(2)}, u32[]{:S(2)}) collective-permute-start(f32[8,3,8,8,128]{4,3,2,1,0:T(8,128)S(1)} %all-to-all-done.refs_1_), channel_id=1, source_target_pairs={{8,0},{9,1},{10,2},{11,3},{12,4},{13,5},{14,6},{15,7}} | collective-permute-start | bytes 2359304 | tf_op jit(solution)/shard_map/ppermute | solution.py:716
  55.5 41.6 %collective-permute-start.5 = (f32[8,3,8,8,128]{4,3,2,1,0:T(8,128)S(1)}, f32[8,3,8,8,128]{4,3,2,1,0:T(8,128)S(1)}, u32[]{:S(2)}, u32[]{:S(2)}) collective-permute-start(f32[8,3,8,8,128]{4,3,2,1,0:T(8,128)S(1)} %all-to-all-done.refs_1_), channel_id=1, source_target_pairs={{16,0},{17,1},{18,2},{19,3},{20,4},{21,5},{22,6},{23,7}} | collective-permute-start | bytes 2359304 | tf_op jit(solution)/shard_map/ppermute | solution.py:717
  56.8 53.9 %copy-start.12 = (f32[3,2,4096]{2,1,0:T(2,128)}, f32[3,2,4096]{2,1,0:T(2,128)S(1)}, u32[]{:S(2)}) copy-start(f32[3,2,4096]{2,1,0:T(2,128)S(1)} %collective-permute-done.12.refs_2_) | copy-start | bytes 294916
  56.8 53.8 %collective-permute-start.14 = (f32[3,2,16,4096]{3,2,1,0:T(8,128)}, f32[3,2,16,4096]{3,2,1,0:T(8,128)}, u32[]{:S(2)}, u32[]{:S(2)}) collective-permute-start(f32[3,2,16,4096]{3,2,1,0:T(8,128)} %get-tuple-element.24.refs_5_), channel_id=1, source_target_pairs={{8,9},{9,10},{10,11},{11,12},{12,13},{13,14},{14,15},{16,17},{17,1... | collective-permute-start | bytes 4718600 | tf_op jit(solution)/shard_map/ppermute | solution.py:626
  58.6 19.3 %copy-start.7 = (f32[4,3,8,8,128]{4,3,2,1,0:T(8,128)}, f32[4,3,8,8,128]{4,3,2,1,0:T(8,128)S(1)}, u32[]{:S(2)}) copy-start(f32[4,3,8,8,128]{4,3,2,1,0:T(8,128)S(1)} %collective-permute-done.2.refs_2_) | copy-start | bytes 1179652
  58.6 52.0 %collective-permute-start.15 = (f32[3,2,16,4096]{3,2,1,0:T(8,128)}, f32[3,2,16,4096]{3,2,1,0:T(8,128)}, u32[]{:S(2)}, u32[]{:S(2)}) collective-permute-start(f32[3,2,16,4096]{3,2,1,0:T(8,128)} %get-tuple-element.23.refs_4_), channel_id=1, source_target_pairs={{9,8},{10,9},{11,10},{12,11},{13,12},{14,13},{15,14},{17,16},{18,1... | collective-permute-start | bytes 4718600 | tf_op jit(solution)/shard_map/ppermute | solution.py:626
  78.0 28.5 %collective-permute-start.8 = (f32[3,2,8,4096]{3,2,1,0:T(8,128)}, f32[3,2,8,4096]{3,2,1,0:T(8,128)S(1)}, u32[]{:S(2)}, u32[]{:S(2)}) collective-permute-start(f32[3,2,8,4096]{3,2,1,0:T(8,128)} %get-tuple-element.19.refs_9_.refs_10_), channel_id=1, source_target_pairs={{8,9},{9,8},{10,11},{11,10},{12,13},{13,12},{14,15},{15,14},{16,17... | collective-permute-start | bytes 2359304 | tf_op jit(solution)/shard_map/ppermute | solution.py:626
  95.2 3.9 %copy-start.3 = (f32[8,3,8,8,128]{4,3,2,1,0:T(8,128)}, f32[8,3,8,8,128]{4,3,2,1,0:T(8,128)S(1)}, u32[]{:S(2)}) copy-start(f32[8,3,8,8,128]{4,3,2,1,0:T(8,128)S(1)} %collective-permute-done.1.refs_0_) | copy-start | bytes 2359300
  95.2 7.6 %collective-permute-start.13 = (f32[3,2,4096]{2,1,0:T(2,128)}, f32[3,2,4096]{2,1,0:T(2,128)S(1)}, u32[]{:S(2)}, u32[]{:S(2)}) collective-permute-start(f32[3,2,4096]{2,1,0:T(2,128)} %get-tuple-element.22), channel_id=1, source_target_pairs={{1,0},{2,1},{3,2},{4,3},{5,4},{6,5},{7,6},{9,8},{10,9},{11,10},{12... | collective-permute-start | bytes 294920 | tf_op jit(solution)/shard_map/ppermute | solution.py:626
  97.1 1.9 %copy-start.4 = (f32[8,3,8,8,128]{4,3,2,1,0:T(8,128)}, f32[8,3,8,8,128]{4,3,2,1,0:T(8,128)S(1)}, u32[]{:S(2)}) copy-start(f32[8,3,8,8,128]{4,3,2,1,0:T(8,128)S(1)} %collective-permute-done.5.refs_4_) | copy-start | bytes 2359300
  97.1 13.5 %collective-permute-start.9 = (f32[3,2,8,4096]{3,2,1,0:T(8,128)}, f32[3,2,8,4096]{3,2,1,0:T(8,128)S(1)}, u32[]{:S(2)}, u32[]{:S(2)}) collective-permute-start(f32[3,2,8,4096]{3,2,1,0:T(8,128)} %get-tuple-element.18.refs_8_.refs_9_), channel_id=1, source_target_pairs={{8,9},{9,8},{10,11},{11,10},{12,13},{13,12},{14,15},{15,14},{16,17... | collective-permute-start | bytes 2359304 | tf_op jit(solution)/shard_map/ppermute | solution.py:626
  102.8 7.9 %copy-start.13 = (f32[3,2,4096]{2,1,0:T(2,128)}, f32[3,2,4096]{2,1,0:T(2,128)S(1)}, u32[]{:S(2)}) copy-start(f32[3,2,4096]{2,1,0:T(2,128)S(1)} %collective-permute-done.13.refs_3_) | copy-start | bytes 294916
  102.8 20.4 %collective-permute-start.6 = (f32[3,2,8,4096]{3,2,1,0:T(8,128)}, f32[3,2,8,4096]{3,2,1,0:T(8,128)S(1)}, u32[]{:S(2)}, u32[]{:S(2)}) collective-permute-start(f32[3,2,8,4096]{3,2,1,0:T(8,128)} %get-tuple-element.17.refs_6_), channel_id=1, source_target_pairs={{0,1},{1,2},{2,3},{3,4},{4,5},{5,6},{6,7}} | collective-permute-start | bytes 2359304 | tf_op jit(solution)/shard_map/ppermute | solution.py:626
  106.5 4.2 %copy-start.1 = (f32[3,2,8,4096]{3,2,1,0:T(8,128)}, f32[3,2,8,4096]{3,2,1,0:T(8,128)S(1)}, u32[]{:S(2)}) copy-start(f32[3,2,8,4096]{3,2,1,0:T(8,128)S(1)} %collective-permute-done.8.refs_10_.refs_11_) | copy-start | bytes 2359300
  106.5 16.8 %collective-permute-start.7 = (f32[3,2,8,4096]{3,2,1,0:T(8,128)}, f32[3,2,8,4096]{3,2,1,0:T(8,128)S(1)}, u32[]{:S(2)}, u32[]{:S(2)}) collective-permute-start(f32[3,2,8,4096]{3,2,1,0:T(8,128)} %get-tuple-element.16.refs_5_), channel_id=1, source_target_pairs={{1,0},{2,1},{3,2},{4,3},{5,4},{6,5},{7,6}} | collective-permute-start | bytes 2359304 | tf_op jit(solution)/shard_map/ppermute | solution.py:626
  110.7 0.9 copy-start.2
  123.2 0.9 copy-start.8
  124.1 0.9 copy-start.9

commit v3 on v2

--- a/solution.py
+++ b/solution.py
@@ -55,7 +55,7 @@
     return jnp.dot(a, b, preferred_element_type=F32)
 
 
-def first_kernel(noise, rim_ref, edge, sem):
+def first_kernel(noise, vel, rim_ref, near_ref, far_ref, edge, sem):
     comps, count, depth, span = noise.shape
     groups = LANES // HALF
     rows = depth // groups
@@ -66,6 +66,15 @@
         for c in range(comps)
     ]
     for copy in copies:
+        copy.start()
+    cells = vel.shape[1]
+    even = lax.rem(lax.axis_index("grp"), 2) == 0
+    x = jnp.where(even, cells - 2, 0)
+    faces = [
+        pltpu.make_async_copy(vel.at[:, pl.ds(x, 2)], near_ref, sem.at[comps]),
+        pltpu.make_async_copy(vel.at[:, pl.ds(cells - 2 - x, 2)], far_ref, sem.at[comps + 1]),
+    ]
+    for copy in faces:
         copy.start()
     lane = lax.broadcasted_iota(jnp.int32, (count, rows, LANES), 2)
     for c in range(comps):
@@ -78,6 +87,8 @@
             piece = jnp.where(use_left, to_left, to_right)
             result = piece if q == 0 else jnp.where(lane >= HALF * q, piece, result)
         rim_ref[c] = result
+    for copy in faces:
+        copy.wait()
 
 
 def face_copies(vel, first, cells, dn, up, sem, at):
@@ -92,19 +103,6 @@
                     )
                 )
     return copies
-
-
-def xfaces_kernel(vel, after, near_ref, far_ref, sem):
-    del after
-    cells = vel.shape[1]
-    even = lax.rem(lax.axis_index("grp"), 2) == 0
-    at = jnp.where(even, cells - 2, 0)
-    run_copies(
-        [
-            pltpu.make_async_copy(vel.at[:, pl.ds(at, 2)], near_ref, sem.at[0]),
-            pltpu.make_async_copy(vel.at[:, pl.ds(cells - 2 - at, 2)], far_ref, sem.at[1]),
-        ]
-    )
 
 
 def zfaces_kernel(vel, after, all_dn, all_up, high_dn, high_up, sem):
@@ -175,9 +173,8 @@
         out_ref[c] = along.reshape(count, depth, width)
 
 
-def filter_kernel(whole, along_hbm, rim, after, previous, decay_ref, factor_ref, mean_ref,
+def filter_kernel(whole, along_hbm, rim, previous, decay_ref, factor_ref, mean_ref,
                     out_ref, planes_ref, prev_ref, along_ref, rim_ref, sem):
-    del after
     comps, count, depth, width = along_ref.shape
     line = lax.axis_index("grp")
     first = part_of(line) * width
@@ -257,13 +254,17 @@
         put(2, p, factor[3] * a + factor[4] * b + factor[5] * d)
 
 
-def sides(near, far):
-    even = lax.rem(lax.axis_index("grp"), 2) == 0
-    return [(even, far, near), (jnp.logical_not(even), near, far)]
-
-
-def corners_kernel(near, far, after, up_ref, dn_ref, sem):
-    del after
+def sides(near, far, detour):
+    line = lax.axis_index("grp")
+    even = lax.rem(line, 2) == 0
+    odd = (jnp.logical_not(even), near, far)
+    if detour is None:
+        return [(even, far, near), odd]
+    return [(line == 2, detour, near), (jnp.logical_and(even, line != 2), far, near), odd]
+
+
+def corners_kernel(*refs):
+    near, far, *detour, _, up_ref, dn_ref, sem = refs
     slab = near.shape[2]
 
     def rows(left, right):
@@ -276,7 +277,7 @@
                     )
         return copies
 
-    for condition, left, right in sides(near, far):
+    for condition, left, right in sides(near, far, detour[0] if detour else None):
 
         @pl.when(condition)
         def _(left=left, right=right):
@@ -414,6 +415,22 @@
     return shift + side + shift
 
 
+def begin(copies, condition=None):
+    if condition is not None:
+        pl.when(condition)(lambda: begin(copies))
+        return
+    for copy in copies:
+        copy.start()
+
+
+def finish(copies, condition=None):
+    if condition is not None:
+        pl.when(condition)(lambda: finish(copies))
+        return
+    for copy in copies:
+        copy.wait()
+
+
 def run_copies(copies):
     for copy in copies:
         copy.start()
@@ -436,54 +453,40 @@
 
 
 def own_kernel(rows, ranks, vel, *refs):
-    (near, far, up_corners, dn_corners, dn_all, up_all, b_all, a_all, dn_hi, up_hi, b_hi, a_hi,
-     out_hbm, start, sect, out, nb, na, b2, b0, a0, a2, eb, ea, corner, sem, out_sem) = refs
+    near, far, *detour = refs[:-25]
+    (up_corners, dn_corners, dn_all, up_all, b_all, a_all, dn_hi, up_hi, b_hi, a_hi, out_hbm,
+     start, sect, out, nb, na, b2, b0, a0, a2, eb, ea, corner, sem, out_sem) = refs[-25:]
     cells = vel.shape[1]
     low = cells - dn_hi.shape[2]
     span = vel.shape[3]
     has_before, has_after, has_left, has_right, is_first = roles(rows, ranks)
     first = jnp.where(is_first, low + 2, 0)
-    always = [
-        (vel.at[:, pl.ds(low, cells - low)], start.at[:, pl.ds(2 + low, cells - low)]),
-        (up_corners, corner.at[0]),
-        (dn_corners, corner.at[1]),
-    ]
-    always = [pltpu.make_async_copy(p, q, sem.at[i]) for i, (p, q) in enumerate(always)]
-    for copy in always:
-        copy.start()
-
-    def rest(pieces):
-        run_copies(
-            [
-                pltpu.make_async_copy(p, q, sem.at[len(always) + i])
-                for i, (p, q) in enumerate(pieces)
-            ]
-        )
-
-    for condition, left, right in sides(near, far):
-
-        @pl.when(condition)
-        def _(left=left, right=right):
-            rest(
-                [(left, start.at[:, pl.ds(0, 2)]), (right, start.at[:, pl.ds(cells + 2, 2)])]
-            )
-
-    @pl.when(is_first)
-    def _():
-        rest(row_pieces((dn_hi, up_hi, b_hi, a_hi), low, nb, na, b2, b0, a0, a2))
-
-    @pl.when(jnp.logical_not(is_first))
-    def _():
-        pieces = row_pieces((dn_all, up_all, b_all, a_all), 0, nb, na, b2, b0, a0, a2)
-        rest(pieces + [(vel.at[:, pl.ds(0, low)], start.at[:, pl.ds(2, low)])])
-
-    for copy in always:
-        copy.wait()
+    is_other = jnp.logical_not(is_first)
+    left_at, right_at = start.at[:, pl.ds(0, 2)], start.at[:, pl.ds(cells + 2, 2)]
+    rows_first = row_pieces((dn_hi, up_hi, b_hi, a_hi), low, nb, na, b2, b0, a0, a2)
+    rows_other = row_pieces((dn_all, up_all, b_all, a_all), 0, nb, na, b2, b0, a0, a2)
+    ends = [(up_corners, corner.at[0]), (dn_corners, corner.at[1])]
+    main = [(vel.at[:, pl.ds(low, cells - low)], start.at[:, pl.ds(2 + low, cells - low)])]
+    rest = [(vel.at[:, pl.ds(0, low)], start.at[:, pl.ds(2, low)])]
+
+    def copies(pieces, at):
+        return [pltpu.make_async_copy(p, q, sem.at[at + i]) for i, (p, q) in enumerate(pieces)]
+
+    begin(copies(rows_first, 0), is_first)
+    begin(copies(rows_other, 0), is_other)
+    begin(copies(ends, 6))
+    begin(copies(main, 8))
+    for condition, left, right in sides(near, far, detour[0] if detour else None):
+        begin(copies([(right, right_at)], 9), condition)
+        begin(copies([(left, left_at)], 10), jnp.logical_and(condition, is_other))
+    begin(copies(rest, 11), is_other)
+    finish(copies(rows_first, 0), is_first)
+    finish(copies(rows_other, 0), is_other)
+    finish(copies(ends, 6))
 
     @pl.when(jnp.logical_not(has_right))
     def _():
         for c in range(3):
-            start[c, cells + 2] = jnp.zeros((SUB, span), F32)
             for i in range(2):
                 corner[i, c, 1:2, :] = jnp.zeros((1, span), F32)
 
@@ -501,6 +504,15 @@
 
     edge_rows(nb, b2, b0, eb, has_before, low // SUB, groups, span)
     edge_rows(na, a0, a2, ea, has_after, low // SUB, groups, span)
+    finish(copies(main, 8))
+    finish(copies([(near, right_at)], 9))
+    finish(copies([(near, left_at)], 10), is_other)
+    finish(copies(rest, 11), is_other)
+
+    @pl.when(jnp.logical_not(has_right))
+    def _():
+        for c in range(3):
+            start[c, cells + 2] = jnp.zeros((SUB, span), F32)
 
     def make(x, keep=None):
         section_plane(x, start, sect, nb, na, span, keep)
@@ -540,27 +552,20 @@
 
     @pl.when(is_first)
     def _():
-        pieces = [(vel.at[:, pl.ds(low, 4)], start.at[:, pl.ds(low + 2, 4)])]
+        edges = row_pieces((dn_in, up_in, b_in, a_in), 0, nb, na, b2, b0, a0, a2)
+        edges += row_pieces((dn_hi, up_hi, b_hi, a_hi), low, nb, na, b2, b0, a0, a2)
+        main = [(vel.at[:, pl.ds(low, 4)], start.at[:, pl.ds(low + 2, 4)])]
         for piece, (source, part, many) in zip(parts, places):
             width = piece.shape[4]
-            for s in range(piece.shape[0]):
-                at = ((source + s) * many + part) * width
-                pieces.append((piece.at[s], start.at[:, pl.ds(2, low), :, pl.ds(at, width)]))
-        for lo, hi, j, ref, first in (
-            (b_in, b_hi, 1, nb, SUB),
-            (a_in, a_hi, 0, na, SUB),
-            (b_in, b_hi, 0, b2, 0),
-            (a_in, a_hi, 1, a2, 0),
-            (dn_in, dn_hi, 0, b0, 0),
-            (up_in, up_hi, 1, a0, 0),
-        ):
-            pieces.append((lo.at[:, j], ref.at[:, pl.ds(first, low)]))
-            pieces.append((hi.at[:, j], ref.at[:, pl.ds(first + low, cells - low)]))
-        copies = [
-            pltpu.make_async_copy(src, dst, sem.at[i]) for i, (src, dst) in enumerate(pieces)
+            for i in range(piece.shape[0]):
+                at = ((source + i) * many + part) * width
+                main.append((piece.at[i], start.at[:, pl.ds(2, low), :, pl.ds(at, width)]))
+        edges = [pltpu.make_async_copy(p, q, sem.at[i]) for i, (p, q) in enumerate(edges)]
+        main = [
+            pltpu.make_async_copy(p, q, sem.at[len(edges) + i]) for i, (p, q) in enumerate(main)
         ]
-        for copy in copies:
-            copy.start()
+        begin(edges)
+        begin(main)
         zero = jnp.zeros((SUB, span), F32)
         for c in range(3):
             start[c, 1] = zero
@@ -568,11 +573,11 @@
             for ref in (nb, na):
                 ref[c, 0:SUB, :] = zero
                 ref[c, SUB + cells :, :] = zero
-        for copy in copies:
-            copy.wait()
+        finish(edges)
         groups = cells // SUB
         edge_rows(nb, b2, b0, eb, has_before, 0, groups, span)
         edge_rows(na, a0, a2, ea, has_after, 0, groups, span)
+        finish(main)
         section_plane(0, start, sect, nb, na, span)
 
         def body(x, _):
@@ -630,14 +635,14 @@
     face_hi = jax.ShapeDtypeStruct((3, 2, high, span), F32)
     xface = jax.ShapeDtypeStruct((3, 2, slab, span), F32)
     full = jax.ShapeDtypeStruct(velocity.shape, F32)
-    rim_out = call(
+    rim_out, near_out, far_out = call(
         first_kernel,
-        packed,
-        VMEM,
-        [ANY],
-        [pltpu.VMEM((comps, count, depth, LANES), F32), dma((comps,))],
+        [packed, xface, xface],
+        [VMEM] * 3,
+        [ANY] * 2,
+        [pltpu.VMEM((comps, count, depth, LANES), F32), dma((comps + 2,))],
         cost(0, noise.size),
-    )(noise)
+    )(noise, velocity)
 
     def idle(lines):
         return [(r * ranks + i, r * ranks + (i ^ 1)) for r in lines for i in range(ranks)]
@@ -678,10 +683,6 @@
             cost(6 * noise.size * width, 4 * noise.size),
         )(*inputs, prev, decay, stress_factor, mean_profile[None])
 
-    near_out, far_out = call(
-        xfaces_kernel, [xface, xface], [VMEM] * 2, [ANY] * 2, [dma((2,))], cost(0, velocity.size)
-    )(velocity, rim_out)
-    far = across(far_out, [p for i in odds for p in ((i, i + 1), (i + 1, i))], lone)
     along = call(
         along_kernel,
         jax.ShapeDtypeStruct((comps, count, depth, width), F32),
@@ -692,7 +693,7 @@
     )(noise)
     kernel_a = functools.partial(filter_kernel, span_local)
     made_a = make(
-        kernel_a, [along, rim, near_out], [ANY] * 3,
+        kernel_a, [along, rim], [ANY] * 2,
         [
             pltpu.VMEM((comps, count, depth, width), F32),
             pltpu.VMEM(packed.shape, F32),
@@ -702,6 +703,13 @@
     got_a = lax.all_to_all(made_a, "gx", 0, 0, tiled=True)
 
     near = across(near_out, [p for i in evens for p in ((i, i + 1), (i + 1, i))], [])
+    detour = []
+    if rows == 4:
+        far = across(far_out, [(1, 3), (2, 1)], [0])
+        detour = [across(far, [(3, 2)], [0, 1])]
+    else:
+        far = across(far_out, [p for i in odds for p in ((i, i + 1), (i + 1, i))], lone)
+    xfaces = [near, far] + detour
     face_all = jax.ShapeDtypeStruct((3, 2, cells, span), F32)
     dn_all, up_all, dn_hi, up_hi = call(
         zfaces_kernel, [face_all, face_all, face_hi, face_hi], [VMEM] * 4, [ANY] * 2,
@@ -725,8 +733,9 @@
     )(made_a)
     pair = jax.ShapeDtypeStruct((3, 2, span), F32)
     up_corner, dn_corner = call(
-        corners_kernel, [pair, pair], [VMEM] * 2, [ANY] * 3, [dma((12,))], cost(0, 24 * span)
-    )(near, far, mark)
+        corners_kernel, [pair, pair], [VMEM] * 2, [ANY] * (len(xfaces) + 1), [dma((12,))],
+        cost(0, 24 * span),
+    )(*xfaces, mark)
     up_corners = along_gx(up_corner, 1, everyone)
     dn_corners = along_gx(dn_corner, -1, everyone)
 
@@ -742,12 +751,12 @@
         functools.partial(own_kernel, rows, ranks),
         full,
         ANY,
-        [ANY] * 13,
+        [ANY] * (11 + len(xfaces)),
         fields(cells)
         + rows_scratch(cells, span)
         + [pltpu.VMEM((2, 3, 2, span), F32), dma((12,)), dma((cells,))],
         cost(50 * velocity.size, 8 * velocity.size),
-    )(velocity, near, far, up_corners, dn_corners, dn_all, up_all, b_all, a_all, dn_hi, up_hi, b_hi,
+    )(velocity, *xfaces, up_corners, dn_corners, dn_all, up_all, b_all, a_all, dn_hi, up_hi, b_hi,
       a_hi)
 
     parts = [hop_1, got_a, hop_3, hop_4, hop_2]

time: 140 us -> 128 us (0.914)
  waiting for transfers between devices: 50.9 us -> 39.7 us
  starting transfers between devices: 34.1 us -> 40 us
  Pallas kernels: 48.4 us -> 43 us
    ppermute x1, waiting for transfers between devices: 13 us -> 0.01 us  [local(): hop_1 = lax.ppermute(got_a, 'grp', [(1, 0)])]
    ppermute x8, waiting for transfers between devices: 2.25 us -> 8.13 us  [along_gx(): return lax.ppermute(array, ('grp', 'gx'), pairs)]
    ppermute x1, waiting for transfers between devices: 17.4 us -> 11.7 us  [local(): hop_4 = lax.ppermute(side, 'grp', [(1, 0)])]
    ppermute x2 -> x3, starting transfers between devices: 1.74 us -> 7.47 us  [across(): return lax.ppermute(array, ('grp', 'gx'), pairs + idle(idlers))]
    pallas_call x10 -> x9, Pallas kernels: 48.4 us -> 43 us  [run(): pl.pallas_call(kernel, out_shape=out_shape, in_specs=in_specs, out_specs=...]
    ppermute x1, waiting for transfers between devices: 0.01 us -> 4.68 us  [local(): hop_3 = lax.ppermute(got_a[:half], 'grp', [(3, 0)])]
    all_to_all x1, waiting for transfers between devices: 18.2 us -> 15.2 us  [local(): got_a = lax.all_to_all(made_a, 'gx', 0, 0, tiled=True)]
    unnamed x28, local copies, waits for them, and re-layouts: 5.18 us -> 3.1 us
  transfers between devices with their start and end apart: 17 -> 18, of which waited for: 4 -> 6; matrix products, arithmetic and copies ran while one was open for 0% -> 1% of each run, Pallas kernels for 20% -> 18%
where the time goes in v3:
time: 128 us; the launch traced here: 127 us
  Pallas kernels  43 us (34%)
  starting transfers between devices  40 us (31%)
  waiting for transfers between devices  39.7 us (31%)
  local copies, waits for them, and re-layouts  3.98 us (3%)
    pallas_call x9, Pallas kernels, run(): pl.pallas_call(kernel, out_shape=out_shape, in_specs=in_specs, out_specs=...  43 us
    ppermute x8, starting transfers between devices, along_gx(): return lax.ppermute(array, ('grp', 'gx'), pairs)  19.5 us
    all_to_all x1, waiting for transfers between devices, local(): got_a = lax.all_to_all(made_a, 'gx', 0, 0, tiled=True)  15.2 us
    ppermute x1, waiting for transfers between devices, local(): hop_4 = lax.ppermute(side, 'grp', [(1, 0)])  11.7 us
    ppermute x8, waiting for transfers between devices, along_gx(): return lax.ppermute(array, ('grp', 'gx'), pairs)  8.13 us
    ppermute x3, starting transfers between devices, across(): return lax.ppermute(array, ('grp', 'gx'), pairs + idle(idlers))  7.47 us
    all_to_all x1, starting transfers between devices, local(): got_a = lax.all_to_all(made_a, 'gx', 0, 0, tiled=True)  6.43 us
    ppermute x1, waiting for transfers between devices, local(): hop_3 = lax.ppermute(got_a[:half], 'grp', [(3, 0)])  4.68 us
  transfers between devices with their start and end apart: 18, of which 6 were waited for; matrix products, arithmetic and copies ran while one was open for 1% of the time, Pallas kernels for 18%

profile of v3, /device:TPU:1, one launch (start us, length us, event | category | flops | bytes accessed | tf_op | source)
XLA Modules:
  0.0 127.1 jit_solution(5634144852405832323)
XLA Ops:
  0.0 2.9 %shard_map.65 = (f32[3,8,16,128]{3,2,1,0:T(8,128)}, f32[3,2,8,4096]{3,2,1,0:T(8,128)}, f32[3,2,8,4096]{3,2,1,0:T(8,128)}) custom-call(f32[3,8,64,512]{3,2,1,0:T(8,128)} %noise.3, f32[3,16,8,4096]{3,2,1,0:T(8,128)} %vel.7), custom_call_target="tpu_custom_call" | custom-call | bytes 786432 | tf_op jit(solution)/shard_map/pallas_call | solution.py:600
  2.9 0.0 copy-start.12
  2.9 0.1 collective-permute-start
  3.0 4.0 %shard_map.64.along_hbm = f32[3,8,64,128]{3,2,1,0:T(8,128)} custom-call(f32[3,8,64,512]{3,2,1,0:T(8,128)} %noise.3), custom_call_target="tpu_custom_call" | custom-call | flops 603979776 | bytes 3145728 | tf_op jit(solution)/shard_map/pallas_call | solution.py:600
  7.0 0.0 collective-permute-done.rim
  7.0 0.0 copy-start.13
  7.0 0.7 copy-done.13
  7.7 4.1 %shard_map.66.after = f32[8,3,8,8,128]{4,3,2,1,0:T(8,128)} custom-call(f32[3,8,64,128]{3,2,1,0:T(8,128)} %shard_map.64.along_hbm, f32[3,8,16,128]{3,2,1,0:T(8,128)} %copy-done.13, f32[3,64,512]{2,1,0:T(8,128)} %previous.1, f32[3,64]{1,0:T(4,128)} %decay_ref.1, f32[6,64]{1,0:T(8,128)} %factor_ref.1, f32[1,64]{1,0:T(1,128)} %bitcast.1), custom_call_target="tpu_custom_call" | custom-call | flops 603979776 | bytes 3145728 | tf_op jit(solution)/shard_map/pallas_call | solution.py:600
  11.8 6.4 %all-to-all-start = ((f32[8,3,8,8,128]{4,3,2,1,0:T(8,128)}), f32[8,3,8,8,128]{4,3,2,1,0:T(8,128)S(1)}, u32[]{:S(2)}, u32[]{:S(2)}) async-start(f32[8,3,8,8,128]{4,3,2,1,0:T(8,128)} %shard_map.66.after), calls=%async_computation | async-start | bytes 1572864 | tf_op jit(solution)/shard_map/all_to_all | solution.py:703
  18.2 0.0 copy-done.12
  18.2 1.9 %collective-permute-start.11 = (f32[3,2,8,4096]{3,2,1,0:T(8,128)S(1)}, f32[3,2,8,4096]{3,2,1,0:T(8,128)S(1)}, u32[]{:S(2)}, u32[]{:S(2)}) collective-permute-start(f32[3,2,8,4096]{3,2,1,0:T(8,128)S(1)} %copy-done.12), channel_id=1, source_target_pairs={{8,24},{9,25},{10,26},{11,27},{12,28},{13,29},{14,30},{15,31},{16,... | collective-permute-start | bytes 2359304 | tf_op jit(solution)/shard_map/ppermute | solution.py:652
  20.2 2.9 %collective-permute-start.10 = (f32[3,2,8,4096]{3,2,1,0:T(8,128)}, f32[3,2,8,4096]{3,2,1,0:T(8,128)}, u32[]{:S(2)}, u32[]{:S(2)}) collective-permute-start(f32[3,2,8,4096]{3,2,1,0:T(8,128)} %get-tuple-element.21), channel_id=1, source_target_pairs={{0,8},{1,9},{2,10},{3,11},{4,12},{5,13},{6,14},{7,15},{8,0},{9,1},... | collective-permute-start | bytes 2359304 | tf_op jit(solution)/shard_map/ppermute | solution.py:652
  23.0 15.2 %all-to-all-done.refs_1_ = f32[8,3,8,8,128]{4,3,2,1,0:T(8,128)S(1)} async-done(((f32[8,3,8,8,128]{4,3,2,1,0:T(8,128)}), f32[8,3,8,8,128]{4,3,2,1,0:T(8,128)S(1)}, u32[]{:S(2)}, u32[]{:S(2)}) %all-to-all-start) | async-done | bytes 786464 | tf_op jit(solution)/shard_map/all_to_all | solution.py:703
  38.2 0.9 fusion
  39.1 1.4 %collective-permute-start.3 = (f32[4,3,8,8,128]{4,3,2,1,0:T(8,128)S(1)}, f32[4,3,8,8,128]{4,3,2,1,0:T(8,128)}, u32[]{:S(2)}, u32[]{:S(2)}) collective-permute-start(f32[4,3,8,8,128]{4,3,2,1,0:T(8,128)S(1)} %get-tuple-element.27), channel_id=1, source_target_pairs={{24,8},{25,9},{26,10},{27,11},{28,12},{29,13},{30,14},{31,15}} | collective-permute-start | bytes 1179656 | tf_op jit(solution)/shard_map/ppermute | solution.py:723
  40.5 1.3 %collective-permute-start.1 = (f32[8,3,8,8,128]{4,3,2,1,0:T(8,128)S(1)}, f32[8,3,8,8,128]{4,3,2,1,0:T(8,128)S(1)}, u32[]{:S(2)}, u32[]{:S(2)}) collective-permute-start(f32[8,3,8,8,128]{4,3,2,1,0:T(8,128)S(1)} %all-to-all-done.refs_1_), channel_id=1, source_target_pairs={{8,0},{9,1},{10,2},{11,3},{12,4},{13,5},{14,6},{15,7}} | collective-permute-start | bytes 2359304 | tf_op jit(solution)/shard_map/ppermute | solution.py:724
  41.8 1.3 %collective-permute-start.2 = (f32[4,3,8,8,128]{4,3,2,1,0:T(8,128)}, f32[4,3,8,8,128]{4,3,2,1,0:T(8,128)S(1)}, u32[]{:S(2)}, u32[]{:S(2)}) collective-permute-start(f32[4,3,8,8,128]{4,3,2,1,0:T(8,128)} %get-tuple-element.28), channel_id=1, source_target_pairs={{24,0},{25,1},{26,2},{27,3},{28,4},{29,5},{30,6},{31,7}} | collective-permute-start | bytes 1179656 | tf_op jit(solution)/shard_map/ppermute | solution.py:726
  43.1 0.0 collective-permute-done.3
  43.1 1.3 %collective-permute-start.4 = (f32[4,3,8,8,128]{4,3,2,1,0:T(8,128)}, f32[4,3,8,8,128]{4,3,2,1,0:T(8,128)S(1)}, u32[]{:S(2)}, u32[]{:S(2)}) collective-permute-start(f32[4,3,8,8,128]{4,3,2,1,0:T(8,128)} %collective-permute-done.3), channel_id=1, source_target_pairs={{8,0},{9,1},{10,2},{11,3},{12,4},{13,5},{14,6},{15,7}} | collective-permute-start | bytes 1179656 | tf_op jit(solution)/shard_map/ppermute | solution.py:749
  44.4 0.0 collective-permute-done.11.refs_1_
  44.4 0.0 copy-start.5
  44.4 1.3 %collective-permute-start.5 = (f32[8,3,8,8,128]{4,3,2,1,0:T(8,128)S(1)}, f32[8,3,8,8,128]{4,3,2,1,0:T(8,128)S(1)}, u32[]{:S(2)}, u32[]{:S(2)}) collective-permute-start(f32[8,3,8,8,128]{4,3,2,1,0:T(8,128)S(1)} %all-to-all-done.refs_1_), channel_id=1, source_target_pairs={{16,0},{17,1},{18,2},{19,3},{20,4},{21,5},{22,6},{23,7}} | collective-permute-start | bytes 2359304 | tf_op jit(solution)/shard_map/ppermute | solution.py:725
  45.7 4.1 %shard_map.68 = (f32[3,2,16,4096]{3,2,1,0:T(8,128)}, f32[3,2,16,4096]{3,2,1,0:T(8,128)}, f32[3,2,8,4096]{3,2,1,0:T(8,128)}, f32[3,2,8,4096]{3,2,1,0:T(8,128)}) custom-call(f32[3,16,8,4096]{3,2,1,0:T(8,128)} %vel.7, f32[8,3,8,8,128]{4,3,2,1,0:T(8,128)} %shard_map.66.after), custom_call_target="tpu_custom_call" | custom-call | bytes 1572864 | tf_op jit(solution)/shard_map/pallas_call | solution.py:600
  49.8 0.0 copy-done
  49.8 0.0 copy-done.5
  49.8 0.0 collective-permute-done.10.refs_0_
  49.8 1.8 %collective-permute-start.15 = (f32[3,2,16,4096]{3,2,1,0:T(8,128)}, f32[3,2,16,4096]{3,2,1,0:T(8,128)}, u32[]{:S(2)}, u32[]{:S(2)}) collective-permute-start(f32[3,2,16,4096]{3,2,1,0:T(8,128)} %get-tuple-element.26.refs_6_), channel_id=1, source_target_pairs={{8,9},{9,10},{10,11},{11,12},{12,13},{13,14},{14,15},{16,17},{17,1... | collective-permute-start | bytes 4718600 | tf_op jit(solution)/shard_map/ppermute | solution.py:631
  51.7 4.7 %collective-permute-done.2.refs_2_ = f32[4,3,8,8,128]{4,3,2,1,0:T(8,128)S(1)} collective-permute-done((f32[4,3,8,8,128]{4,3,2,1,0:T(8,128)}, f32[4,3,8,8,128]{4,3,2,1,0:T(8,128)S(1)}, u32[]{:S(2)}, u32[]{:S(2)}) %collective-permute-start.2) | collective-permute-done | bytes 393248 | tf_op jit(solution)/shard_map/ppermute | solution.py:726
  56.3 1.9 %collective-permute-start.16 = (f32[3,2,16,4096]{3,2,1,0:T(8,128)}, f32[3,2,16,4096]{3,2,1,0:T(8,128)}, u32[]{:S(2)}, u32[]{:S(2)}) collective-permute-start(f32[3,2,16,4096]{3,2,1,0:T(8,128)} %get-tuple-element.25.refs_5_), channel_id=1, source_target_pairs={{9,8},{10,9},{11,10},{12,11},{13,12},{14,13},{15,14},{17,16},{18,1... | collective-permute-start | bytes 4718600 | tf_op jit(solution)/shard_map/ppermute | solution.py:631
  58.2 11.7 %collective-permute-done.4.refs_3_ = f32[4,3,8,8,128]{4,3,2,1,0:T(8,128)S(1)} collective-permute-done((f32[4,3,8,8,128]{4,3,2,1,0:T(8,128)}, f32[4,3,8,8,128]{4,3,2,1,0:T(8,128)S(1)}, u32[]{:S(2)}, u32[]{:S(2)}) %collective-permute-start.4) | collective-permute-done | bytes 393248 | tf_op jit(solution)/shard_map/ppermute | solution.py:749
  69.9 2.1 %collective-permute-start.8 = (f32[3,2,8,4096]{3,2,1,0:T(8,128)}, f32[3,2,8,4096]{3,2,1,0:T(8,128)S(1)}, u32[]{:S(2)}, u32[]{:S(2)}) collective-permute-start(f32[3,2,8,4096]{3,2,1,0:T(8,128)} %get-tuple-element.20.refs_10_), channel_id=1, source_target_pairs={{8,9},{9,8},{10,11},{11,10},{12,13},{13,12},{14,15},{15,14},{16,17... | collective-permute-start | bytes 2359304 | tf_op jit(solution)/shard_map/ppermute | solution.py:631
  72.0 0.0 collective-permute-done.1.refs_0_
  72.0 0.0 copy-start.3
  72.0 2.7 %collective-permute-start.12 = (f32[3,2,8,4096]{3,2,1,0:T(8,128)}, f32[3,2,8,4096]{3,2,1,0:T(8,128)}, u32[]{:S(2)}, u32[]{:S(2)}) collective-permute-start(f32[3,2,8,4096]{3,2,1,0:T(8,128)} %copy-done.5), channel_id=1, source_target_pairs={{24,16},{25,17},{26,18},{27,19},{28,20},{29,21},{30,22},{31,23},{0... | collective-permute-start | bytes 2359304 | tf_op jit(solution)/shard_map/ppermute | solution.py:652
  74.7 0.0 collective-permute-done.5.refs_4_
  74.7 0.0 copy-done.7
  74.7 0.0 copy-start.4
  74.7 1.9 %collective-permute-start.9 = (f32[3,2,8,4096]{3,2,1,0:T(8,128)}, f32[3,2,8,4096]{3,2,1,0:T(8,128)S(1)}, u32[]{:S(2)}, u32[]{:S(2)}) collective-permute-start(f32[3,2,8,4096]{3,2,1,0:T(8,128)} %get-tuple-element.19.refs_9_), channel_id=1, source_target_pairs={{8,9},{9,8},{10,11},{11,10},{12,13},{13,12},{14,15},{15,14},{16,17... | collective-permute-start | bytes 2359304 | tf_op jit(solution)/shard_map/ppermute | solution.py:631
  76.7 0.0 copy-done.6
  76.7 3.7 %shard_map.67 = (f32[3,2,8,4096]{3,2,1,0:T(8,128)}, f32[3,2,8,4096]{3,2,1,0:T(8,128)}) custom-call(f32[8,3,8,8,128]{4,3,2,1,0:T(8,128)} %copy-done.3, f32[8,3,8,8,128]{4,3,2,1,0:T(8,128)} %copy-done, f32[4,3,8,8,128]{4,3,2,1,0:T(8,128)} %copy-done.6, f32[4,3,8,8,128]{4,3,2,1,0:T(8,128)} %copy-done.7, f32[8,3,8,8,128]{4,3,2,1,0:T(8,128)} %copy-done.4), custom_call_target="tpu_custom_call" | custom-call | bytes 6291456 | tf_op jit(solution)/shard_map/pallas_call | solution.py:600
  80.4 0.8 collective-permute-done.8.refs_11_
  81.3 4.3 %collective-permute-start.6 = (f32[3,2,8,4096]{3,2,1,0:T(8,128)}, f32[3,2,8,4096]{3,2,1,0:T(8,128)S(1)}, u32[]{:S(2)}, u32[]{:S(2)}) collective-permute-start(f32[3,2,8,4096]{3,2,1,0:T(8,128)} %get-tuple-element.18.refs_6_), channel_id=1, source_target_pairs={{0,1},{1,2},{2,3},{3,4},{4,5},{5,6},{6,7}} | collective-permute-start | bytes 2359304 | tf_op jit(solution)/shard_map/ppermute | solution.py:631
  85.5 0.0 collective-permute-done.12.refs_2_
  85.5 1.9 %collective-permute-start.7 = (f32[3,2,8,4096]{3,2,1,0:T(8,128)}, f32[3,2,8,4096]{3,2,1,0:T(8,128)S(1)}, u32[]{:S(2)}, u32[]{:S(2)}) collective-permute-start(f32[3,2,8,4096]{3,2,1,0:T(8,128)} %get-tuple-element.17.refs_5_), channel_id=1, source_target_pairs={{1,0},{2,1},{3,2},{4,3},{5,4},{6,5},{7,6}} | collective-permute-start | bytes 2359304 | tf_op jit(solution)/shard_map/ppermute | solution.py:631
  87.5 0.6 shard_map.69.refs_3_
  88.1 1.6 %shard_map.70 = (f32[3,2,4096]{2,1,0:T(2,128)}, f32[3,2,4096]{2,1,0:T(2,128)}) custom-call(f32[3,2,8,4096]{3,2,1,0:T(8,128)} %collective-permute-done.10.refs_0_, f32[3,2,8,4096]{3,2,1,0:T(8,128)} %copy-done.5, f32[3,2,8,4096]{3,2,1,0:T(8,128)} %collective-permute-done.12.refs_2_, f32[8,128]{1,0:T(8,128)} %shard_map.69.refs_3_), custom_call_target="tpu_custom_call" | custom-call | bytes 98304 | tf_op jit(solution)/shard_map/pallas_call | solution.py:600
  89.7 0.0 collective-permute-done.9.refs_12_
  89.7 0.0 copy-start.2
  89.7 3.6 %collective-permute-start.13 = (f32[3,2,4096]{2,1,0:T(2,128)}, f32[3,2,4096]{2,1,0:T(2,128)S(1)}, u32[]{:S(2)}, u32[]{:S(2)}) collective-permute-start(f32[3,2,4096]{2,1,0:T(2,128)} %get-tuple-element.23), channel_id=1, source_target_pairs={{0,1},{1,2},{2,3},{3,4},{4,5},{5,6},{6,7},{8,9},{9,10},{10,11},{11... | collective-permute-start | bytes 294920 | tf_op jit(solution)/shard_map/ppermute | solution.py:631
  93.4 2.4 %collective-permute-done.13.refs_3_ = f32[3,2,4096]{2,1,0:T(2,128)S(1)} collective-permute-done((f32[3,2,4096]{2,1,0:T(2,128)}, f32[3,2,4096]{2,1,0:T(2,128)S(1)}, u32[]{:S(2)}, u32[]{:S(2)}) %collective-permute-start.13) | collective-permute-done | bytes 98336 | tf_op jit(solution)/shard_map/ppermute | solution.py:631
  95.8 1.9 %collective-permute-start.14 = (f32[3,2,4096]{2,1,0:T(2,128)}, f32[3,2,4096]{2,1,0:T(2,128)S(1)}, u32[]{:S(2)}, u32[]{:S(2)}) collective-permute-start(f32[3,2,4096]{2,1,0:T(2,128)} %get-tuple-element.24), channel_id=1, source_target_pairs={{1,0},{2,1},{3,2},{4,3},{5,4},{6,5},{7,6},{9,8},{10,9},{11,10},{12... | collective-permute-start | bytes 294920 | tf_op jit(solution)/shard_map/ppermute | solution.py:631
  97.7 4.9 %collective-permute-done.14.refs_4_ = f32[3,2,4096]{2,1,0:T(2,128)S(1)} collective-permute-done((f32[3,2,4096]{2,1,0:T(2,128)}, f32[3,2,4096]{2,1,0:T(2,128)S(1)}, u32[]{:S(2)}, u32[]{:S(2)}) %collective-permute-start.14) | collective-permute-done | bytes 98336 | tf_op jit(solution)/shard_map/ppermute | solution.py:631
  102.6 0.0 collective-permute-done.15.refs_7_
  102.6 0.0 collective-permute-done.16.refs_8_
  102.6 0.0 copy-done.1
  102.6 0.0 copy-done.2
  102.6 0.0 copy-done.10
  102.6 0.6 copy-done.11
  103.2 9.3 %shard_map.71.refs_13_ = f32[3,16,8,4096]{3,2,1,0:T(8,128)} custom-call(f32[3,16,8,4096]{3,2,1,0:T(8,128)} %vel.7, f32[3,2,8,4096]{3,2,1,0:T(8,128)} %collective-permute-done.10.refs_0_, f32[3,2,8,4096]{3,2,1,0:T(8,128)} %copy-done.5, f32[3,2,8,4096]{3,2,1,0:T(8,128)} %collective-permute-done.12.refs_2_, f32[3,2,4096]{2,1,0:T(2,128)} %copy-done.10, ...), custom_call_target="tpu_custom_call" | custom-call | flops 78643200 | bytes 12582912 | tf_op jit(solution)/shard_map/pallas_call | solution.py:600
  112.6 0.0 collective-permute-done.6.refs_7_
  112.6 0.0 collective-permute-done.7.refs_8_
  112.6 0.9 copy-done.8
  113.5 0.9 copy-done.9
  114.4 12.7 %shard_map.72 = f32[3,16,8,4096]{3,2,1,0:T(8,128)} custom-call(f32[3,16,8,4096]{3,2,1,0:T(8,128)} %vel.7, f32[8,3,8,8,128]{4,3,2,1,0:T(8,128)} %copy-done.3, f32[8,3,8,8,128]{4,3,2,1,0:T(8,128)} %copy-done, f32[4,3,8,8,128]{4,3,2,1,0:T(8,128)} %copy-done.6, f32[4,3,8,8,128]{4,3,2,1,0:T(8,128)} %copy-done.7, ...), custom_call_target="tpu_custom_call", output_to_operand_aliasing={{}: (14, {})} | custom-call | flops 47185920 | bytes 7864320 | tf_op jit(solution)/shard_map/pallas_call | solution.py:600
  (10 shorter events, 0.0 us)
Async XLA Ops:
  2.9 15.3 %copy-start.12 = (f32[3,2,8,4096]{3,2,1,0:T(8,128)S(1)}, f32[3,2,8,4096]{3,2,1,0:T(8,128)}, u32[]{:S(2)}) copy-start(f32[3,2,8,4096]{3,2,1,0:T(8,128)} %get-tuple-element.22) | copy-start | bytes 2359300
  2.9 4.1 %collective-permute-start = (f32[3,8,16,128]{3,2,1,0:T(8,128)}, f32[3,8,16,128]{3,2,1,0:T(8,128)S(1)}, u32[]{:S(2)}, u32[]{:S(2)}) collective-permute-start(f32[3,8,16,128]{3,2,1,0:T(8,128)} %get-tuple-element.16), channel_id=1, source_target_pairs={{0,1},{1,0},{2,3},{3,2},{4,5},{5,4},{6,7},{7,6},{24,25},{25,24},{2... | collective-permute-start | bytes 589832 | tf_op jit(solution)/shard_map/ppermute | solution.py:657
  7.0 0.7 copy-start.13
  11.8 26.4 %all-to-all-start = ((f32[8,3,8,8,128]{4,3,2,1,0:T(8,128)}), f32[8,3,8,8,128]{4,3,2,1,0:T(8,128)S(1)}, u32[]{:S(2)}, u32[]{:S(2)}) async-start(f32[8,3,8,8,128]{4,3,2,1,0:T(8,128)} %shard_map.66.after), calls=%async_computation | async-start | bytes 1572864 | tf_op jit(solution)/shard_map/all_to_all | solution.py:703
  18.2 26.2 %collective-permute-start.11 = (f32[3,2,8,4096]{3,2,1,0:T(8,128)S(1)}, f32[3,2,8,4096]{3,2,1,0:T(8,128)S(1)}, u32[]{:S(2)}, u32[]{:S(2)}) collective-permute-start(f32[3,2,8,4096]{3,2,1,0:T(8,128)S(1)} %copy-done.12), channel_id=1, source_target_pairs={{8,24},{9,25},{10,26},{11,27},{12,28},{13,29},{14,30},{15,31},{16,... | collective-permute-start | bytes 2359304 | tf_op jit(solution)/shard_map/ppermute | solution.py:652
  20.2 29.7 %collective-permute-start.10 = (f32[3,2,8,4096]{3,2,1,0:T(8,128)}, f32[3,2,8,4096]{3,2,1,0:T(8,128)}, u32[]{:S(2)}, u32[]{:S(2)}) collective-permute-start(f32[3,2,8,4096]{3,2,1,0:T(8,128)} %get-tuple-element.21), channel_id=1, source_target_pairs={{0,8},{1,9},{2,10},{3,11},{4,12},{5,13},{6,14},{7,15},{8,0},{9,1},... | collective-permute-start | bytes 2359304 | tf_op jit(solution)/shard_map/ppermute | solution.py:652
  38.2 11.6 %copy-start = (f32[8,3,8,8,128]{4,3,2,1,0:T(8,128)}, f32[8,3,8,8,128]{4,3,2,1,0:T(8,128)S(1)}, u32[]{:S(2)}) copy-start(f32[8,3,8,8,128]{4,3,2,1,0:T(8,128)S(1)} %all-to-all-done.refs_1_) | copy-start | bytes 2359300
  39.1 4.0 %collective-permute-start.3 = (f32[4,3,8,8,128]{4,3,2,1,0:T(8,128)S(1)}, f32[4,3,8,8,128]{4,3,2,1,0:T(8,128)}, u32[]{:S(2)}, u32[]{:S(2)}) collective-permute-start(f32[4,3,8,8,128]{4,3,2,1,0:T(8,128)S(1)} %get-tuple-element.27), channel_id=1, source_target_pairs={{24,8},{25,9},{26,10},{27,11},{28,12},{29,13},{30,14},{31,15}} | collective-permute-start | bytes 1179656 | tf_op jit(solution)/shard_map/ppermute | solution.py:723
  40.5 31.5 %collective-permute-start.1 = (f32[8,3,8,8,128]{4,3,2,1,0:T(8,128)S(1)}, f32[8,3,8,8,128]{4,3,2,1,0:T(8,128)S(1)}, u32[]{:S(2)}, u32[]{:S(2)}) collective-permute-start(f32[8,3,8,8,128]{4,3,2,1,0:T(8,128)S(1)} %all-to-all-done.refs_1_), channel_id=1, source_target_pairs={{8,0},{9,1},{10,2},{11,3},{12,4},{13,5},{14,6},{15,7}} | collective-permute-start | bytes 2359304 | tf_op jit(solution)/shard_map/ppermute | solution.py:724
  41.8 14.5 %collective-permute-start.2 = (f32[4,3,8,8,128]{4,3,2,1,0:T(8,128)}, f32[4,3,8,8,128]{4,3,2,1,0:T(8,128)S(1)}, u32[]{:S(2)}, u32[]{:S(2)}) collective-permute-start(f32[4,3,8,8,128]{4,3,2,1,0:T(8,128)} %get-tuple-element.28), channel_id=1, source_target_pairs={{24,0},{25,1},{26,2},{27,3},{28,4},{29,5},{30,6},{31,7}} | collective-permute-start | bytes 1179656 | tf_op jit(solution)/shard_map/ppermute | solution.py:726
  43.1 26.8 %collective-permute-start.4 = (f32[4,3,8,8,128]{4,3,2,1,0:T(8,128)}, f32[4,3,8,8,128]{4,3,2,1,0:T(8,128)S(1)}, u32[]{:S(2)}, u32[]{:S(2)}) collective-permute-start(f32[4,3,8,8,128]{4,3,2,1,0:T(8,128)} %collective-permute-done.3), channel_id=1, source_target_pairs={{8,0},{9,1},{10,2},{11,3},{12,4},{13,5},{14,6},{15,7}} | collective-permute-start | bytes 1179656 | tf_op jit(solution)/shard_map/ppermute | solution.py:749
  44.4 5.4 %copy-start.5 = (f32[3,2,8,4096]{3,2,1,0:T(8,128)}, f32[3,2,8,4096]{3,2,1,0:T(8,128)S(1)}, u32[]{:S(2)}) copy-start(f32[3,2,8,4096]{3,2,1,0:T(8,128)S(1)} %collective-permute-done.11.refs_1_) | copy-start | bytes 2359300
  44.4 30.3 %collective-permute-start.5 = (f32[8,3,8,8,128]{4,3,2,1,0:T(8,128)S(1)}, f32[8,3,8,8,128]{4,3,2,1,0:T(8,128)S(1)}, u32[]{:S(2)}, u32[]{:S(2)}) collective-permute-start(f32[8,3,8,8,128]{4,3,2,1,0:T(8,128)S(1)} %all-to-all-done.refs_1_), channel_id=1, source_target_pairs={{16,0},{17,1},{18,2},{19,3},{20,4},{21,5},{22,6},{23,7}} | collective-permute-start | bytes 2359304 | tf_op jit(solution)/shard_map/ppermute | solution.py:725
  49.8 52.8 %collective-permute-start.15 = (f32[3,2,16,4096]{3,2,1,0:T(8,128)}, f32[3,2,16,4096]{3,2,1,0:T(8,128)}, u32[]{:S(2)}, u32[]{:S(2)}) collective-permute-start(f32[3,2,16,4096]{3,2,1,0:T(8,128)} %get-tuple-element.26.refs_6_), channel_id=1, source_target_pairs={{8,9},{9,10},{10,11},{11,12},{12,13},{13,14},{14,15},{16,17},{17,1... | collective-permute-start | bytes 4718600 | tf_op jit(solution)/shard_map/ppermute | solution.py:631
  56.3 20.3 %copy-start.6 = (f32[4,3,8,8,128]{4,3,2,1,0:T(8,128)}, f32[4,3,8,8,128]{4,3,2,1,0:T(8,128)S(1)}, u32[]{:S(2)}) copy-start(f32[4,3,8,8,128]{4,3,2,1,0:T(8,128)S(1)} %collective-permute-done.2.refs_2_) | copy-start | bytes 1179652
  56.3 46.3 %collective-permute-start.16 = (f32[3,2,16,4096]{3,2,1,0:T(8,128)}, f32[3,2,16,4096]{3,2,1,0:T(8,128)}, u32[]{:S(2)}, u32[]{:S(2)}) collective-permute-start(f32[3,2,16,4096]{3,2,1,0:T(8,128)} %get-tuple-element.25.refs_5_), channel_id=1, source_target_pairs={{9,8},{10,9},{11,10},{12,11},{13,12},{14,13},{15,14},{17,16},{18,1... | collective-permute-start | bytes 4718600 | tf_op jit(solution)/shard_map/ppermute | solution.py:631
  69.9 4.8 %copy-start.7 = (f32[4,3,8,8,128]{4,3,2,1,0:T(8,128)}, f32[4,3,8,8,128]{4,3,2,1,0:T(8,128)S(1)}, u32[]{:S(2)}) copy-start(f32[4,3,8,8,128]{4,3,2,1,0:T(8,128)S(1)} %collective-permute-done.4.refs_3_) | copy-start | bytes 1179652
  69.9 11.4 %collective-permute-start.8 = (f32[3,2,8,4096]{3,2,1,0:T(8,128)}, f32[3,2,8,4096]{3,2,1,0:T(8,128)S(1)}, u32[]{:S(2)}, u32[]{:S(2)}) collective-permute-start(f32[3,2,8,4096]{3,2,1,0:T(8,128)} %get-tuple-element.20.refs_10_), channel_id=1, source_target_pairs={{8,9},{9,8},{10,11},{11,10},{12,13},{13,12},{14,15},{15,14},{16,17... | collective-permute-start | bytes 2359304 | tf_op jit(solution)/shard_map/ppermute | solution.py:631
  72.0 4.7 %copy-start.3 = (f32[8,3,8,8,128]{4,3,2,1,0:T(8,128)}, f32[8,3,8,8,128]{4,3,2,1,0:T(8,128)S(1)}, u32[]{:S(2)}) copy-start(f32[8,3,8,8,128]{4,3,2,1,0:T(8,128)S(1)} %collective-permute-done.1.refs_0_) | copy-start | bytes 2359300
  72.0 13.5 %collective-permute-start.12 = (f32[3,2,8,4096]{3,2,1,0:T(8,128)}, f32[3,2,8,4096]{3,2,1,0:T(8,128)}, u32[]{:S(2)}, u32[]{:S(2)}) collective-permute-start(f32[3,2,8,4096]{3,2,1,0:T(8,128)} %copy-done.5), channel_id=1, source_target_pairs={{24,16},{25,17},{26,18},{27,19},{28,20},{29,21},{30,22},{31,23},{0... | collective-permute-start | bytes 2359304 | tf_op jit(solution)/shard_map/ppermute | solution.py:652
  74.7 2.0 %copy-start.4 = (f32[8,3,8,8,128]{4,3,2,1,0:T(8,128)}, f32[8,3,8,8,128]{4,3,2,1,0:T(8,128)S(1)}, u32[]{:S(2)}) copy-start(f32[8,3,8,8,128]{4,3,2,1,0:T(8,128)S(1)} %collective-permute-done.5.refs_4_) | copy-start | bytes 2359300
  74.7 15.0 %collective-permute-start.9 = (f32[3,2,8,4096]{3,2,1,0:T(8,128)}, f32[3,2,8,4096]{3,2,1,0:T(8,128)S(1)}, u32[]{:S(2)}, u32[]{:S(2)}) collective-permute-start(f32[3,2,8,4096]{3,2,1,0:T(8,128)} %get-tuple-element.19.refs_9_), channel_id=1, source_target_pairs={{8,9},{9,8},{10,11},{11,10},{12,13},{13,12},{14,15},{15,14},{16,17... | collective-permute-start | bytes 2359304 | tf_op jit(solution)/shard_map/ppermute | solution.py:631
  81.3 21.4 %copy-start.1 = (f32[3,2,8,4096]{3,2,1,0:T(8,128)}, f32[3,2,8,4096]{3,2,1,0:T(8,128)S(1)}, u32[]{:S(2)}) copy-start(f32[3,2,8,4096]{3,2,1,0:T(8,128)S(1)} %collective-permute-done.8.refs_11_) | copy-start | bytes 2359300
  81.3 31.3 %collective-permute-start.6 = (f32[3,2,8,4096]{3,2,1,0:T(8,128)}, f32[3,2,8,4096]{3,2,1,0:T(8,128)S(1)}, u32[]{:S(2)}, u32[]{:S(2)}) collective-permute-start(f32[3,2,8,4096]{3,2,1,0:T(8,128)} %get-tuple-element.18.refs_6_), channel_id=1, source_target_pairs={{0,1},{1,2},{2,3},{3,4},{4,5},{5,6},{6,7}} | collective-permute-start | bytes 2359304 | tf_op jit(solution)/shard_map/ppermute | solution.py:631
  85.5 27.1 %collective-permute-start.7 = (f32[3,2,8,4096]{3,2,1,0:T(8,128)}, f32[3,2,8,4096]{3,2,1,0:T(8,128)S(1)}, u32[]{:S(2)}, u32[]{:S(2)}) collective-permute-start(f32[3,2,8,4096]{3,2,1,0:T(8,128)} %get-tuple-element.17.refs_5_), channel_id=1, source_target_pairs={{1,0},{2,1},{3,2},{4,3},{5,4},{6,5},{7,6}} | collective-permute-start | bytes 2359304 | tf_op jit(solution)/shard_map/ppermute | solution.py:631
  89.7 12.9 %copy-start.2 = (f32[3,2,8,4096]{3,2,1,0:T(8,128)}, f32[3,2,8,4096]{3,2,1,0:T(8,128)S(1)}, u32[]{:S(2)}) copy-start(f32[3,2,8,4096]{3,2,1,0:T(8,128)S(1)} %collective-permute-done.9.refs_12_) | copy-start | bytes 2359300
  89.7 6.1 %collective-permute-start.13 = (f32[3,2,4096]{2,1,0:T(2,128)}, f32[3,2,4096]{2,1,0:T(2,128)S(1)}, u32[]{:S(2)}, u32[]{:S(2)}) collective-permute-start(f32[3,2,4096]{2,1,0:T(2,128)} %get-tuple-element.23), channel_id=1, source_target_pairs={{0,1},{1,2},{2,3},{3,4},{4,5},{5,6},{6,7},{8,9},{9,10},{10,11},{11... | collective-permute-start | bytes 294920 | tf_op jit(solution)/shard_map/ppermute | solution.py:631
  95.8 6.8 %copy-start.10 = (f32[3,2,4096]{2,1,0:T(2,128)}, f32[3,2,4096]{2,1,0:T(2,128)S(1)}, u32[]{:S(2)}) copy-start(f32[3,2,4096]{2,1,0:T(2,128)S(1)} %collective-permute-done.13.refs_3_) | copy-start | bytes 294916
  95.8 6.8 %collective-permute-start.14 = (f32[3,2,4096]{2,1,0:T(2,128)}, f32[3,2,4096]{2,1,0:T(2,128)S(1)}, u32[]{:S(2)}, u32[]{:S(2)}) collective-permute-start(f32[3,2,4096]{2,1,0:T(2,128)} %get-tuple-element.24), channel_id=1, source_target_pairs={{1,0},{2,1},{3,2},{4,3},{5,4},{6,5},{7,6},{9,8},{10,9},{11,10},{12... | collective-permute-start | bytes 294920 | tf_op jit(solution)/shard_map/ppermute | solution.py:631
  102.6 0.6 copy-start.11
  112.6 0.9 copy-start.8
  113.5 0.9 copy-start.9

commit v4 on v3

--- a/solution.py
+++ b/solution.py
@@ -284,23 +284,22 @@
             run_copies(rows(left, right))
 
 
-def inflow_faces_kernel(places, *refs):
+def inflow_faces_kernel(*refs):
     pieces = refs[:-3]
     dn, up, sem = refs[-3:]
-    copies = []
-    for piece, (source, part, parts) in zip(pieces, places):
-        slab, width = piece.shape[3:]
-        for s in range(piece.shape[0]):
-            at = ((source + s) * parts + part) * width
-            for j in range(2):
-                for ref, z in ((dn, j), (up, slab - 2 + j)):
-                    copies.append(
-                        pltpu.make_async_copy(
-                            piece.at[s, :, :, z],
-                            ref.at[:, j, :, pl.ds(at, width)],
-                            sem.at[len(copies)],
-                        )
+    copies, first = [], 0
+    for piece in pieces:
+        count, slab = piece.shape[0], piece.shape[3]
+        for j in range(2):
+            for ref, z in ((dn, j), (up, slab - 2 + j)):
+                copies.append(
+                    pltpu.make_async_copy(
+                        piece.at[:, :, :, z],
+                        ref.at[pl.ds(first, count), :, j],
+                        sem.at[len(copies)],
                     )
+                )
+        first += count
 
     @pl.when(lax.axis_index("grp") == 0)
     def _():
@@ -443,12 +442,14 @@
     return g > 0, g < ranks - 1, r > 0, r < rows - 1, r == 0
 
 
-def row_pieces(faces, first, nb, na, b2, b0, a0, a2):
+ROWS = ((2, 1, 0, SUB), (3, 0, 1, SUB), (2, 0, 2, 0), (0, 0, 3, 0), (1, 1, 4, 0), (3, 1, 5, 0))
+
+
+def row_pieces(faces, first, *scratch):
     count = faces[0].shape[2]
     return [
-        (faces[i].at[:, j], ref.at[:, pl.ds(at + first, count)])
-        for i, j, ref, at in ((2, 1, nb, SUB), (3, 0, na, SUB), (2, 0, b2, 0), (3, 1, a2, 0),
-                              (0, 0, b0, 0), (1, 1, a0, 0))
+        (faces[i].at[:, j], scratch[ref].at[:, pl.ds(at + first, count)])
+        for i, j, ref, at in ROWS
     ]
 
 
@@ -540,26 +541,36 @@
     lax.fori_loop(first, cells, drain, 0)
 
 
-def inflow_kernel(rows, ranks, places, vel, *refs):
-    parts, refs = refs[:-23], refs[-23:]
-    dn_in, up_in, b_in, a_in, dn_hi, up_hi, b_hi, a_hi, _, out_hbm = refs[:10]
-    start, sect, out, nb, na, b2, b0, a0, a2, eb, ea, sem, out_sem = refs[10:]
-    low = dn_in.shape[2]
+def inflow_kernel(rows, ranks, groups_of, vel, *refs):
+    many = sum(len(places) for places in groups_of)
+    parts, refs = refs[:many], refs[many:]
+    faces, refs = refs[: 4 * len(groups_of)], refs[4 * len(groups_of) :]
+    dn_hi, up_hi, b_hi, a_hi, _, out_hbm = refs[:6]
+    start, sect, out, nb, na, b2, b0, a0, a2, eb, ea, spread, sem, out_sem = refs[6:]
+    cells = b2.shape[1]
+    low = cells - dn_hi.shape[2]
     span = vel.shape[3]
     reach = out.shape[1]
-    cells = b2.shape[1]
     has_before, has_after, _, _, is_first = roles(rows, ranks)
+    scratch = (nb, na, b2, b0, a0, a2)
 
     @pl.when(is_first)
     def _():
-        edges = row_pieces((dn_in, up_in, b_in, a_in), 0, nb, na, b2, b0, a0, a2)
-        edges += row_pieces((dn_hi, up_hi, b_hi, a_hi), low, nb, na, b2, b0, a0, a2)
+        edges = row_pieces((dn_hi, up_hi, b_hi, a_hi), low, *scratch)
         main = [(vel.at[:, pl.ds(low, 4)], start.at[:, pl.ds(low + 2, 4)])]
-        for piece, (source, part, many) in zip(parts, places):
-            width = piece.shape[4]
-            for i in range(piece.shape[0]):
-                at = ((source + i) * many + part) * width
-                main.append((piece.at[i], start.at[:, pl.ds(2, low), :, pl.ds(at, width)]))
+        lanes_of, at = [], 0
+        for k, places in enumerate(groups_of):
+            first = len(lanes_of)
+            for piece, (source, part, parts_in) in zip(parts[at : at + len(places)], places):
+                width = piece.shape[4]
+                for i in range(piece.shape[0]):
+                    lane = ((source + i) * parts_in + part) * width
+                    main.append((piece.at[i], start.at[:, pl.ds(2, low), :, pl.ds(lane, width)]))
+                    lanes_of.append(lane)
+            at += len(places)
+            for i in range(4):
+                face = faces[4 * k + i]
+                edges.append((face, spread.at[i, pl.ds(first, len(lanes_of) - first)]))
         edges = [pltpu.make_async_copy(p, q, sem.at[i]) for i, (p, q) in enumerate(edges)]
         main = [
             pltpu.make_async_copy(p, q, sem.at[len(edges) + i]) for i, (p, q) in enumerate(main)
@@ -574,6 +585,10 @@
                 ref[c, 0:SUB, :] = zero
                 ref[c, SUB + cells :, :] = zero
         finish(edges)
+        for n, lane in enumerate(lanes_of):
+            for i, j, ref, first in ROWS:
+                for c in range(3):
+                    scratch[ref][c, first : first + low, lane : lane + LANES] = spread[i, n, c, j]
         groups = cells // SUB
         edge_rows(nb, b2, b0, eb, has_before, 0, groups, span)
         edge_rows(na, a0, a2, ea, has_after, 0, groups, span)
@@ -631,7 +646,6 @@
         return lax.ppermute(array, ("grp", "gx"), pairs)
 
     packed = jax.ShapeDtypeStruct((comps, count, depth * HALF // LANES, LANES), F32)
-    face = jax.ShapeDtypeStruct((3, 2, low, span), F32)
     face_hi = jax.ShapeDtypeStruct((3, 2, high, span), F32)
     xface = jax.ShapeDtypeStruct((3, 2, slab, span), F32)
     full = jax.ShapeDtypeStruct(velocity.shape, F32)
@@ -759,37 +773,50 @@
     )(velocity, *xfaces, up_corners, dn_corners, dn_all, up_all, b_all, a_all, dn_hi, up_hi, b_hi,
       a_hi)
 
-    parts = [hop_1, got_a, hop_3, hop_4, hop_2]
-    places = [(0, 0, PARTS), (0, 1, PARTS), (0, 2, PARTS), (half, 2, PARTS), (0, 3, PARTS)]
+    parts = [[hop_1, got_a, hop_3, hop_4, hop_2]]
+    groups_of = [
+        [(0, 0, PARTS), (0, 1, PARTS), (0, 2, PARTS), (half, 2, PARTS), (0, 3, PARTS)]
+    ]
     if width != LANES:
         joined = [hop_1, got_a, jnp.concatenate([hop_3, hop_4], axis=0), hop_2]
         joined = jnp.concatenate(joined, axis=4)
-        parts = [joined[..., at : at + LANES] for at in range(0, span_local, LANES)]
-        places = [(0, i, len(parts)) for i in range(len(parts))]
-    many = len(parts)
-    dn_in, up_in = call(
-        functools.partial(inflow_faces_kernel, places),
-        [face, face],
-        [VMEM] * 2,
-        [ANY] * many,
-        [dma((4 * sum(p.shape[0] for p in parts),))],
-        cost(0, 8 * noise.size),
-    )(*parts)
-    b_in = along_gx(up_in, 1, [0])
-    a_in = along_gx(dn_in, -1, [0])
+        parts = [[joined[..., at : at + LANES] for at in range(0, span_local, LANES)]]
+        groups_of = [[(0, i, len(parts[0])) for i in range(len(parts[0]))]]
+    faces = []
+    for group in parts:
+        number = sum(p.shape[0] for p in group)
+        part_face = jax.ShapeDtypeStruct((number, 3, 2, low, LANES), F32)
+        dn_in, up_in = call(
+            inflow_faces_kernel,
+            [part_face, part_face],
+            [VMEM] * 2,
+            [ANY] * len(group),
+            [dma((4 * len(group),))],
+            cost(0, 2 * noise.size),
+        )(*group)
+        b_in = along_gx(up_in, 1, [0])
+        a_in = along_gx(dn_in, -1, [0])
+        faces += [dn_in, up_in, b_in, a_in]
+    parts = [p for group in parts for p in group]
+    many = len(parts) + len(faces)
+    number = sum(p.shape[0] for p in parts)
 
     reach = low + 2
     return call(
-        functools.partial(inflow_kernel, rows, ranks, places),
+        functools.partial(inflow_kernel, rows, ranks, groups_of),
         full,
         ANY,
-        [ANY] * (many + 10),
+        [ANY] * (many + 6),
         fields(reach)
         + rows_scratch(low + high, span)
-        + [dma((sum(p.shape[0] for p in parts) + 13,)), dma((reach,))],
+        + [
+            pltpu.VMEM((4, number, 3, 2, low, LANES), F32),
+            dma((number + 7 + len(faces),)),
+            dma((reach,)),
+        ],
         cost(30 * velocity.size, 5 * velocity.size),
-        {many + 9: 0},
-    )(velocity, *parts, dn_in, up_in, b_in, a_in, dn_hi, up_hi, b_hi, a_hi, own)
+        {many + 5: 0},
+    )(velocity, *parts, *faces, dn_hi, up_hi, b_hi, a_hi, own)
 
 
 def solution(mesh):

time: 128 us -> 128 us (level)
  no operation moved by 1% of the time
where the time goes in v4:
time: 128 us
  Pallas kernels  42.7 us (33%)
  waiting for transfers between devices  40.6 us (32%)
  starting transfers between devices  40 us (31%)
  local copies, waits for them, and re-layouts  3.98 us (3%)
    pallas_call x9, Pallas kernels, run(): pl.pallas_call(kernel, out_shape=out_shape, in_specs=in_specs, out_specs=...  42.7 us
    ppermute x8, starting transfers between devices, along_gx(): return lax.ppermute(array, ('grp', 'gx'), pairs)  19.5 us
    all_to_all x1, waiting for transfers between devices, local(): got_a = lax.all_to_all(made_a, 'gx', 0, 0, tiled=True)  15.2 us
    ppermute x1, waiting for transfers between devices, local(): hop_4 = lax.ppermute(side, 'grp', [(1, 0)])  11.7 us
    ppermute x8, waiting for transfers between devices, along_gx(): return lax.ppermute(array, ('grp', 'gx'), pairs)  9.06 us
    ppermute x3, starting transfers between devices, across(): return lax.ppermute(array, ('grp', 'gx'), pairs + idle(idlers))  7.47 us
    all_to_all x1, starting transfers between devices, local(): got_a = lax.all_to_all(made_a, 'gx', 0, 0, tiled=True)  6.43 us
    ppermute x1, waiting for transfers between devices, local(): hop_3 = lax.ppermute(got_a[:half], 'grp', [(3, 0)])  4.68 us
  transfers between devices with their start and end apart: 18, of which 6 were waited for; matrix products, arithmetic and copies ran while one was open for 1% of the time, Pallas kernels for 18%

profile of v4, /device:TPU:1, one launch (start us, length us, event | category | flops | bytes accessed | tf_op | source)
XLA Modules:
  0.0 127.6 jit_solution(8115311876438591894)
XLA Ops:
  0.0 2.9 %shard_map.65 = (f32[3,8,16,128]{3,2,1,0:T(8,128)}, f32[3,2,8,4096]{3,2,1,0:T(8,128)}, f32[3,2,8,4096]{3,2,1,0:T(8,128)}) custom-call(f32[3,8,64,512]{3,2,1,0:T(8,128)} %noise.3, f32[3,16,8,4096]{3,2,1,0:T(8,128)} %vel.7), custom_call_target="tpu_custom_call" | custom-call | bytes 786432 | tf_op jit(solution)/shard_map/pallas_call | solution.py:615
  2.9 0.0 copy-start.12
  2.9 0.1 collective-permute-start
  3.0 4.0 %shard_map.64.along_hbm = f32[3,8,64,128]{3,2,1,0:T(8,128)} custom-call(f32[3,8,64,512]{3,2,1,0:T(8,128)} %noise.3), custom_call_target="tpu_custom_call" | custom-call | flops 603979776 | bytes 3145728 | tf_op jit(solution)/shard_map/pallas_call | solution.py:615
  7.0 0.0 collective-permute-done.rim
  7.0 0.0 copy-start.13
  7.0 0.7 copy-done.13
  7.7 4.1 %shard_map.66.after = f32[8,3,8,8,128]{4,3,2,1,0:T(8,128)} custom-call(f32[3,8,64,128]{3,2,1,0:T(8,128)} %shard_map.64.along_hbm, f32[3,8,16,128]{3,2,1,0:T(8,128)} %copy-done.13, f32[3,64,512]{2,1,0:T(8,128)} %previous.1, f32[3,64]{1,0:T(4,128)} %decay_ref.1, f32[6,64]{1,0:T(8,128)} %factor_ref.1, f32[1,64]{1,0:T(1,128)} %bitcast.1), custom_call_target="tpu_custom_call" | custom-call | flops 603979776 | bytes 3145728 | tf_op jit(solution)/shard_map/pallas_call | solution.py:615
  11.8 6.4 %all-to-all-start = ((f32[8,3,8,8,128]{4,3,2,1,0:T(8,128)}), f32[8,3,8,8,128]{4,3,2,1,0:T(8,128)S(1)}, u32[]{:S(2)}, u32[]{:S(2)}) async-start(f32[8,3,8,8,128]{4,3,2,1,0:T(8,128)} %shard_map.66.after), calls=%async_computation | async-start | bytes 1572864 | tf_op jit(solution)/shard_map/all_to_all | solution.py:717
  18.2 0.0 copy-done.12
  18.2 1.9 %collective-permute-start.11 = (f32[3,2,8,4096]{3,2,1,0:T(8,128)S(1)}, f32[3,2,8,4096]{3,2,1,0:T(8,128)S(1)}, u32[]{:S(2)}, u32[]{:S(2)}) collective-permute-start(f32[3,2,8,4096]{3,2,1,0:T(8,128)S(1)} %copy-done.12), channel_id=1, source_target_pairs={{8,24},{9,25},{10,26},{11,27},{12,28},{13,29},{14,30},{15,31},{16,... | collective-permute-start | bytes 2359304 | tf_op jit(solution)/shard_map/ppermute | solution.py:666
  20.2 2.9 %collective-permute-start.10 = (f32[3,2,8,4096]{3,2,1,0:T(8,128)}, f32[3,2,8,4096]{3,2,1,0:T(8,128)}, u32[]{:S(2)}, u32[]{:S(2)}) collective-permute-start(f32[3,2,8,4096]{3,2,1,0:T(8,128)} %get-tuple-element.21), channel_id=1, source_target_pairs={{0,8},{1,9},{2,10},{3,11},{4,12},{5,13},{6,14},{7,15},{8,0},{9,1},... | collective-permute-start | bytes 2359304 | tf_op jit(solution)/shard_map/ppermute | solution.py:666
  23.0 15.2 %all-to-all-done.refs_1_ = f32[8,3,8,8,128]{4,3,2,1,0:T(8,128)S(1)} async-done(((f32[8,3,8,8,128]{4,3,2,1,0:T(8,128)}), f32[8,3,8,8,128]{4,3,2,1,0:T(8,128)S(1)}, u32[]{:S(2)}, u32[]{:S(2)}) %all-to-all-start) | async-done | bytes 786464 | tf_op jit(solution)/shard_map/all_to_all | solution.py:717
  38.2 0.9 fusion
  39.1 1.4 %collective-permute-start.3 = (f32[4,3,8,8,128]{4,3,2,1,0:T(8,128)S(1)}, f32[4,3,8,8,128]{4,3,2,1,0:T(8,128)}, u32[]{:S(2)}, u32[]{:S(2)}) collective-permute-start(f32[4,3,8,8,128]{4,3,2,1,0:T(8,128)S(1)} %get-tuple-element.27), channel_id=1, source_target_pairs={{24,8},{25,9},{26,10},{27,11},{28,12},{29,13},{30,14},{31,15}} | collective-permute-start | bytes 1179656 | tf_op jit(solution)/shard_map/ppermute | solution.py:737
  40.5 1.3 %collective-permute-start.1 = (f32[8,3,8,8,128]{4,3,2,1,0:T(8,128)S(1)}, f32[8,3,8,8,128]{4,3,2,1,0:T(8,128)S(1)}, u32[]{:S(2)}, u32[]{:S(2)}) collective-permute-start(f32[8,3,8,8,128]{4,3,2,1,0:T(8,128)S(1)} %all-to-all-done.refs_1_), channel_id=1, source_target_pairs={{8,0},{9,1},{10,2},{11,3},{12,4},{13,5},{14,6},{15,7}} | collective-permute-start | bytes 2359304 | tf_op jit(solution)/shard_map/ppermute | solution.py:738
  41.8 1.3 %collective-permute-start.2 = (f32[4,3,8,8,128]{4,3,2,1,0:T(8,128)}, f32[4,3,8,8,128]{4,3,2,1,0:T(8,128)S(1)}, u32[]{:S(2)}, u32[]{:S(2)}) collective-permute-start(f32[4,3,8,8,128]{4,3,2,1,0:T(8,128)} %get-tuple-element.28), channel_id=1, source_target_pairs={{24,0},{25,1},{26,2},{27,3},{28,4},{29,5},{30,6},{31,7}} | collective-permute-start | bytes 1179656 | tf_op jit(solution)/shard_map/ppermute | solution.py:740
  43.1 0.0 collective-permute-done.3
  43.1 1.3 %collective-permute-start.4 = (f32[4,3,8,8,128]{4,3,2,1,0:T(8,128)}, f32[4,3,8,8,128]{4,3,2,1,0:T(8,128)S(1)}, u32[]{:S(2)}, u32[]{:S(2)}) collective-permute-start(f32[4,3,8,8,128]{4,3,2,1,0:T(8,128)} %collective-permute-done.3), channel_id=1, source_target_pairs={{8,0},{9,1},{10,2},{11,3},{12,4},{13,5},{14,6},{15,7}} | collective-permute-start | bytes 1179656 | tf_op jit(solution)/shard_map/ppermute | solution.py:763
  44.4 0.0 collective-permute-done.11.refs_1_
  44.4 0.0 copy-start.5
  44.4 1.3 %collective-permute-start.5 = (f32[8,3,8,8,128]{4,3,2,1,0:T(8,128)S(1)}, f32[8,3,8,8,128]{4,3,2,1,0:T(8,128)S(1)}, u32[]{:S(2)}, u32[]{:S(2)}) collective-permute-start(f32[8,3,8,8,128]{4,3,2,1,0:T(8,128)S(1)} %all-to-all-done.refs_1_), channel_id=1, source_target_pairs={{16,0},{17,1},{18,2},{19,3},{20,4},{21,5},{22,6},{23,7}} | collective-permute-start | bytes 2359304 | tf_op jit(solution)/shard_map/ppermute | solution.py:739
  45.7 4.1 %shard_map.68 = (f32[3,2,16,4096]{3,2,1,0:T(8,128)}, f32[3,2,16,4096]{3,2,1,0:T(8,128)}, f32[3,2,8,4096]{3,2,1,0:T(8,128)}, f32[3,2,8,4096]{3,2,1,0:T(8,128)}) custom-call(f32[3,16,8,4096]{3,2,1,0:T(8,128)} %vel.7, f32[8,3,8,8,128]{4,3,2,1,0:T(8,128)} %shard_map.66.after), custom_call_target="tpu_custom_call" | custom-call | bytes 1572864 | tf_op jit(solution)/shard_map/pallas_call | solution.py:615
  49.8 0.0 copy-done
  49.8 0.0 copy-done.5
  49.8 0.0 collective-permute-done.10.refs_0_
  49.8 1.8 %collective-permute-start.15 = (f32[3,2,16,4096]{3,2,1,0:T(8,128)}, f32[3,2,16,4096]{3,2,1,0:T(8,128)}, u32[]{:S(2)}, u32[]{:S(2)}) collective-permute-start(f32[3,2,16,4096]{3,2,1,0:T(8,128)} %get-tuple-element.26.refs_6_), channel_id=1, source_target_pairs={{8,9},{9,10},{10,11},{11,12},{12,13},{13,14},{14,15},{16,17},{17,1... | collective-permute-start | bytes 4718600 | tf_op jit(solution)/shard_map/ppermute | solution.py:646
  51.7 4.7 %collective-permute-done.2.refs_2_ = f32[4,3,8,8,128]{4,3,2,1,0:T(8,128)S(1)} collective-permute-done((f32[4,3,8,8,128]{4,3,2,1,0:T(8,128)}, f32[4,3,8,8,128]{4,3,2,1,0:T(8,128)S(1)}, u32[]{:S(2)}, u32[]{:S(2)}) %collective-permute-start.2) | collective-permute-done | bytes 393248 | tf_op jit(solution)/shard_map/ppermute | solution.py:740
  56.3 1.9 %collective-permute-start.16 = (f32[3,2,16,4096]{3,2,1,0:T(8,128)}, f32[3,2,16,4096]{3,2,1,0:T(8,128)}, u32[]{:S(2)}, u32[]{:S(2)}) collective-permute-start(f32[3,2,16,4096]{3,2,1,0:T(8,128)} %get-tuple-element.25.refs_5_), channel_id=1, source_target_pairs={{9,8},{10,9},{11,10},{12,11},{13,12},{14,13},{15,14},{17,16},{18,1... | collective-permute-start | bytes 4718600 | tf_op jit(solution)/shard_map/ppermute | solution.py:646
  58.2 11.7 %collective-permute-done.4.refs_3_ = f32[4,3,8,8,128]{4,3,2,1,0:T(8,128)S(1)} collective-permute-done((f32[4,3,8,8,128]{4,3,2,1,0:T(8,128)}, f32[4,3,8,8,128]{4,3,2,1,0:T(8,128)S(1)}, u32[]{:S(2)}, u32[]{:S(2)}) %collective-permute-start.4) | collective-permute-done | bytes 393248 | tf_op jit(solution)/shard_map/ppermute | solution.py:763
  69.9 2.1 %collective-permute-start.8 = (f32[3,2,8,4096]{3,2,1,0:T(8,128)}, f32[3,2,8,4096]{3,2,1,0:T(8,128)S(1)}, u32[]{:S(2)}, u32[]{:S(2)}) collective-permute-start(f32[3,2,8,4096]{3,2,1,0:T(8,128)} %get-tuple-element.20.refs_10_), channel_id=1, source_target_pairs={{8,9},{9,8},{10,11},{11,10},{12,13},{13,12},{14,15},{15,14},{16,17... | collective-permute-start | bytes 2359304 | tf_op jit(solution)/shard_map/ppermute | solution.py:646
  72.0 0.0 collective-permute-done.1.refs_0_
  72.0 0.0 copy-start.3
  72.0 2.7 %collective-permute-start.12 = (f32[3,2,8,4096]{3,2,1,0:T(8,128)}, f32[3,2,8,4096]{3,2,1,0:T(8,128)}, u32[]{:S(2)}, u32[]{:S(2)}) collective-permute-start(f32[3,2,8,4096]{3,2,1,0:T(8,128)} %copy-done.5), channel_id=1, source_target_pairs={{24,16},{25,17},{26,18},{27,19},{28,20},{29,21},{30,22},{31,23},{0... | collective-permute-start | bytes 2359304 | tf_op jit(solution)/shard_map/ppermute | solution.py:666
  74.7 0.0 collective-permute-done.5.refs_4_
  74.7 0.0 copy-done.7
  74.7 0.0 copy-start.4
  74.7 1.9 %collective-permute-start.9 = (f32[3,2,8,4096]{3,2,1,0:T(8,128)}, f32[3,2,8,4096]{3,2,1,0:T(8,128)S(1)}, u32[]{:S(2)}, u32[]{:S(2)}) collective-permute-start(f32[3,2,8,4096]{3,2,1,0:T(8,128)} %get-tuple-element.19.refs_9_), channel_id=1, source_target_pairs={{8,9},{9,8},{10,11},{11,10},{12,13},{13,12},{14,15},{15,14},{16,17... | collective-permute-start | bytes 2359304 | tf_op jit(solution)/shard_map/ppermute | solution.py:646
  76.7 0.0 copy-done.6
  76.7 2.8 %shard_map.67 = (f32[32,3,2,8,128]{4,3,2,1,0:T(8,128)}, f32[32,3,2,8,128]{4,3,2,1,0:T(8,128)}) custom-call(f32[8,3,8,8,128]{4,3,2,1,0:T(8,128)} %copy-done.3, f32[8,3,8,8,128]{4,3,2,1,0:T(8,128)} %copy-done, f32[4,3,8,8,128]{4,3,2,1,0:T(8,128)} %copy-done.6, f32[4,3,8,8,128]{4,3,2,1,0:T(8,128)} %copy-done.7, f32[8,3,8,8,128]{4,3,2,1,0:T(8,128)} %copy-done.4), custom_call_target="tpu_custom_call" | custom-call | bytes 1572864 | tf_op jit(solution)/shard_map/pallas_call | solution.py:615
  79.5 1.7 %collective-permute-done.8.refs_11_ = f32[3,2,8,4096]{3,2,1,0:T(8,128)S(1)} collective-permute-done((f32[3,2,8,4096]{3,2,1,0:T(8,128)}, f32[3,2,8,4096]{3,2,1,0:T(8,128)S(1)}, u32[]{:S(2)}, u32[]{:S(2)}) %collective-permute-start.8) | collective-permute-done | bytes 786464 | tf_op jit(solution)/shard_map/ppermute | solution.py:646
  81.3 4.3 %collective-permute-start.6 = (f32[32,3,2,8,128]{4,3,2,1,0:T(8,128)}, f32[32,3,2,8,128]{4,3,2,1,0:T(8,128)S(1)}, u32[]{:S(2)}, u32[]{:S(2)}) collective-permute-start(f32[32,3,2,8,128]{4,3,2,1,0:T(8,128)} %get-tuple-element.18.refs_6_), channel_id=1, source_target_pairs={{0,1},{1,2},{2,3},{3,4},{4,5},{5,6},{6,7}} | collective-permute-start | bytes 2359304 | tf_op jit(solution)/shard_map/ppermute | solution.py:646
  85.5 0.0 collective-permute-done.12.refs_2_
  85.5 1.9 %collective-permute-start.7 = (f32[32,3,2,8,128]{4,3,2,1,0:T(8,128)}, f32[32,3,2,8,128]{4,3,2,1,0:T(8,128)S(1)}, u32[]{:S(2)}, u32[]{:S(2)}) collective-permute-start(f32[32,3,2,8,128]{4,3,2,1,0:T(8,128)} %get-tuple-element.17.refs_5_), channel_id=1, source_target_pairs={{1,0},{2,1},{3,2},{4,3},{5,4},{6,5},{7,6}} | collective-permute-start | bytes 2359304 | tf_op jit(solution)/shard_map/ppermute | solution.py:646
  87.5 0.6 shard_map.69.refs_3_
  88.1 1.6 %shard_map.70 = (f32[3,2,4096]{2,1,0:T(2,128)}, f32[3,2,4096]{2,1,0:T(2,128)}) custom-call(f32[3,2,8,4096]{3,2,1,0:T(8,128)} %collective-permute-done.10.refs_0_, f32[3,2,8,4096]{3,2,1,0:T(8,128)} %copy-done.5, f32[3,2,8,4096]{3,2,1,0:T(8,128)} %collective-permute-done.12.refs_2_, f32[8,128]{1,0:T(8,128)} %shard_map.69.refs_3_), custom_call_target="tpu_custom_call" | custom-call | bytes 98304 | tf_op jit(solution)/shard_map/pallas_call | solution.py:615
  89.7 0.0 collective-permute-done.9.refs_12_
  89.7 0.0 copy-start.2
  89.7 3.6 %collective-permute-start.13 = (f32[3,2,4096]{2,1,0:T(2,128)}, f32[3,2,4096]{2,1,0:T(2,128)S(1)}, u32[]{:S(2)}, u32[]{:S(2)}) collective-permute-start(f32[3,2,4096]{2,1,0:T(2,128)} %get-tuple-element.23), channel_id=1, source_target_pairs={{0,1},{1,2},{2,3},{3,4},{4,5},{5,6},{6,7},{8,9},{9,10},{10,11},{11... | collective-permute-start | bytes 294920 | tf_op jit(solution)/shard_map/ppermute | solution.py:646
  93.4 2.4 %collective-permute-done.13.refs_3_ = f32[3,2,4096]{2,1,0:T(2,128)S(1)} collective-permute-done((f32[3,2,4096]{2,1,0:T(2,128)}, f32[3,2,4096]{2,1,0:T(2,128)S(1)}, u32[]{:S(2)}, u32[]{:S(2)}) %collective-permute-start.13) | collective-permute-done | bytes 98336 | tf_op jit(solution)/shard_map/ppermute | solution.py:646
  95.8 1.9 %collective-permute-start.14 = (f32[3,2,4096]{2,1,0:T(2,128)}, f32[3,2,4096]{2,1,0:T(2,128)S(1)}, u32[]{:S(2)}, u32[]{:S(2)}) collective-permute-start(f32[3,2,4096]{2,1,0:T(2,128)} %get-tuple-element.24), channel_id=1, source_target_pairs={{1,0},{2,1},{3,2},{4,3},{5,4},{6,5},{7,6},{9,8},{10,9},{11,10},{12... | collective-permute-start | bytes 294920 | tf_op jit(solution)/shard_map/ppermute | solution.py:646
  97.7 4.9 %collective-permute-done.14.refs_4_ = f32[3,2,4096]{2,1,0:T(2,128)S(1)} collective-permute-done((f32[3,2,4096]{2,1,0:T(2,128)}, f32[3,2,4096]{2,1,0:T(2,128)S(1)}, u32[]{:S(2)}, u32[]{:S(2)}) %collective-permute-start.14) | collective-permute-done | bytes 98336 | tf_op jit(solution)/shard_map/ppermute | solution.py:646
  102.6 0.0 collective-permute-done.15.refs_7_
  102.6 0.0 collective-permute-done.16.refs_8_
  102.6 0.0 copy-done.1
  102.6 0.0 copy-done.2
  102.6 0.0 copy-done.10
  102.6 0.6 copy-done.11
  103.2 9.3 %shard_map.71.refs_13_ = f32[3,16,8,4096]{3,2,1,0:T(8,128)} custom-call(f32[3,16,8,4096]{3,2,1,0:T(8,128)} %vel.7, f32[3,2,8,4096]{3,2,1,0:T(8,128)} %collective-permute-done.10.refs_0_, f32[3,2,8,4096]{3,2,1,0:T(8,128)} %copy-done.5, f32[3,2,8,4096]{3,2,1,0:T(8,128)} %collective-permute-done.12.refs_2_, f32[3,2,4096]{2,1,0:T(2,128)} %copy-done.10, ...), custom_call_target="tpu_custom_call" | custom-call | flops 78643200 | bytes 12582912 | tf_op jit(solution)/shard_map/pallas_call | solution.py:615
  112.6 0.0 collective-permute-done.6.refs_7_
  112.6 0.0 collective-permute-done.7.refs_8_
  112.6 0.9 copy-done.8
  113.5 0.9 copy-done.9
  114.4 13.2 %shard_map.72 = f32[3,16,8,4096]{3,2,1,0:T(8,128)} custom-call(f32[3,16,8,4096]{3,2,1,0:T(8,128)} %vel.7, f32[8,3,8,8,128]{4,3,2,1,0:T(8,128)} %copy-done.3, f32[8,3,8,8,128]{4,3,2,1,0:T(8,128)} %copy-done, f32[4,3,8,8,128]{4,3,2,1,0:T(8,128)} %copy-done.6, f32[4,3,8,8,128]{4,3,2,1,0:T(8,128)} %copy-done.7, ...), custom_call_target="tpu_custom_call", output_to_operand_aliasing={{}: (14, {})} | custom-call | flops 47185920 | bytes 7864320 | tf_op jit(solution)/shard_map/pallas_call | solution.py:615
  (10 shorter events, 0.0 us)
Async XLA Ops:
  2.9 15.3 %copy-start.12 = (f32[3,2,8,4096]{3,2,1,0:T(8,128)S(1)}, f32[3,2,8,4096]{3,2,1,0:T(8,128)}, u32[]{:S(2)}) copy-start(f32[3,2,8,4096]{3,2,1,0:T(8,128)} %get-tuple-element.22) | copy-start | bytes 2359300
  2.9 4.1 %collective-permute-start = (f32[3,8,16,128]{3,2,1,0:T(8,128)}, f32[3,8,16,128]{3,2,1,0:T(8,128)S(1)}, u32[]{:S(2)}, u32[]{:S(2)}) collective-permute-start(f32[3,8,16,128]{3,2,1,0:T(8,128)} %get-tuple-element.16), channel_id=1, source_target_pairs={{0,1},{1,0},{2,3},{3,2},{4,5},{5,4},{6,7},{7,6},{24,25},{25,24},{2... | collective-permute-start | bytes 589832 | tf_op jit(solution)/shard_map/ppermute | solution.py:671
  7.0 0.7 copy-start.13
  11.8 26.4 %all-to-all-start = ((f32[8,3,8,8,128]{4,3,2,1,0:T(8,128)}), f32[8,3,8,8,128]{4,3,2,1,0:T(8,128)S(1)}, u32[]{:S(2)}, u32[]{:S(2)}) async-start(f32[8,3,8,8,128]{4,3,2,1,0:T(8,128)} %shard_map.66.after), calls=%async_computation | async-start | bytes 1572864 | tf_op jit(solution)/shard_map/all_to_all | solution.py:717
  18.2 26.2 %collective-permute-start.11 = (f32[3,2,8,4096]{3,2,1,0:T(8,128)S(1)}, f32[3,2,8,4096]{3,2,1,0:T(8,128)S(1)}, u32[]{:S(2)}, u32[]{:S(2)}) collective-permute-start(f32[3,2,8,4096]{3,2,1,0:T(8,128)S(1)} %copy-done.12), channel_id=1, source_target_pairs={{8,24},{9,25},{10,26},{11,27},{12,28},{13,29},{14,30},{15,31},{16,... | collective-permute-start | bytes 2359304 | tf_op jit(solution)/shard_map/ppermute | solution.py:666
  20.2 29.7 %collective-permute-start.10 = (f32[3,2,8,4096]{3,2,1,0:T(8,128)}, f32[3,2,8,4096]{3,2,1,0:T(8,128)}, u32[]{:S(2)}, u32[]{:S(2)}) collective-permute-start(f32[3,2,8,4096]{3,2,1,0:T(8,128)} %get-tuple-element.21), channel_id=1, source_target_pairs={{0,8},{1,9},{2,10},{3,11},{4,12},{5,13},{6,14},{7,15},{8,0},{9,1},... | collective-permute-start | bytes 2359304 | tf_op jit(solution)/shard_map/ppermute | solution.py:666
  38.2 11.6 %copy-start = (f32[8,3,8,8,128]{4,3,2,1,0:T(8,128)}, f32[8,3,8,8,128]{4,3,2,1,0:T(8,128)S(1)}, u32[]{:S(2)}) copy-start(f32[8,3,8,8,128]{4,3,2,1,0:T(8,128)S(1)} %all-to-all-done.refs_1_) | copy-start | bytes 2359300
  39.1 4.0 %collective-permute-start.3 = (f32[4,3,8,8,128]{4,3,2,1,0:T(8,128)S(1)}, f32[4,3,8,8,128]{4,3,2,1,0:T(8,128)}, u32[]{:S(2)}, u32[]{:S(2)}) collective-permute-start(f32[4,3,8,8,128]{4,3,2,1,0:T(8,128)S(1)} %get-tuple-element.27), channel_id=1, source_target_pairs={{24,8},{25,9},{26,10},{27,11},{28,12},{29,13},{30,14},{31,15}} | collective-permute-start | bytes 1179656 | tf_op jit(solution)/shard_map/ppermute | solution.py:737
  40.5 31.5 %collective-permute-start.1 = (f32[8,3,8,8,128]{4,3,2,1,0:T(8,128)S(1)}, f32[8,3,8,8,128]{4,3,2,1,0:T(8,128)S(1)}, u32[]{:S(2)}, u32[]{:S(2)}) collective-permute-start(f32[8,3,8,8,128]{4,3,2,1,0:T(8,128)S(1)} %all-to-all-done.refs_1_), channel_id=1, source_target_pairs={{8,0},{9,1},{10,2},{11,3},{12,4},{13,5},{14,6},{15,7}} | collective-permute-start | bytes 2359304 | tf_op jit(solution)/shard_map/ppermute | solution.py:738
  41.8 14.5 %collective-permute-start.2 = (f32[4,3,8,8,128]{4,3,2,1,0:T(8,128)}, f32[4,3,8,8,128]{4,3,2,1,0:T(8,128)S(1)}, u32[]{:S(2)}, u32[]{:S(2)}) collective-permute-start(f32[4,3,8,8,128]{4,3,2,1,0:T(8,128)} %get-tuple-element.28), channel_id=1, source_target_pairs={{24,0},{25,1},{26,2},{27,3},{28,4},{29,5},{30,6},{31,7}} | collective-permute-start | bytes 1179656 | tf_op jit(solution)/shard_map/ppermute | solution.py:740
  43.1 26.8 %collective-permute-start.4 = (f32[4,3,8,8,128]{4,3,2,1,0:T(8,128)}, f32[4,3,8,8,128]{4,3,2,1,0:T(8,128)S(1)}, u32[]{:S(2)}, u32[]{:S(2)}) collective-permute-start(f32[4,3,8,8,128]{4,3,2,1,0:T(8,128)} %collective-permute-done.3), channel_id=1, source_target_pairs={{8,0},{9,1},{10,2},{11,3},{12,4},{13,5},{14,6},{15,7}} | collective-permute-start | bytes 1179656 | tf_op jit(solution)/shard_map/ppermute | solution.py:763
  44.4 5.4 %copy-start.5 = (f32[3,2,8,4096]{3,2,1,0:T(8,128)}, f32[3,2,8,4096]{3,2,1,0:T(8,128)S(1)}, u32[]{:S(2)}) copy-start(f32[3,2,8,4096]{3,2,1,0:T(8,128)S(1)} %collective-permute-done.11.refs_1_) | copy-start | bytes 2359300
  44.4 30.3 %collective-permute-start.5 = (f32[8,3,8,8,128]{4,3,2,1,0:T(8,128)S(1)}, f32[8,3,8,8,128]{4,3,2,1,0:T(8,128)S(1)}, u32[]{:S(2)}, u32[]{:S(2)}) collective-permute-start(f32[8,3,8,8,128]{4,3,2,1,0:T(8,128)S(1)} %all-to-all-done.refs_1_), channel_id=1, source_target_pairs={{16,0},{17,1},{18,2},{19,3},{20,4},{21,5},{22,6},{23,7}} | collective-permute-start | bytes 2359304 | tf_op jit(solution)/shard_map/ppermute | solution.py:739
  49.8 52.8 %collective-permute-start.15 = (f32[3,2,16,4096]{3,2,1,0:T(8,128)}, f32[3,2,16,4096]{3,2,1,0:T(8,128)}, u32[]{:S(2)}, u32[]{:S(2)}) collective-permute-start(f32[3,2,16,4096]{3,2,1,0:T(8,128)} %get-tuple-element.26.refs_6_), channel_id=1, source_target_pairs={{8,9},{9,10},{10,11},{11,12},{12,13},{13,14},{14,15},{16,17},{17,1... | collective-permute-start | bytes 4718600 | tf_op jit(solution)/shard_map/ppermute | solution.py:646
  56.3 20.3 %copy-start.6 = (f32[4,3,8,8,128]{4,3,2,1,0:T(8,128)}, f32[4,3,8,8,128]{4,3,2,1,0:T(8,128)S(1)}, u32[]{:S(2)}) copy-start(f32[4,3,8,8,128]{4,3,2,1,0:T(8,128)S(1)} %collective-permute-done.2.refs_2_) | copy-start | bytes 1179652
  56.3 46.3 %collective-permute-start.16 = (f32[3,2,16,4096]{3,2,1,0:T(8,128)}, f32[3,2,16,4096]{3,2,1,0:T(8,128)}, u32[]{:S(2)}, u32[]{:S(2)}) collective-permute-start(f32[3,2,16,4096]{3,2,1,0:T(8,128)} %get-tuple-element.25.refs_5_), channel_id=1, source_target_pairs={{9,8},{10,9},{11,10},{12,11},{13,12},{14,13},{15,14},{17,16},{18,1... | collective-permute-start | bytes 4718600 | tf_op jit(solution)/shard_map/ppermute | solution.py:646
  69.9 4.8 %copy-start.7 = (f32[4,3,8,8,128]{4,3,2,1,0:T(8,128)}, f32[4,3,8,8,128]{4,3,2,1,0:T(8,128)S(1)}, u32[]{:S(2)}) copy-start(f32[4,3,8,8,128]{4,3,2,1,0:T(8,128)S(1)} %collective-permute-done.4.refs_3_) | copy-start | bytes 1179652
  69.9 11.4 %collective-permute-start.8 = (f32[3,2,8,4096]{3,2,1,0:T(8,128)}, f32[3,2,8,4096]{3,2,1,0:T(8,128)S(1)}, u32[]{:S(2)}, u32[]{:S(2)}) collective-permute-start(f32[3,2,8,4096]{3,2,1,0:T(8,128)} %get-tuple-element.20.refs_10_), channel_id=1, source_target_pairs={{8,9},{9,8},{10,11},{11,10},{12,13},{13,12},{14,15},{15,14},{16,17... | collective-permute-start | bytes 2359304 | tf_op jit(solution)/shard_map/ppermute | solution.py:646
  72.0 4.7 %copy-start.3 = (f32[8,3,8,8,128]{4,3,2,1,0:T(8,128)}, f32[8,3,8,8,128]{4,3,2,1,0:T(8,128)S(1)}, u32[]{:S(2)}) copy-start(f32[8,3,8,8,128]{4,3,2,1,0:T(8,128)S(1)} %collective-permute-done.1.refs_0_) | copy-start | bytes 2359300
  72.0 13.5 %collective-permute-start.12 = (f32[3,2,8,4096]{3,2,1,0:T(8,128)}, f32[3,2,8,4096]{3,2,1,0:T(8,128)}, u32[]{:S(2)}, u32[]{:S(2)}) collective-permute-start(f32[3,2,8,4096]{3,2,1,0:T(8,128)} %copy-done.5), channel_id=1, source_target_pairs={{24,16},{25,17},{26,18},{27,19},{28,20},{29,21},{30,22},{31,23},{0... | collective-permute-start | bytes 2359304 | tf_op jit(solution)/shard_map/ppermute | solution.py:666
  74.7 2.0 %copy-start.4 = (f32[8,3,8,8,128]{4,3,2,1,0:T(8,128)}, f32[8,3,8,8,128]{4,3,2,1,0:T(8,128)S(1)}, u32[]{:S(2)}) copy-start(f32[8,3,8,8,128]{4,3,2,1,0:T(8,128)S(1)} %collective-permute-done.5.refs_4_) | copy-start | bytes 2359300
  74.7 15.0 %collective-permute-start.9 = (f32[3,2,8,4096]{3,2,1,0:T(8,128)}, f32[3,2,8,4096]{3,2,1,0:T(8,128)S(1)}, u32[]{:S(2)}, u32[]{:S(2)}) collective-permute-start(f32[3,2,8,4096]{3,2,1,0:T(8,128)} %get-tuple-element.19.refs_9_), channel_id=1, source_target_pairs={{8,9},{9,8},{10,11},{11,10},{12,13},{13,12},{14,15},{15,14},{16,17... | collective-permute-start | bytes 2359304 | tf_op jit(solution)/shard_map/ppermute | solution.py:646
  81.3 21.4 %copy-start.1 = (f32[3,2,8,4096]{3,2,1,0:T(8,128)}, f32[3,2,8,4096]{3,2,1,0:T(8,128)S(1)}, u32[]{:S(2)}) copy-start(f32[3,2,8,4096]{3,2,1,0:T(8,128)S(1)} %collective-permute-done.8.refs_11_) | copy-start | bytes 2359300
  81.3 31.3 %collective-permute-start.6 = (f32[32,3,2,8,128]{4,3,2,1,0:T(8,128)}, f32[32,3,2,8,128]{4,3,2,1,0:T(8,128)S(1)}, u32[]{:S(2)}, u32[]{:S(2)}) collective-permute-start(f32[32,3,2,8,128]{4,3,2,1,0:T(8,128)} %get-tuple-element.18.refs_6_), channel_id=1, source_target_pairs={{0,1},{1,2},{2,3},{3,4},{4,5},{5,6},{6,7}} | collective-permute-start | bytes 2359304 | tf_op jit(solution)/shard_map/ppermute | solution.py:646
  85.5 27.1 %collective-permute-start.7 = (f32[32,3,2,8,128]{4,3,2,1,0:T(8,128)}, f32[32,3,2,8,128]{4,3,2,1,0:T(8,128)S(1)}, u32[]{:S(2)}, u32[]{:S(2)}) collective-permute-start(f32[32,3,2,8,128]{4,3,2,1,0:T(8,128)} %get-tuple-element.17.refs_5_), channel_id=1, source_target_pairs={{1,0},{2,1},{3,2},{4,3},{5,4},{6,5},{7,6}} | collective-permute-start | bytes 2359304 | tf_op jit(solution)/shard_map/ppermute | solution.py:646
  89.7 12.9 %copy-start.2 = (f32[3,2,8,4096]{3,2,1,0:T(8,128)}, f32[3,2,8,4096]{3,2,1,0:T(8,128)S(1)}, u32[]{:S(2)}) copy-start(f32[3,2,8,4096]{3,2,1,0:T(8,128)S(1)} %collective-permute-done.9.refs_12_) | copy-start | bytes 2359300
  89.7 6.1 %collective-permute-start.13 = (f32[3,2,4096]{2,1,0:T(2,128)}, f32[3,2,4096]{2,1,0:T(2,128)S(1)}, u32[]{:S(2)}, u32[]{:S(2)}) collective-permute-start(f32[3,2,4096]{2,1,0:T(2,128)} %get-tuple-element.23), channel_id=1, source_target_pairs={{0,1},{1,2},{2,3},{3,4},{4,5},{5,6},{6,7},{8,9},{9,10},{10,11},{11... | collective-permute-start | bytes 294920 | tf_op jit(solution)/shard_map/ppermute | solution.py:646
  95.8 6.8 %copy-start.10 = (f32[3,2,4096]{2,1,0:T(2,128)}, f32[3,2,4096]{2,1,0:T(2,128)S(1)}, u32[]{:S(2)}) copy-start(f32[3,2,4096]{2,1,0:T(2,128)S(1)} %collective-permute-done.13.refs_3_) | copy-start | bytes 294916
  95.8 6.8 %collective-permute-start.14 = (f32[3,2,4096]{2,1,0:T(2,128)}, f32[3,2,4096]{2,1,0:T(2,128)S(1)}, u32[]{:S(2)}, u32[]{:S(2)}) collective-permute-start(f32[3,2,4096]{2,1,0:T(2,128)} %get-tuple-element.24), channel_id=1, source_target_pairs={{1,0},{2,1},{3,2},{4,3},{5,4},{6,5},{7,6},{9,8},{10,9},{11,10},{12... | collective-permute-start | bytes 294920 | tf_op jit(solution)/shard_map/ppermute | solution.py:646
  102.6 0.6 copy-start.11
  112.6 0.9 copy-start.8
  113.5 0.9 copy-start.9

commit v5 on v4

--- a/solution.py
+++ b/solution.py
@@ -734,10 +734,11 @@
     a_hi = along_gx(dn_hi, -1, [0], others)
 
     half = ranks // 2
-    side = lax.ppermute(got_a[half:], "grp", [(3, 1)])
+    first_half, last_half = got_a[:half], got_a[half:]
+    side = lax.ppermute(last_half, "grp", [(3, 1)])
     hop_1 = lax.ppermute(got_a, "grp", [(1, 0)])
     hop_2 = lax.ppermute(got_a, "grp", [(2, 0)])
-    hop_3 = lax.ppermute(got_a[:half], "grp", [(3, 0)])
+    hop_3 = lax.ppermute(first_half, "grp", [(3, 0)])
 
     b_all = along_gx(up_all, 1, others)
     a_all = along_gx(dn_all, -1, others)

time: 128 us -> 128 us (level)
  no operation moved by 1% of the time
where the time goes in v5:
time: 128 us
  Pallas kernels  42.7 us (33%)
  waiting for transfers between devices  40.6 us (32%)
  starting transfers between devices  40 us (31%)
  local copies, waits for them, and re-layouts  3.98 us (3%)
    pallas_call x9, Pallas kernels, run(): pl.pallas_call(kernel, out_shape=out_shape, in_specs=in_specs, out_specs=...  42.7 us
    ppermute x8, starting transfers between devices, along_gx(): return lax.ppermute(array, ('grp', 'gx'), pairs)  19.5 us
    all_to_all x1, waiting for transfers between devices, local(): got_a = lax.all_to_all(made_a, 'gx', 0, 0, tiled=True)  15.2 us
    ppermute x1, waiting for transfers between devices, local(): hop_4 = lax.ppermute(side, 'grp', [(1, 0)])  11.7 us
    ppermute x8, waiting for transfers between devices, along_gx(): return lax.ppermute(array, ('grp', 'gx'), pairs)  9.06 us
    ppermute x3, starting transfers between devices, across(): return lax.ppermute(array, ('grp', 'gx'), pairs + idle(idlers))  7.47 us
    all_to_all x1, starting transfers between devices, local(): got_a = lax.all_to_all(made_a, 'gx', 0, 0, tiled=True)  6.43 us
    ppermute x1, waiting for transfers between devices, local(): hop_3 = lax.ppermute(first_half, 'grp', [(3, 0)])  4.68 us
  transfers between devices with their start and end apart: 18, of which 6 were waited for; matrix products, arithmetic and copies ran while one was open for 1% of the time, Pallas kernels for 18%

profile of v5, /device:TPU:1, one launch (start us, length us, event | category | flops | bytes accessed | tf_op | source)
XLA Modules:
  0.0 127.6 jit_solution(8115311876438591894)
XLA Ops:
  0.0 2.9 %shard_map.65 = (f32[3,8,16,128]{3,2,1,0:T(8,128)}, f32[3,2,8,4096]{3,2,1,0:T(8,128)}, f32[3,2,8,4096]{3,2,1,0:T(8,128)}) custom-call(f32[3,8,64,512]{3,2,1,0:T(8,128)} %noise.3, f32[3,16,8,4096]{3,2,1,0:T(8,128)} %vel.7), custom_call_target="tpu_custom_call" | custom-call | bytes 786432 | tf_op jit(solution)/shard_map/pallas_call | solution.py:615
  2.9 0.0 copy-start.12
  2.9 0.1 collective-permute-start
  3.0 4.0 %shard_map.64.along_hbm = f32[3,8,64,128]{3,2,1,0:T(8,128)} custom-call(f32[3,8,64,512]{3,2,1,0:T(8,128)} %noise.3), custom_call_target="tpu_custom_call" | custom-call | flops 603979776 | bytes 3145728 | tf_op jit(solution)/shard_map/pallas_call | solution.py:615
  7.0 0.0 collective-permute-done.rim
  7.0 0.0 copy-start.13
  7.0 0.7 copy-done.13
  7.7 4.1 %shard_map.66.after = f32[8,3,8,8,128]{4,3,2,1,0:T(8,128)} custom-call(f32[3,8,64,128]{3,2,1,0:T(8,128)} %shard_map.64.along_hbm, f32[3,8,16,128]{3,2,1,0:T(8,128)} %copy-done.13, f32[3,64,512]{2,1,0:T(8,128)} %previous.1, f32[3,64]{1,0:T(4,128)} %decay_ref.1, f32[6,64]{1,0:T(8,128)} %factor_ref.1, f32[1,64]{1,0:T(1,128)} %bitcast.1), custom_call_target="tpu_custom_call" | custom-call | flops 603979776 | bytes 3145728 | tf_op jit(solution)/shard_map/pallas_call | solution.py:615
  11.8 6.4 %all-to-all-start = ((f32[8,3,8,8,128]{4,3,2,1,0:T(8,128)}), f32[8,3,8,8,128]{4,3,2,1,0:T(8,128)S(1)}, u32[]{:S(2)}, u32[]{:S(2)}) async-start(f32[8,3,8,8,128]{4,3,2,1,0:T(8,128)} %shard_map.66.after), calls=%async_computation | async-start | bytes 1572864 | tf_op jit(solution)/shard_map/all_to_all | solution.py:717
  18.2 0.0 copy-done.12
  18.2 1.9 %collective-permute-start.11 = (f32[3,2,8,4096]{3,2,1,0:T(8,128)S(1)}, f32[3,2,8,4096]{3,2,1,0:T(8,128)S(1)}, u32[]{:S(2)}, u32[]{:S(2)}) collective-permute-start(f32[3,2,8,4096]{3,2,1,0:T(8,128)S(1)} %copy-done.12), channel_id=1, source_target_pairs={{8,24},{9,25},{10,26},{11,27},{12,28},{13,29},{14,30},{15,31},{16,... | collective-permute-start | bytes 2359304 | tf_op jit(solution)/shard_map/ppermute | solution.py:666
  20.2 2.9 %collective-permute-start.10 = (f32[3,2,8,4096]{3,2,1,0:T(8,128)}, f32[3,2,8,4096]{3,2,1,0:T(8,128)}, u32[]{:S(2)}, u32[]{:S(2)}) collective-permute-start(f32[3,2,8,4096]{3,2,1,0:T(8,128)} %get-tuple-element.21), channel_id=1, source_target_pairs={{0,8},{1,9},{2,10},{3,11},{4,12},{5,13},{6,14},{7,15},{8,0},{9,1},... | collective-permute-start | bytes 2359304 | tf_op jit(solution)/shard_map/ppermute | solution.py:666
  23.0 15.2 %all-to-all-done.refs_1_ = f32[8,3,8,8,128]{4,3,2,1,0:T(8,128)S(1)} async-done(((f32[8,3,8,8,128]{4,3,2,1,0:T(8,128)}), f32[8,3,8,8,128]{4,3,2,1,0:T(8,128)S(1)}, u32[]{:S(2)}, u32[]{:S(2)}) %all-to-all-start) | async-done | bytes 786464 | tf_op jit(solution)/shard_map/all_to_all | solution.py:717
  38.2 0.9 fusion
  39.1 1.4 %collective-permute-start.3 = (f32[4,3,8,8,128]{4,3,2,1,0:T(8,128)S(1)}, f32[4,3,8,8,128]{4,3,2,1,0:T(8,128)}, u32[]{:S(2)}, u32[]{:S(2)}) collective-permute-start(f32[4,3,8,8,128]{4,3,2,1,0:T(8,128)S(1)} %get-tuple-element.27), channel_id=1, source_target_pairs={{24,8},{25,9},{26,10},{27,11},{28,12},{29,13},{30,14},{31,15}} | collective-permute-start | bytes 1179656 | tf_op jit(solution)/shard_map/ppermute | solution.py:738
  40.5 1.3 %collective-permute-start.1 = (f32[8,3,8,8,128]{4,3,2,1,0:T(8,128)S(1)}, f32[8,3,8,8,128]{4,3,2,1,0:T(8,128)S(1)}, u32[]{:S(2)}, u32[]{:S(2)}) collective-permute-start(f32[8,3,8,8,128]{4,3,2,1,0:T(8,128)S(1)} %all-to-all-done.refs_1_), channel_id=1, source_target_pairs={{8,0},{9,1},{10,2},{11,3},{12,4},{13,5},{14,6},{15,7}} | collective-permute-start | bytes 2359304 | tf_op jit(solution)/shard_map/ppermute | solution.py:739
  41.8 1.3 %collective-permute-start.2 = (f32[4,3,8,8,128]{4,3,2,1,0:T(8,128)}, f32[4,3,8,8,128]{4,3,2,1,0:T(8,128)S(1)}, u32[]{:S(2)}, u32[]{:S(2)}) collective-permute-start(f32[4,3,8,8,128]{4,3,2,1,0:T(8,128)} %get-tuple-element.28), channel_id=1, source_target_pairs={{24,0},{25,1},{26,2},{27,3},{28,4},{29,5},{30,6},{31,7}} | collective-permute-start | bytes 1179656 | tf_op jit(solution)/shard_map/ppermute | solution.py:741
  43.1 0.0 collective-permute-done.3
  43.1 1.3 %collective-permute-start.4 = (f32[4,3,8,8,128]{4,3,2,1,0:T(8,128)}, f32[4,3,8,8,128]{4,3,2,1,0:T(8,128)S(1)}, u32[]{:S(2)}, u32[]{:S(2)}) collective-permute-start(f32[4,3,8,8,128]{4,3,2,1,0:T(8,128)} %collective-permute-done.3), channel_id=1, source_target_pairs={{8,0},{9,1},{10,2},{11,3},{12,4},{13,5},{14,6},{15,7}} | collective-permute-start | bytes 1179656 | tf_op jit(solution)/shard_map/ppermute | solution.py:764
  44.4 0.0 collective-permute-done.11.refs_1_
  44.4 0.0 copy-start.5
  44.4 1.3 %collective-permute-start.5 = (f32[8,3,8,8,128]{4,3,2,1,0:T(8,128)S(1)}, f32[8,3,8,8,128]{4,3,2,1,0:T(8,128)S(1)}, u32[]{:S(2)}, u32[]{:S(2)}) collective-permute-start(f32[8,3,8,8,128]{4,3,2,1,0:T(8,128)S(1)} %all-to-all-done.refs_1_), channel_id=1, source_target_pairs={{16,0},{17,1},{18,2},{19,3},{20,4},{21,5},{22,6},{23,7}} | collective-permute-start | bytes 2359304 | tf_op jit(solution)/shard_map/ppermute | solution.py:740
  45.7 4.1 %shard_map.68 = (f32[3,2,16,4096]{3,2,1,0:T(8,128)}, f32[3,2,16,4096]{3,2,1,0:T(8,128)}, f32[3,2,8,4096]{3,2,1,0:T(8,128)}, f32[3,2,8,4096]{3,2,1,0:T(8,128)}) custom-call(f32[3,16,8,4096]{3,2,1,0:T(8,128)} %vel.7, f32[8,3,8,8,128]{4,3,2,1,0:T(8,128)} %shard_map.66.after), custom_call_target="tpu_custom_call" | custom-call | bytes 1572864 | tf_op jit(solution)/shard_map/pallas_call | solution.py:615
  49.8 0.0 copy-done
  49.8 0.0 copy-done.5
  49.8 0.0 collective-permute-done.10.refs_0_
  49.8 1.8 %collective-permute-start.15 = (f32[3,2,16,4096]{3,2,1,0:T(8,128)}, f32[3,2,16,4096]{3,2,1,0:T(8,128)}, u32[]{:S(2)}, u32[]{:S(2)}) collective-permute-start(f32[3,2,16,4096]{3,2,1,0:T(8,128)} %get-tuple-element.26.refs_6_), channel_id=1, source_target_pairs={{8,9},{9,10},{10,11},{11,12},{12,13},{13,14},{14,15},{16,17},{17,1... | collective-permute-start | bytes 4718600 | tf_op jit(solution)/shard_map/ppermute | solution.py:646
  51.7 4.7 %collective-permute-done.2.refs_2_ = f32[4,3,8,8,128]{4,3,2,1,0:T(8,128)S(1)} collective-permute-done((f32[4,3,8,8,128]{4,3,2,1,0:T(8,128)}, f32[4,3,8,8,128]{4,3,2,1,0:T(8,128)S(1)}, u32[]{:S(2)}, u32[]{:S(2)}) %collective-permute-start.2) | collective-permute-done | bytes 393248 | tf_op jit(solution)/shard_map/ppermute | solution.py:741
  56.3 1.9 %collective-permute-start.16 = (f32[3,2,16,4096]{3,2,1,0:T(8,128)}, f32[3,2,16,4096]{3,2,1,0:T(8,128)}, u32[]{:S(2)}, u32[]{:S(2)}) collective-permute-start(f32[3,2,16,4096]{3,2,1,0:T(8,128)} %get-tuple-element.25.refs_5_), channel_id=1, source_target_pairs={{9,8},{10,9},{11,10},{12,11},{13,12},{14,13},{15,14},{17,16},{18,1... | collective-permute-start | bytes 4718600 | tf_op jit(solution)/shard_map/ppermute | solution.py:646
  58.2 11.7 %collective-permute-done.4.refs_3_ = f32[4,3,8,8,128]{4,3,2,1,0:T(8,128)S(1)} collective-permute-done((f32[4,3,8,8,128]{4,3,2,1,0:T(8,128)}, f32[4,3,8,8,128]{4,3,2,1,0:T(8,128)S(1)}, u32[]{:S(2)}, u32[]{:S(2)}) %collective-permute-start.4) | collective-permute-done | bytes 393248 | tf_op jit(solution)/shard_map/ppermute | solution.py:764
  69.9 2.1 %collective-permute-start.8 = (f32[3,2,8,4096]{3,2,1,0:T(8,128)}, f32[3,2,8,4096]{3,2,1,0:T(8,128)S(1)}, u32[]{:S(2)}, u32[]{:S(2)}) collective-permute-start(f32[3,2,8,4096]{3,2,1,0:T(8,128)} %get-tuple-element.20.refs_10_), channel_id=1, source_target_pairs={{8,9},{9,8},{10,11},{11,10},{12,13},{13,12},{14,15},{15,14},{16,17... | collective-permute-start | bytes 2359304 | tf_op jit(solution)/shard_map/ppermute | solution.py:646
  72.0 0.0 collective-permute-done.1.refs_0_
  72.0 0.0 copy-start.3
  72.0 2.7 %collective-permute-start.12 = (f32[3,2,8,4096]{3,2,1,0:T(8,128)}, f32[3,2,8,4096]{3,2,1,0:T(8,128)}, u32[]{:S(2)}, u32[]{:S(2)}) collective-permute-start(f32[3,2,8,4096]{3,2,1,0:T(8,128)} %copy-done.5), channel_id=1, source_target_pairs={{24,16},{25,17},{26,18},{27,19},{28,20},{29,21},{30,22},{31,23},{0... | collective-permute-start | bytes 2359304 | tf_op jit(solution)/shard_map/ppermute | solution.py:666
  74.7 0.0 collective-permute-done.5.refs_4_
  74.7 0.0 copy-done.7
  74.7 0.0 copy-start.4
  74.7 1.9 %collective-permute-start.9 = (f32[3,2,8,4096]{3,2,1,0:T(8,128)}, f32[3,2,8,4096]{3,2,1,0:T(8,128)S(1)}, u32[]{:S(2)}, u32[]{:S(2)}) collective-permute-start(f32[3,2,8,4096]{3,2,1,0:T(8,128)} %get-tuple-element.19.refs_9_), channel_id=1, source_target_pairs={{8,9},{9,8},{10,11},{11,10},{12,13},{13,12},{14,15},{15,14},{16,17... | collective-permute-start | bytes 2359304 | tf_op jit(solution)/shard_map/ppermute | solution.py:646
  76.7 0.0 copy-done.6
  76.7 2.8 %shard_map.67 = (f32[32,3,2,8,128]{4,3,2,1,0:T(8,128)}, f32[32,3,2,8,128]{4,3,2,1,0:T(8,128)}) custom-call(f32[8,3,8,8,128]{4,3,2,1,0:T(8,128)} %copy-done.3, f32[8,3,8,8,128]{4,3,2,1,0:T(8,128)} %copy-done, f32[4,3,8,8,128]{4,3,2,1,0:T(8,128)} %copy-done.6, f32[4,3,8,8,128]{4,3,2,1,0:T(8,128)} %copy-done.7, f32[8,3,8,8,128]{4,3,2,1,0:T(8,128)} %copy-done.4), custom_call_target="tpu_custom_call" | custom-call | bytes 1572864 | tf_op jit(solution)/shard_map/pallas_call | solution.py:615
  79.5 1.7 %collective-permute-done.8.refs_11_ = f32[3,2,8,4096]{3,2,1,0:T(8,128)S(1)} collective-permute-done((f32[3,2,8,4096]{3,2,1,0:T(8,128)}, f32[3,2,8,4096]{3,2,1,0:T(8,128)S(1)}, u32[]{:S(2)}, u32[]{:S(2)}) %collective-permute-start.8) | collective-permute-done | bytes 786464 | tf_op jit(solution)/shard_map/ppermute | solution.py:646
  81.3 4.3 %collective-permute-start.6 = (f32[32,3,2,8,128]{4,3,2,1,0:T(8,128)}, f32[32,3,2,8,128]{4,3,2,1,0:T(8,128)S(1)}, u32[]{:S(2)}, u32[]{:S(2)}) collective-permute-start(f32[32,3,2,8,128]{4,3,2,1,0:T(8,128)} %get-tuple-element.18.refs_6_), channel_id=1, source_target_pairs={{0,1},{1,2},{2,3},{3,4},{4,5},{5,6},{6,7}} | collective-permute-start | bytes 2359304 | tf_op jit(solution)/shard_map/ppermute | solution.py:646
  85.5 0.0 collective-permute-done.12.refs_2_
  85.5 1.9 %collective-permute-start.7 = (f32[32,3,2,8,128]{4,3,2,1,0:T(8,128)}, f32[32,3,2,8,128]{4,3,2,1,0:T(8,128)S(1)}, u32[]{:S(2)}, u32[]{:S(2)}) collective-permute-start(f32[32,3,2,8,128]{4,3,2,1,0:T(8,128)} %get-tuple-element.17.refs_5_), channel_id=1, source_target_pairs={{1,0},{2,1},{3,2},{4,3},{5,4},{6,5},{7,6}} | collective-permute-start | bytes 2359304 | tf_op jit(solution)/shard_map/ppermute | solution.py:646
  87.5 0.6 shard_map.69.refs_3_
  88.1 1.6 %shard_map.70 = (f32[3,2,4096]{2,1,0:T(2,128)}, f32[3,2,4096]{2,1,0:T(2,128)}) custom-call(f32[3,2,8,4096]{3,2,1,0:T(8,128)} %collective-permute-done.10.refs_0_, f32[3,2,8,4096]{3,2,1,0:T(8,128)} %copy-done.5, f32[3,2,8,4096]{3,2,1,0:T(8,128)} %collective-permute-done.12.refs_2_, f32[8,128]{1,0:T(8,128)} %shard_map.69.refs_3_), custom_call_target="tpu_custom_call" | custom-call | bytes 98304 | tf_op jit(solution)/shard_map/pallas_call | solution.py:615
  89.7 0.0 collective-permute-done.9.refs_12_
  89.7 0.0 copy-start.2
  89.7 3.6 %collective-permute-start.13 = (f32[3,2,4096]{2,1,0:T(2,128)}, f32[3,2,4096]{2,1,0:T(2,128)S(1)}, u32[]{:S(2)}, u32[]{:S(2)}) collective-permute-start(f32[3,2,4096]{2,1,0:T(2,128)} %get-tuple-element.23), channel_id=1, source_target_pairs={{0,1},{1,2},{2,3},{3,4},{4,5},{5,6},{6,7},{8,9},{9,10},{10,11},{11... | collective-permute-start | bytes 294920 | tf_op jit(solution)/shard_map/ppermute | solution.py:646
  93.4 2.4 %collective-permute-done.13.refs_3_ = f32[3,2,4096]{2,1,0:T(2,128)S(1)} collective-permute-done((f32[3,2,4096]{2,1,0:T(2,128)}, f32[3,2,4096]{2,1,0:T(2,128)S(1)}, u32[]{:S(2)}, u32[]{:S(2)}) %collective-permute-start.13) | collective-permute-done | bytes 98336 | tf_op jit(solution)/shard_map/ppermute | solution.py:646
  95.8 1.9 %collective-permute-start.14 = (f32[3,2,4096]{2,1,0:T(2,128)}, f32[3,2,4096]{2,1,0:T(2,128)S(1)}, u32[]{:S(2)}, u32[]{:S(2)}) collective-permute-start(f32[3,2,4096]{2,1,0:T(2,128)} %get-tuple-element.24), channel_id=1, source_target_pairs={{1,0},{2,1},{3,2},{4,3},{5,4},{6,5},{7,6},{9,8},{10,9},{11,10},{12... | collective-permute-start | bytes 294920 | tf_op jit(solution)/shard_map/ppermute | solution.py:646
  97.7 4.9 %collective-permute-done.14.refs_4_ = f32[3,2,4096]{2,1,0:T(2,128)S(1)} collective-permute-done((f32[3,2,4096]{2,1,0:T(2,128)}, f32[3,2,4096]{2,1,0:T(2,128)S(1)}, u32[]{:S(2)}, u32[]{:S(2)}) %collective-permute-start.14) | collective-permute-done | bytes 98336 | tf_op jit(solution)/shard_map/ppermute | solution.py:646
  102.6 0.0 collective-permute-done.15.refs_7_
  102.6 0.0 collective-permute-done.16.refs_8_
  102.6 0.0 copy-done.1
  102.6 0.0 copy-done.2
  102.6 0.0 copy-done.10
  102.6 0.6 copy-done.11
  103.2 9.3 %shard_map.71.refs_13_ = f32[3,16,8,4096]{3,2,1,0:T(8,128)} custom-call(f32[3,16,8,4096]{3,2,1,0:T(8,128)} %vel.7, f32[3,2,8,4096]{3,2,1,0:T(8,128)} %collective-permute-done.10.refs_0_, f32[3,2,8,4096]{3,2,1,0:T(8,128)} %copy-done.5, f32[3,2,8,4096]{3,2,1,0:T(8,128)} %collective-permute-done.12.refs_2_, f32[3,2,4096]{2,1,0:T(2,128)} %copy-done.10, ...), custom_call_target="tpu_custom_call" | custom-call | flops 78643200 | bytes 12582912 | tf_op jit(solution)/shard_map/pallas_call | solution.py:615
  112.6 0.0 collective-permute-done.6.refs_7_
  112.6 0.0 collective-permute-done.7.refs_8_
  112.6 0.9 copy-done.8
  113.5 0.9 copy-done.9
  114.4 13.2 %shard_map.72 = f32[3,16,8,4096]{3,2,1,0:T(8,128)} custom-call(f32[3,16,8,4096]{3,2,1,0:T(8,128)} %vel.7, f32[8,3,8,8,128]{4,3,2,1,0:T(8,128)} %copy-done.3, f32[8,3,8,8,128]{4,3,2,1,0:T(8,128)} %copy-done, f32[4,3,8,8,128]{4,3,2,1,0:T(8,128)} %copy-done.6, f32[4,3,8,8,128]{4,3,2,1,0:T(8,128)} %copy-done.7, ...), custom_call_target="tpu_custom_call", output_to_operand_aliasing={{}: (14, {})} | custom-call | flops 47185920 | bytes 7864320 | tf_op jit(solution)/shard_map/pallas_call | solution.py:615
  (10 shorter events, 0.0 us)
Async XLA Ops:
  2.9 15.3 %copy-start.12 = (f32[3,2,8,4096]{3,2,1,0:T(8,128)S(1)}, f32[3,2,8,4096]{3,2,1,0:T(8,128)}, u32[]{:S(2)}) copy-start(f32[3,2,8,4096]{3,2,1,0:T(8,128)} %get-tuple-element.22) | copy-start | bytes 2359300
  2.9 4.1 %collective-permute-start = (f32[3,8,16,128]{3,2,1,0:T(8,128)}, f32[3,8,16,128]{3,2,1,0:T(8,128)S(1)}, u32[]{:S(2)}, u32[]{:S(2)}) collective-permute-start(f32[3,8,16,128]{3,2,1,0:T(8,128)} %get-tuple-element.16), channel_id=1, source_target_pairs={{0,1},{1,0},{2,3},{3,2},{4,5},{5,4},{6,7},{7,6},{24,25},{25,24},{2... | collective-permute-start | bytes 589832 | tf_op jit(solution)/shard_map/ppermute | solution.py:671
  7.0 0.7 copy-start.13
  11.8 26.4 %all-to-all-start = ((f32[8,3,8,8,128]{4,3,2,1,0:T(8,128)}), f32[8,3,8,8,128]{4,3,2,1,0:T(8,128)S(1)}, u32[]{:S(2)}, u32[]{:S(2)}) async-start(f32[8,3,8,8,128]{4,3,2,1,0:T(8,128)} %shard_map.66.after), calls=%async_computation | async-start | bytes 1572864 | tf_op jit(solution)/shard_map/all_to_all | solution.py:717
  18.2 26.2 %collective-permute-start.11 = (f32[3,2,8,4096]{3,2,1,0:T(8,128)S(1)}, f32[3,2,8,4096]{3,2,1,0:T(8,128)S(1)}, u32[]{:S(2)}, u32[]{:S(2)}) collective-permute-start(f32[3,2,8,4096]{3,2,1,0:T(8,128)S(1)} %copy-done.12), channel_id=1, source_target_pairs={{8,24},{9,25},{10,26},{11,27},{12,28},{13,29},{14,30},{15,31},{16,... | collective-permute-start | bytes 2359304 | tf_op jit(solution)/shard_map/ppermute | solution.py:666
  20.2 29.7 %collective-permute-start.10 = (f32[3,2,8,4096]{3,2,1,0:T(8,128)}, f32[3,2,8,4096]{3,2,1,0:T(8,128)}, u32[]{:S(2)}, u32[]{:S(2)}) collective-permute-start(f32[3,2,8,4096]{3,2,1,0:T(8,128)} %get-tuple-element.21), channel_id=1, source_target_pairs={{0,8},{1,9},{2,10},{3,11},{4,12},{5,13},{6,14},{7,15},{8,0},{9,1},... | collective-permute-start | bytes 2359304 | tf_op jit(solution)/shard_map/ppermute | solution.py:666
  38.2 11.6 %copy-start = (f32[8,3,8,8,128]{4,3,2,1,0:T(8,128)}, f32[8,3,8,8,128]{4,3,2,1,0:T(8,128)S(1)}, u32[]{:S(2)}) copy-start(f32[8,3,8,8,128]{4,3,2,1,0:T(8,128)S(1)} %all-to-all-done.refs_1_) | copy-start | bytes 2359300
  39.1 4.0 %collective-permute-start.3 = (f32[4,3,8,8,128]{4,3,2,1,0:T(8,128)S(1)}, f32[4,3,8,8,128]{4,3,2,1,0:T(8,128)}, u32[]{:S(2)}, u32[]{:S(2)}) collective-permute-start(f32[4,3,8,8,128]{4,3,2,1,0:T(8,128)S(1)} %get-tuple-element.27), channel_id=1, source_target_pairs={{24,8},{25,9},{26,10},{27,11},{28,12},{29,13},{30,14},{31,15}} | collective-permute-start | bytes 1179656 | tf_op jit(solution)/shard_map/ppermute | solution.py:738
  40.5 31.5 %collective-permute-start.1 = (f32[8,3,8,8,128]{4,3,2,1,0:T(8,128)S(1)}, f32[8,3,8,8,128]{4,3,2,1,0:T(8,128)S(1)}, u32[]{:S(2)}, u32[]{:S(2)}) collective-permute-start(f32[8,3,8,8,128]{4,3,2,1,0:T(8,128)S(1)} %all-to-all-done.refs_1_), channel_id=1, source_target_pairs={{8,0},{9,1},{10,2},{11,3},{12,4},{13,5},{14,6},{15,7}} | collective-permute-start | bytes 2359304 | tf_op jit(solution)/shard_map/ppermute | solution.py:739
  41.8 14.5 %collective-permute-start.2 = (f32[4,3,8,8,128]{4,3,2,1,0:T(8,128)}, f32[4,3,8,8,128]{4,3,2,1,0:T(8,128)S(1)}, u32[]{:S(2)}, u32[]{:S(2)}) collective-permute-start(f32[4,3,8,8,128]{4,3,2,1,0:T(8,128)} %get-tuple-element.28), channel_id=1, source_target_pairs={{24,0},{25,1},{26,2},{27,3},{28,4},{29,5},{30,6},{31,7}} | collective-permute-start | bytes 1179656 | tf_op jit(solution)/shard_map/ppermute | solution.py:741
  43.1 26.8 %collective-permute-start.4 = (f32[4,3,8,8,128]{4,3,2,1,0:T(8,128)}, f32[4,3,8,8,128]{4,3,2,1,0:T(8,128)S(1)}, u32[]{:S(2)}, u32[]{:S(2)}) collective-permute-start(f32[4,3,8,8,128]{4,3,2,1,0:T(8,128)} %collective-permute-done.3), channel_id=1, source_target_pairs={{8,0},{9,1},{10,2},{11,3},{12,4},{13,5},{14,6},{15,7}} | collective-permute-start | bytes 1179656 | tf_op jit(solution)/shard_map/ppermute | solution.py:764
  44.4 5.4 %copy-start.5 = (f32[3,2,8,4096]{3,2,1,0:T(8,128)}, f32[3,2,8,4096]{3,2,1,0:T(8,128)S(1)}, u32[]{:S(2)}) copy-start(f32[3,2,8,4096]{3,2,1,0:T(8,128)S(1)} %collective-permute-done.11.refs_1_) | copy-start | bytes 2359300
  44.4 30.3 %collective-permute-start.5 = (f32[8,3,8,8,128]{4,3,2,1,0:T(8,128)S(1)}, f32[8,3,8,8,128]{4,3,2,1,0:T(8,128)S(1)}, u32[]{:S(2)}, u32[]{:S(2)}) collective-permute-start(f32[8,3,8,8,128]{4,3,2,1,0:T(8,128)S(1)} %all-to-all-done.refs_1_), channel_id=1, source_target_pairs={{16,0},{17,1},{18,2},{19,3},{20,4},{21,5},{22,6},{23,7}} | collective-permute-start | bytes 2359304 | tf_op jit(solution)/shard_map/ppermute | solution.py:740
  49.8 52.8 %collective-permute-start.15 = (f32[3,2,16,4096]{3,2,1,0:T(8,128)}, f32[3,2,16,4096]{3,2,1,0:T(8,128)}, u32[]{:S(2)}, u32[]{:S(2)}) collective-permute-start(f32[3,2,16,4096]{3,2,1,0:T(8,128)} %get-tuple-element.26.refs_6_), channel_id=1, source_target_pairs={{8,9},{9,10},{10,11},{11,12},{12,13},{13,14},{14,15},{16,17},{17,1... | collective-permute-start | bytes 4718600 | tf_op jit(solution)/shard_map/ppermute | solution.py:646
  56.3 20.3 %copy-start.6 = (f32[4,3,8,8,128]{4,3,2,1,0:T(8,128)}, f32[4,3,8,8,128]{4,3,2,1,0:T(8,128)S(1)}, u32[]{:S(2)}) copy-start(f32[4,3,8,8,128]{4,3,2,1,0:T(8,128)S(1)} %collective-permute-done.2.refs_2_) | copy-start | bytes 1179652
  56.3 46.3 %collective-permute-start.16 = (f32[3,2,16,4096]{3,2,1,0:T(8,128)}, f32[3,2,16,4096]{3,2,1,0:T(8,128)}, u32[]{:S(2)}, u32[]{:S(2)}) collective-permute-start(f32[3,2,16,4096]{3,2,1,0:T(8,128)} %get-tuple-element.25.refs_5_), channel_id=1, source_target_pairs={{9,8},{10,9},{11,10},{12,11},{13,12},{14,13},{15,14},{17,16},{18,1... | collective-permute-start | bytes 4718600 | tf_op jit(solution)/shard_map/ppermute | solution.py:646
  69.9 4.8 %copy-start.7 = (f32[4,3,8,8,128]{4,3,2,1,0:T(8,128)}, f32[4,3,8,8,128]{4,3,2,1,0:T(8,128)S(1)}, u32[]{:S(2)}) copy-start(f32[4,3,8,8,128]{4,3,2,1,0:T(8,128)S(1)} %collective-permute-done.4.refs_3_) | copy-start | bytes 1179652
  69.9 11.4 %collective-permute-start.8 = (f32[3,2,8,4096]{3,2,1,0:T(8,128)}, f32[3,2,8,4096]{3,2,1,0:T(8,128)S(1)}, u32[]{:S(2)}, u32[]{:S(2)}) collective-permute-start(f32[3,2,8,4096]{3,2,1,0:T(8,128)} %get-tuple-element.20.refs_10_), channel_id=1, source_target_pairs={{8,9},{9,8},{10,11},{11,10},{12,13},{13,12},{14,15},{15,14},{16,17... | collective-permute-start | bytes 2359304 | tf_op jit(solution)/shard_map/ppermute | solution.py:646
  72.0 4.7 %copy-start.3 = (f32[8,3,8,8,128]{4,3,2,1,0:T(8,128)}, f32[8,3,8,8,128]{4,3,2,1,0:T(8,128)S(1)}, u32[]{:S(2)}) copy-start(f32[8,3,8,8,128]{4,3,2,1,0:T(8,128)S(1)} %collective-permute-done.1.refs_0_) | copy-start | bytes 2359300
  72.0 13.5 %collective-permute-start.12 = (f32[3,2,8,4096]{3,2,1,0:T(8,128)}, f32[3,2,8,4096]{3,2,1,0:T(8,128)}, u32[]{:S(2)}, u32[]{:S(2)}) collective-permute-start(f32[3,2,8,4096]{3,2,1,0:T(8,128)} %copy-done.5), channel_id=1, source_target_pairs={{24,16},{25,17},{26,18},{27,19},{28,20},{29,21},{30,22},{31,23},{0... | collective-permute-start | bytes 2359304 | tf_op jit(solution)/shard_map/ppermute | solution.py:666
  74.7 2.0 %copy-start.4 = (f32[8,3,8,8,128]{4,3,2,1,0:T(8,128)}, f32[8,3,8,8,128]{4,3,2,1,0:T(8,128)S(1)}, u32[]{:S(2)}) copy-start(f32[8,3,8,8,128]{4,3,2,1,0:T(8,128)S(1)} %collective-permute-done.5.refs_4_) | copy-start | bytes 2359300
  74.7 15.0 %collective-permute-start.9 = (f32[3,2,8,4096]{3,2,1,0:T(8,128)}, f32[3,2,8,4096]{3,2,1,0:T(8,128)S(1)}, u32[]{:S(2)}, u32[]{:S(2)}) collective-permute-start(f32[3,2,8,4096]{3,2,1,0:T(8,128)} %get-tuple-element.19.refs_9_), channel_id=1, source_target_pairs={{8,9},{9,8},{10,11},{11,10},{12,13},{13,12},{14,15},{15,14},{16,17... | collective-permute-start | bytes 2359304 | tf_op jit(solution)/shard_map/ppermute | solution.py:646
  81.3 21.4 %copy-start.1 = (f32[3,2,8,4096]{3,2,1,0:T(8,128)}, f32[3,2,8,4096]{3,2,1,0:T(8,128)S(1)}, u32[]{:S(2)}) copy-start(f32[3,2,8,4096]{3,2,1,0:T(8,128)S(1)} %collective-permute-done.8.refs_11_) | copy-start | bytes 2359300
  81.3 31.3 %collective-permute-start.6 = (f32[32,3,2,8,128]{4,3,2,1,0:T(8,128)}, f32[32,3,2,8,128]{4,3,2,1,0:T(8,128)S(1)}, u32[]{:S(2)}, u32[]{:S(2)}) collective-permute-start(f32[32,3,2,8,128]{4,3,2,1,0:T(8,128)} %get-tuple-element.18.refs_6_), channel_id=1, source_target_pairs={{0,1},{1,2},{2,3},{3,4},{4,5},{5,6},{6,7}} | collective-permute-start | bytes 2359304 | tf_op jit(solution)/shard_map/ppermute | solution.py:646
  85.5 27.1 %collective-permute-start.7 = (f32[32,3,2,8,128]{4,3,2,1,0:T(8,128)}, f32[32,3,2,8,128]{4,3,2,1,0:T(8,128)S(1)}, u32[]{:S(2)}, u32[]{:S(2)}) collective-permute-start(f32[32,3,2,8,128]{4,3,2,1,0:T(8,128)} %get-tuple-element.17.refs_5_), channel_id=1, source_target_pairs={{1,0},{2,1},{3,2},{4,3},{5,4},{6,5},{7,6}} | collective-permute-start | bytes 2359304 | tf_op jit(solution)/shard_map/ppermute | solution.py:646
  89.7 12.9 %copy-start.2 = (f32[3,2,8,4096]{3,2,1,0:T(8,128)}, f32[3,2,8,4096]{3,2,1,0:T(8,128)S(1)}, u32[]{:S(2)}) copy-start(f32[3,2,8,4096]{3,2,1,0:T(8,128)S(1)} %collective-permute-done.9.refs_12_) | copy-start | bytes 2359300
  89.7 6.1 %collective-permute-start.13 = (f32[3,2,4096]{2,1,0:T(2,128)}, f32[3,2,4096]{2,1,0:T(2,128)S(1)}, u32[]{:S(2)}, u32[]{:S(2)}) collective-permute-start(f32[3,2,4096]{2,1,0:T(2,128)} %get-tuple-element.23), channel_id=1, source_target_pairs={{0,1},{1,2},{2,3},{3,4},{4,5},{5,6},{6,7},{8,9},{9,10},{10,11},{11... | collective-permute-start | bytes 294920 | tf_op jit(solution)/shard_map/ppermute | solution.py:646
  95.8 6.8 %copy-start.10 = (f32[3,2,4096]{2,1,0:T(2,128)}, f32[3,2,4096]{2,1,0:T(2,128)S(1)}, u32[]{:S(2)}) copy-start(f32[3,2,4096]{2,1,0:T(2,128)S(1)} %collective-permute-done.13.refs_3_) | copy-start | bytes 294916
  95.8 6.8 %collective-permute-start.14 = (f32[3,2,4096]{2,1,0:T(2,128)}, f32[3,2,4096]{2,1,0:T(2,128)S(1)}, u32[]{:S(2)}, u32[]{:S(2)}) collective-permute-start(f32[3,2,4096]{2,1,0:T(2,128)} %get-tuple-element.24), channel_id=1, source_target_pairs={{1,0},{2,1},{3,2},{4,3},{5,4},{6,5},{7,6},{9,8},{10,9},{11,10},{12... | collective-permute-start | bytes 294920 | tf_op jit(solution)/shard_map/ppermute | solution.py:646
  102.6 0.6 copy-start.11
  112.6 0.9 copy-start.8
  113.5 0.9 copy-start.9
